TPU v7x, 128 devices: a whole 4x4x4 slice. The times are simulated.
128 devices in a mesh: shot: 4 (over x_lo, core), sub: 32 (over x_hi, z, y).
Axes of the slice: x: 4 (x_hi: 2, x_lo: 2; x = x_hi * 2 + x_lo), y: 4, z: 4, core: 2. Of those that a mesh axis runs over, the one named last changes fastest.
Arguments:
- velocity: float32 [512, 128, 256], P(('shot', 'sub')), may hold values from 1.5 to 4.5
- density: float32 [512, 128, 256], P(('shot', 'sub')), may hold values from 1 to 3
- aperture_start: int32 [4], P('shot'), may hold values from 0 to 96
- source_cell: int32 [4], P('shot'), may hold values from 0 to 4194303
- receiver_cells: int32 [4, 256], P('shot'), may hold values from 0 to 4194303, as said below
- wavelet: float32 [4, 4], P('shot'), may hold values from -6 to 6
- observed: float32 [4, 4, 256], P('shot'), may hold values from -6 to 6
- forward_old: float32 [4, 128, 128, 256], P('shot', 'sub'), may hold values from -6 to 6
- forward_now: float32 [4, 128, 128, 256], P('shot', 'sub'), may hold values from -6 to 6
- adjoint_later: float32 [4, 128, 128, 256], P('shot', 'sub'), may hold values from -6 to 6
- adjoint_now: float32 [4, 128, 128, 256], P('shot', 'sub'), may hold values from -6 to 6
Outputs:
- gradient: float32 [512, 128, 256], P(('shot', 'sub'))
- forward_last: float32 [4, 128, 128, 256], P('shot', 'sub')
- adjoint_first: float32 [4, 128, 128, 256], P('shot', 'sub')
Inputs may be any that keep to these rules, and one draw needn't show every extreme that they name: `aperture_start`: the aperture of a shot lies inside the model. `receiver_cells`: several receivers of a shot may share a cell; their injections add up.
All inputs are finite; a program needn't handle non-finite values.
Results may differ from a plain program's by a relative error of at most 0.00002.
Values sent between devices are 32-bit elements; how exact they have to be, the bound alone decides.
No kernel may reach another device: no remote copies, remote signals or barrier semaphores. Data moves between devices by JAX's collectives and lax.ppermute only.
A program may use at most 64 MiB of HBM per device.

v0:
```python
import functools

import jax
import jax.numpy as jnp
from jax import lax
from jax.experimental import pallas as pl
from jax.experimental.pallas import tpu as pltpu
from jax.sharding import PartitionSpec as P

lap_coeffs = (-205.0 / 72.0, 8.0 / 5.0, -1.0 / 5.0, 8.0 / 315.0, -1.0 / 560.0)
diff_coeffs = (4.0 / 5.0, -1.0 / 5.0, 4.0 / 105.0, -1.0 / 280.0)
time_step_sq = 0.0088

ROWS = 16
CELLS = 32
SPAN = CELLS + 16
NY = 128
NZ = 256
F32 = jnp.float32
LIMIT = 24 * 2**20


def pairs_by(move):
    pairs = []
    for shot in range(4):
        for sub in range(32):
            x = 2 * (sub // 16) + shot // 2
            target = move(x, shot % 2, (sub // 4) % 4, sub % 4)
            if target is None:
                continue
            tx, tcore, tz, ty = target
            pairs.append((shot * 32 + sub, ((tx % 2) * 2 + tcore) * 32 + (tx // 2) * 16 + tz * 4 + ty))
    return pairs


def send(value, move):
    return lax.ppermute(value, ("shot", "sub"), pairs_by(move))


def send_x(value, steps):
    return send(value, lambda x, c, z, y: ((x + steps) % 4, c, z, y))


def send_core(value):
    return send(value, lambda x, c, z, y: (x, 1 - c, z, y))


def send_z(value, steps):
    return send(value, lambda x, c, z, y: (x, c, (z + steps) % 4, y))


def send_y(value, steps):
    return send(value, lambda x, c, z, y: (x, c, z, (y + steps) % 4))


def next_rows(x, z, steps):
    group = (x // 2) * 4 + z + steps
    if group < 0 or group > 7:
        return None
    return (2 * (group // 4) + x % 2, group % 4)


def send_group(value, steps):
    def move(x, c, z, y):
        place = next_rows(x, z, steps)
        return None if place is None else (place[0], c, place[1], y)

    return send(value, move)


def send_cells(value, steps):
    return send(value, lambda x, c, z, y: (x, c, z, y + steps) if 0 <= y + steps < 4 else None)


def shape(*sizes):
    return jax.ShapeDtypeStruct(sizes, F32)


def region(rows, cells):
    return shape(rows, 2, cells, 128)


BLOCK = region(ROWS, CELLS)
NEAR = region(ROWS + 8, SPAN)
WIDE = region(ROWS + 16, SPAN)


def call(body, outs, n_smem, operands, scratch=()):
    specs = [pl.BlockSpec(memory_space=pltpu.SMEM)] * n_smem
    specs += [pl.BlockSpec(memory_space=pltpu.VMEM)] * (len(operands) - n_smem)
    return pl.pallas_call(
        body,
        out_shape=tuple(outs),
        in_specs=specs,
        out_specs=tuple(pl.BlockSpec(memory_space=pltpu.VMEM) for _ in outs),
        scratch_shapes=[pltpu.VMEM(s.shape, s.dtype) for s in scratch],
        compiler_params=pltpu.CompilerParams(vmem_limit_bytes=LIMIT),
    )(*operands)


def lanes():
    return lax.broadcasted_iota(jnp.int32, (8, 128), 1)


class Stencil:
    def __init__(self, source, row, cell, lane):
        self.source, self.row, self.cell, self.lane = source, row, cell, lane
        self.center = [self.load(0, 0, half) for half in (0, 1)]
        low, high = self.center
        self.deep = []
        for reach in range(1, 5):
            ahead = [pltpu.roll(v, 128 - reach, 1) for v in (low, high)]
            behind = [pltpu.roll(v, reach, 1) for v in (low, high)]
            front = lane < 128 - reach
            back = lane >= reach
            self.deep.append(
                (
                    (jnp.where(front, ahead[0], ahead[1]), jnp.where(front, ahead[1], 0.0)),
                    (jnp.where(back, behind[0], 0.0), jnp.where(back, behind[1], behind[0])),
                )
            )

    def load(self, rows, cells, half):
        first = self.cell + cells
        return self.source[self.row + rows, half, first : first + 8, :]

    def both(self, direction, reach, half):
        if direction == 0:
            return self.load(reach, 0, half), self.load(-reach, 0, half)
        if direction == 1:
            return self.load(0, reach, half), self.load(0, -reach, half)
        ahead, behind = self.deep[reach - 1]
        return ahead[half], behind[half]

    def derivative(self, direction, half):
        ahead, behind = self.both(direction, 1, half)
        total = ahead - behind
        for reach in range(2, 5):
            ahead, behind = self.both(direction, reach, half)
            total = total + (diff_coeffs[reach - 1] / diff_coeffs[0]) * (ahead - behind)
        return total

    def advanced(self, half, previous, speed_sq, slopes):
        center = self.center[half]
        lap = (3.0 * lap_coeffs[0] / lap_coeffs[1]) * center
        derived = [None, None, None]
        for reach in range(1, 5):
            around = None
            for direction in range(3):
                ahead, behind = self.both(direction, reach, half)
                pair = ahead + behind
                around = pair if around is None else around + pair
                part = ahead - behind
                if reach > 1:
                    part = derived[direction] + (diff_coeffs[reach - 1] / diff_coeffs[0]) * part
                derived[direction] = part
            if reach > 1:
                around = (lap_coeffs[reach] / lap_coeffs[1]) * around
            lap = lap + around
        result = 2.0 * center - previous + speed_sq * lap
        for direction in range(3):
            result = result - slopes[direction] * derived[direction]
        return result


def row_pairs(visit, first, last, cells):
    def step(pair, carry):
        for row in (first + 2 * pair, first + 2 * pair + 1):
            for cell in cells:
                visit(row, cell)
        return carry

    lax.fori_loop(0, (last - first) // 2, step, 0)


def over_block(visit):
    row_pairs(visit, 0, ROWS, range(0, CELLS, 8))


def over_near(visit):
    sides, middle = range(8, 8 + CELLS, 8), range(4, 12 + CELLS, 8)
    row_pairs(visit, 0, 4, sides)
    row_pairs(visit, 4, 4 + ROWS, middle)
    row_pairs(visit, 4 + ROWS, 8 + ROWS, sides)


def add_source(place, amount, first, target):
    @pl.when(place[first] > 0)
    def _():
        row, half = place[first + 1], place[first + 2]
        values = target[row, half]
        cell = lax.broadcasted_iota(jnp.int32, values.shape, 0)
        lane = lax.broadcasted_iota(jnp.int32, values.shape, 1)
        hit = (cell == place[first + 3]) & (lane == place[first + 4])
        target[row, half] = values + jnp.where(hit, amount, 0.0)


def near_step(source, old, model, lane, out, extra=None):
    speed_sq, slopes = model[0], model[1:]

    def visit(row, cell):
        stencil = Stencil(source, row + 4, cell, lane)
        cut = slice(cell, cell + 8)
        for half in (0, 1):
            value = stencil.advanced(
                half,
                old[row, half, cut, :],
                speed_sq[row, half, cut, :],
                [s[row, half, cut, :] for s in slopes],
            )
            if extra is not None:
                value = value + extra(row, half, cut)
            out[row, half, cut, :] = value

    over_near(visit)


def block_step(source, old, model, lane, finish):
    speed_sq, slopes = model[0], model[1:]

    def visit(row, cell):
        stencil = Stencil(source, row + 4, cell + 8, lane)
        near = slice(cell + 8, cell + 16)
        for half in (0, 1):
            value = stencil.advanced(
                half,
                old(row, half, slice(cell, cell + 8)),
                speed_sq[row + 4, half, near, :],
                [s[row + 4, half, near, :] for s in slopes],
            )
            finish(row, half, slice(cell, cell + 8), value)

    over_block(visit)


def of_block(ref):
    return lambda row, half, cut: ref[row, half, cut, :]


def of_near(ref):
    return lambda row, half, cut: ref[row + 4, half, cut.start + 8 : cut.stop + 8, :]


def of_wide(ref):
    return lambda row, half, cut: ref[row + 8, half, cut.start + 8 : cut.stop + 8, :]


def injected(maps, index, field):
    def near(row, half, cut):
        hits = maps[row, half, cut, 0:128]
        seen = maps[row, half, cut, 128 * index : 128 * index + 128]
        return hits * field[row, half, cut, :] - seen

    return near


def fill_wide(wide, block, halo):
    below, above, left, right, left_corners, right_corners = halo
    wide[0:8, :, 8 : 8 + CELLS, :] = below[...]
    wide[8 : 8 + ROWS, :, 8 : 8 + CELLS, :] = block[...]
    wide[8 + ROWS : 16 + ROWS, :, 8 : 8 + CELLS, :] = above[...]
    for cells, side, corners in (
        (slice(0, 8), left, left_corners),
        (slice(8 + CELLS, SPAN), right, right_corners),
    ):
        wide[4:8, :, cells, :] = corners[0:4]
        wide[8 : 8 + ROWS, :, cells, :] = side[...]
        wide[8 + ROWS : 12 + ROWS, :, cells, :] = corners[4:8]


WIDE_EDGES = [region(8, CELLS)] * 2 + [region(ROWS, 8)] * 2


def write_wide_edges(block, edges):
    low, high, low_cells, high_cells = edges
    low[...] = block[0:8]
    high[...] = block[ROWS - 8 : ROWS]
    low_cells[...] = block[:, :, 0:8, :]
    high_cells[...] = block[:, :, CELLS - 8 : CELLS, :]


def rim_body(below, above, low, high):
    for out, cut in ((low, slice(0, 8)), (high, slice(CELLS - 8, CELLS))):
        out[0:4] = below[4:8, :, cut, :]
        out[4:8] = above[0:4, :, cut, :]


def swap_wide_edges(edges):
    low, high, low_cells, high_cells = edges
    below, above = send_group(high, 1), send_group(low, -1)
    left, right = send_cells(high_cells, 1), send_cells(low_cells, -1)
    low_corners, high_corners = call(rim_body, [region(8, 8)] * 2, 0, (below, above))
    return below, above, left, right, send_cells(high_corners, 1), send_cells(low_corners, -1)


def cut_body(chunks, *refs, margins):
    count = len(margins)
    slabs, pieces = refs[:count], refs[count:]
    for turn in range(4):
        chunk = chunks[turn]
        first = pl.multiple_of(chunk * CELLS, CELLS)
        before = pl.multiple_of(jnp.maximum(first - 8, 0), 8)
        after = pl.multiple_of(jnp.minimum(first + CELLS, NY - 8), 8)
        at = 0
        for slab, margin in zip(slabs, margins):
            if margin:
                pieces[turn][:, at : at + 8, :] = jnp.where(chunk > 0, slab[:, pl.ds(before, 8), :], 0.0)
                at += 8
            pieces[turn][:, at : at + CELLS, :] = slab[:, pl.ds(first, CELLS), :]
            at += CELLS
            if margin:
                pieces[turn][:, at : at + 8, :] = jnp.where(chunk < 3, slab[:, pl.ds(after, 8), :], 0.0)
                at += 8


def cut_pieces(slabs, margins, chunks):
    width = sum(SPAN if margin else CELLS for margin in margins)
    pieces = call(functools.partial(cut_body, margins=margins), [shape(4, width, NZ)] * 4, 1, (chunks, *slabs))
    return pieces


def place_pieces(slots, pieces, outs):
    for turn in range(4):
        slot = pl.multiple_of(slots[turn] * 4, 4)
        at = 0
        for out in outs:
            width = out.shape[2]
            for half in (0, 1):
                out[pl.ds(slot, 4), half] = pieces[turn][:, at : at + width, 128 * half : 128 * half + 128]
            at += width


def gather_body(slots, *refs, depths):
    pieces, outs = refs[:4], refs[4:]
    low, high = outs[-2:]
    place_pieces(slots, pieces, outs[:-2])
    at = 0
    core = slice(8, 8 + CELLS)
    for out, depth in zip(outs, depths):
        if depth == 8:
            low[:, :, at : at + SPAN, :] = out[0:4]
            high[:, :, at : at + SPAN, :] = out[ROWS - 4 : ROWS]
            at += SPAN
            low[:, :, at : at + CELLS, :] = out[4:8, :, core, :]
            high[:, :, at : at + CELLS, :] = out[ROWS - 8 : ROWS - 4, :, core, :]
            at += CELLS
        elif depth == 4:
            low[:, :, at : at + CELLS, :] = out[0:4, :, core, :]
            high[:, :, at : at + CELLS, :] = out[ROWS - 4 : ROWS, :, core, :]
            at += CELLS


def gather_blocks(pieces, slots, depths):
    outs = [region(ROWS, SPAN if depth else CELLS) for depth in depths]
    packed = sum({8: SPAN + CELLS, 4: CELLS, 0: 0}[depth] for depth in depths)
    outs += [region(4, packed)] * 2
    return call(functools.partial(gather_body, depths=depths), outs, 1, (slots, *pieces))


def stack_wide(out, below, middle, above, at):
    core = slice(8, 8 + CELLS)
    end = at + SPAN + CELLS
    out[0:4, :, core, :] = below[:, :, at + SPAN : end, :]
    out[4:8] = below[:, :, at : at + SPAN, :]
    out[8 : 8 + ROWS] = middle[...]
    out[8 + ROWS : 12 + ROWS] = above[:, :, at : at + SPAN, :]
    out[12 + ROWS : 16 + ROWS, :, core, :] = above[:, :, at + SPAN : end, :]


def stack_near(out, below, middle, above, at):
    core = slice(8, 8 + CELLS)
    out[0:4, :, core, :] = below[:, :, at : at + CELLS, :]
    out[4 : 4 + ROWS] = middle[...]
    out[4 + ROWS : 8 + ROWS, :, core, :] = above[:, :, at : at + CELLS, :]


def fields_body(now, old, adjoint, below, above, wide, old_near, adjoint_near):
    stack_wide(wide, below, now, above, 0)
    stack_near(old_near, below, old, above, SPAN + CELLS)
    stack_near(adjoint_near, below, adjoint, above, SPAN + 2 * CELLS)


def model_body(log_mass, speed, below, above, speed_sq, s0, s1, s2, twice, wide, speed_near):
    stack_wide(wide, below, log_mass, above, 0)
    stack_near(speed_near, below, speed, above, SPAN + CELLS)
    twice[...] = 2.0 / speed[:, :, 8 : 8 + CELLS, :]
    lane = lanes()

    def visit(row, cell):
        stencil = Stencil(wide, row + 4, cell, lane)
        cut = slice(cell, cell + 8)
        for half in (0, 1):
            value = speed_near[row, half, cut, :]
            scale = time_step_sq * value * value
            speed_sq[row, half, cut, :] = lap_coeffs[1] * scale
            scale = (diff_coeffs[0] * diff_coeffs[0]) * scale
            for direction, out in enumerate((s0, s1, s2)):
                out[row, half, cut, :] = scale * stencil.derivative(direction, half)

    over_near(visit)


def forward_body(place, amount, wide, old, speed_sq, s0, s1, s2, near, new, *edges):
    model = (speed_sq, s0, s1, s2)
    lane = lanes()
    near_step(wide, old, model, lane, near)
    add_source(place, amount[0], 0, near)

    def finish(row, half, cut, value):
        new[row, half, cut, :] = value

    block_step(near, of_wide(wide), model, lane, finish)
    add_source(place, amount[1], 5, new)
    write_wide_edges(new, edges)


def write_pieces(slots, block, pieces, at):
    for turn in range(4):
        slot = pl.multiple_of(slots[turn] * 4, 4)
        for half in (0, 1):
            pieces[turn][:, at : at + CELLS, 128 * half : 128 * half + 128] = block[pl.ds(slot, 4), half]


def turn_body(place, amount, block, *refs):
    halo, refs = refs[:6], refs[6:]
    old, speed_sq, s0, s1, s2, adjoint, later, maps, near, new, adjoint_new, summed = refs[:12]
    edges, wide = refs[12:16], refs[16]
    model = (speed_sq, s0, s1, s2)
    lane = lanes()
    fill_wide(wide, block, halo)
    near_step(wide, old, model, lane, near)
    add_source(place, amount[2], 0, near)

    def finish(row, half, cut, value):
        new[row, half, cut, :] = value

    block_step(near, of_block(block), model, lane, finish)
    add_source(place, amount[3], 5, new)

    def finish_adjoint(row, half, cut, value):
        hits = of_near(maps)(row, half, cut)
        ahead = new[row, half, cut, :]
        value = value + (hits[:, 0:128] * ahead - hits[:, 4 * 128 : 5 * 128])
        adjoint_new[row, half, cut, :] = value
        summed[row, half, cut, :] = value * (
            ahead - 2.0 * of_near(near)(row, half, cut) + block[row, half, cut, :]
        )

    block_step(adjoint, of_block(later), model, lane, finish_adjoint)
    write_wide_edges(adjoint_new, edges)


def adjoint_body(block, *refs):
    halo, refs = refs[:6], refs[6:]
    old, speed_sq, s0, s1, s2, maps, u3, u2, u1, u0, sums = refs[:11]
    near, new, summed, low, high, low_cells, high_cells, wide = refs[11:]
    model = (speed_sq, s0, s1, s2)
    lane = lanes()
    fill_wide(wide, block, halo)
    near_step(wide, old, model, lane, near, injected(maps, 3, u3))

    def finish(row, half, cut, value):
        hits = of_near(maps)(row, half, cut)
        third = of_near(u3)(row, half, cut)
        second = u2[row, half, cut, :]
        first = of_near(u1)(row, half, cut)
        zeroth = of_wide(u0)(row, half, cut)
        value = value + (hits[:, 0:128] * second - hits[:, 2 * 128 : 3 * 128])
        new[row, half, cut, :] = value
        total = sums[row, half, cut, :]
        total = total + of_near(near)(row, half, cut) * (third - 2.0 * second + first)
        summed[row, half, cut, :] = total + value * (second - 2.0 * first + zeroth)

    block_step(near, of_block(block), model, lane, finish)
    low[...] = new[0:4]
    high[...] = new[ROWS - 4 : ROWS]
    low_cells[...] = new[:, :, 0:8, :]
    high_cells[...] = new[:, :, CELLS - 8 : CELLS, :]


def last_body(
    slots, model_slots, block, below, above, left, right, old, speed_sq, s0, s1, s2, maps,
    u1, u0, u_before, sums, twice, u4, p0, p1, p2, p3, q0, q1, q2, q3, near, new, image,
):
    near[0:4, :, 8 : 8 + CELLS, :] = below[...]
    near[4 : 4 + ROWS, :, 8 : 8 + CELLS, :] = block[...]
    near[4 + ROWS : 8 + ROWS, :, 8 : 8 + CELLS, :] = above[...]
    near[4 : 4 + ROWS, :, 0:8, :] = left[...]
    near[4 : 4 + ROWS, :, 8 + CELLS : SPAN, :] = right[...]
    lane = lanes()

    def finish(row, half, cut, value):
        hits = of_near(maps)(row, half, cut)
        first = of_near(u1)(row, half, cut)
        value = value + (hits[:, 0:128] * first - hits[:, 128:256])
        new[row, half, cut, :] = value
        curvature = first - 2.0 * of_wide(u0)(row, half, cut) + of_near(u_before)(row, half, cut)
        image[row, half, cut, :] = twice[row, half, cut, :] * (sums[row, half, cut, :] + value * curvature)

    block_step(near, of_near(old), (speed_sq, s0, s1, s2), lane, finish)
    write_pieces(model_slots, image, (p0, p1, p2, p3), 0)
    write_pieces(slots, new, (q0, q1, q2, q3), 0)
    write_pieces(slots, u4, (q0, q1, q2, q3), CELLS)


def spread_body(chunks, p0, p1, p2, p3, *outs):
    for turn, piece in enumerate((p0, p1, p2, p3)):
        first = pl.multiple_of(chunks[turn] * CELLS, CELLS)
        for index, out in enumerate(outs):
            out[:, pl.ds(first, CELLS), :] = piece[:, CELLS * index : CELLS * index + CELLS, :]


def sent_pieces(pieces):
    return [pieces[0]] + [send_y(pieces[turn], turn) for turn in (1, 2, 3)]


def to_slabs(pieces, chunks, count):
    return call(spread_body, [shape(4, NY, NZ)] * count, 1, (chunks, *pieces))


def on_device(
    velocity,
    density,
    aperture_start,
    source_cell,
    receiver_cells,
    wavelet,
    observed,
    forward_old,
    forward_now,
    adjoint_later,
    adjoint_now,
):
    shot = lax.axis_index("shot")
    sub = lax.axis_index("sub")
    core = shot % 2
    x_hi = sub // 16
    x = 2 * x_hi + shot // 2
    z = (sub // 4) % 4
    y = sub % 4
    group = sub // 4
    start = aperture_start[0]
    partner = send_core(aperture_start)

    def wanted(first_slab):
        upper = first_slab // 4 + (y < first_slab % 4).astype(jnp.int32)
        block = jnp.clip(x_hi + (upper - z + 3) // 4, 0, 7)
        position = 2 * (block % 2) + block // 4
        return (block // 2) % 2, (position - x) % 4, upper % 4

    own_core, own_step, turn_by = wanted(start)
    turns = jnp.arange(4, dtype=jnp.int32)
    chunks_out = (y + turns) % 4
    chunks_in = (y - turns) % 4
    slots_in = (y - turns - start % 4) % 4
    slots_out = (y + turns - start % 4) % 4

    pieces = cut_pieces(
        [forward_now[0], forward_old[0], adjoint_now[0], adjoint_later[0]],
        (True, True, True, False),
        chunks_out,
    )
    velocity, partner, *pieces = lax.optimization_barrier((velocity, partner, *pieces))
    pair_core, pair_step, _ = wanted(partner[0])

    def gathered(slab):
        from_below = send_x(slab, 1)
        from_above = send_x(slab, -1)
        far = jnp.concatenate([send_x(from_below[0:2], 1), send_x(from_above[2:4], -1)])

        def pick(step):
            return jnp.where(
                step < 2, jnp.where(step == 0, slab, from_above), jnp.where(step == 2, far, from_below)
            )

        other = send_core(pick(pair_step))
        return jnp.where(own_core == core, pick(own_step), other)

    def turned(arrays, steps):
        def branch(count):
            return lambda *values: tuple(send_z(value, count) if count else value for value in values)

        return lax.switch(steps, [branch(count) for count in (0, 1, 2, -1)], *arrays)

    log_slab = gathered(jnp.log(density))
    speed_slab = gathered(velocity)
    pieces = sent_pieces(pieces)

    def local_place(cells, rows_more, cells_more):
        rows = cells // (NY * NZ) - group * ROWS + rows_more
        columns = (cells // NZ) % NY - y * CELLS + cells_more
        inside = (rows >= 0) & (rows < ROWS + 2 * rows_more)
        inside = inside & (columns >= 0) & (columns < CELLS + 2 * cells_more)
        return inside, rows, (cells // 128) % 2, columns, cells % 128

    inside, rows, half, columns, lane = local_place(receiver_cells[0], 4, 8)
    line = jnp.where(inside, (rows * 2 + half) * SPAN + columns, -1)
    lines = (ROWS + 8) * 2 * SPAN
    on_line = (jnp.arange(lines, dtype=jnp.int32)[:, None] == line[None, :]).astype(F32)
    weights = jnp.concatenate([jnp.ones_like(observed[0, :1]), observed[0]])
    hit = lane[:, None, None] == jnp.arange(128, dtype=jnp.int32)[None, None, :]
    at_lane = jnp.where(hit, weights.T[:, :, None], 0.0).reshape(-1, 5 * 128)
    maps = jnp.dot(on_line, at_lane, precision=lax.Precision.HIGHEST)
    maps = maps.reshape(ROWS + 8, 2, SPAN, 5 * 128)

    def source_place(rows_more, cells_more):
        inside, rows, half, columns, lane = local_place(source_cell[0], rows_more, cells_more)
        rows = jnp.clip(rows, 0, ROWS + 2 * rows_more - 1)
        return [inside.astype(jnp.int32), rows, half, columns, lane]

    place = jnp.stack(source_place(4, 8) + source_place(0, 0))
    amount = wavelet[0]

    log_slab, speed_slab = lax.optimization_barrier((log_slab, speed_slab))
    log_slab, speed_slab = turned((log_slab, speed_slab), (4 - turn_by) % 4)
    log_slab, speed_slab, *pieces = lax.optimization_barrier((log_slab, speed_slab, *pieces))
    model_pieces = sent_pieces(cut_pieces([log_slab, speed_slab], (True, True), chunks_out))
    now, old, adjoint, a_later, side_low, side_high = gather_blocks(pieces, chunks_in, (8, 4, 4, 0))
    below, above = send_group(side_high, 1), send_group(side_low, -1)
    u_wide, old_near, a_near = call(
        fields_body, [WIDE, NEAR, NEAR], 0, (now, old, adjoint, below, above)
    )
    log_mass, speed, side_low, side_high = gather_blocks(model_pieces, slots_in, (8, 4))
    below, above = send_group(side_high, 1), send_group(side_low, -1)
    below, above, maps = lax.optimization_barrier((below, above, maps))
    *model, twice = call(
        model_body, [NEAR] * 4 + [BLOCK], 0, (log_mass, speed, below, above), (WIDE, NEAR)
    )

    u1, u2, *edges = call(
        forward_body, [NEAR, BLOCK] + WIDE_EDGES, 2, (place, amount, u_wide, old_near, *model)
    )
    halo = swap_wide_edges(edges)
    u3, u4, a3, sums, *edges = call(
        turn_body,
        [NEAR, BLOCK, BLOCK, BLOCK] + WIDE_EDGES,
        2,
        (place, amount, u2, *halo, u1, *model, a_near, a_later, maps),
        (WIDE,),
    )
    halo = swap_wide_edges(edges)
    a2, a1, sums, side_low, side_high, low_cells, high_cells = call(
        adjoint_body,
        [NEAR, BLOCK, BLOCK] + [region(4, CELLS)] * 2 + [region(ROWS, 8)] * 2,
        0,
        (a3, *halo, a_near, *model, maps, u3, u2, u1, u_wide, sums),
        (WIDE,),
    )
    halo = (
        send_group(side_high, 1),
        send_group(side_low, -1),
        send_cells(high_cells, 1),
        send_cells(low_cells, -1),
    )
    pieces = call(
        last_body,
        [shape(4, CELLS, NZ)] * 4 + [shape(4, 2 * CELLS, NZ)] * 4,
        2,
        (chunks_out, slots_out, a1, *halo, a2, *model, maps, u1, u_wide, old_near, sums, twice, u4),
        (NEAR, BLOCK, BLOCK),
    )
    pieces = lax.optimization_barrier((*sent_pieces(pieces[:4]), *pieces[4:]))
    (image,) = to_slabs(pieces[:4], chunks_in, 1)

    def both(first_half, second_half):
        return jnp.concatenate([first_half, second_half])

    (image,) = turned((image,), turn_by)
    image, *pieces = lax.optimization_barrier((image, *sent_pieces(pieces[4:])))
    adjoint_first, forward_last = to_slabs(pieces, chunks_in, 2)
    other = send_core(image)

    def share(step):
        mine = jnp.where((own_core == core) & (own_step == step), image, 0.0)
        return mine + jnp.where((pair_core == core) & (pair_step == step), other, 0.0)

    far = share(2)
    passing_up = send_x(far[0:2], 1)
    passing_down = send_x(far[2:4], -1)
    up = share(1)
    down = share(3)
    up = send_x(both(up[0:2] + passing_up, up[2:4]), 1)
    down = send_x(both(down[0:2], down[2:4] + passing_down), -1)
    gradient = share(0) + up + down
    return (gradient, forward_last[None], adjoint_first[None])


def solution(mesh):
    placed = (
        P(("shot", "sub"), None, None),
        P(("shot", "sub"), None, None),
        P("shot"),
        P("shot"),
        P("shot", None),
        P("shot", None),
        P("shot", None, None),
        P("shot", "sub", None, None),
        P("shot", "sub", None, None),
        P("shot", "sub", None, None),
        P("shot", "sub", None, None),
    )
    return jax.shard_map(
        on_device,
        mesh=mesh,
        in_specs=placed,
        out_specs=(
            P(("shot", "sub"), None, None),
            P("shot", "sub", None, None),
            P("shot", "sub", None, None),
        ),
        check_vma=False,
    )
```

profile of v0, /device:TPU:0, one launch (start us, length us, event | category | flops | bytes accessed | tf_op | source)
XLA Modules:
  0.0 274.2 jit_solution(8901545039193777827)
XLA Ops:
  13.1 5.8 %collective-permute-done.10 = f32[4,128,256]{2,1,0:T(8,128)S(1)} collective-permute-done((f32[4,128,256]{2,1,0:T(8,128)}, f32[4,128,256]{2,1,0:T(8,128)S(1)}, u32[]{:S(2)}, u32[]{:S(2)}) %collective-permute-start.10) | collective-permute-done | bytes 524320 | tf_op jit(solution)/shard_map/ppermute | solution.py:37
  30.2 3.3 %collective-permute-start.21 = (f32[4,176,256]{2,1,0:T(8,128)}, f32[4,176,256]{2,1,0:T(8,128)S(1)}, u32[]{:S(2)}, u32[]{:S(2)}) collective-permute-start(f32[4,176,256]{2,1,0:T(8,128)} %get-tuple-element.135), channel_id=1, source_target_pairs={{0,2},{1,3},{2,0},{3,1},{4,6},{5,7},{6,4},{7,5},{8,10},{9,11},{10,... | collective-permute-start | bytes 2162696 | tf_op jit(solution)/shard_map/ppermute | solution.py:37
  37.9 3.0 %collective-permute-start.18 = (f32[2,128,256]{2,1,0:T(8,128)S(1)}, f32[2,128,256]{2,1,0:T(8,128)S(1)}, u32[]{:S(2)}, u32[]{:S(2)}) collective-permute-start(f32[2,128,256]{2,1,0:T(8,128)S(1)} %slice.43), channel_id=1, source_target_pairs={{0,80},{1,81},{2,82},{3,83},{4,84},{5,85},{6,86},{7,87},{8,88},{9,... | collective-permute-start | bytes 786440 | tf_op jit(solution)/shard_map/ppermute | solution.py:37
  50.6 11.2 %collective-permute-done.21.refs_2_ = f32[4,176,256]{2,1,0:T(8,128)S(1)} collective-permute-done((f32[4,176,256]{2,1,0:T(8,128)}, f32[4,176,256]{2,1,0:T(8,128)S(1)}, u32[]{:S(2)}, u32[]{:S(2)}) %collective-permute-start.21) | collective-permute-done | bytes 720928 | tf_op jit(solution)/shard_map/ppermute | solution.py:37
  72.3 3.9 %collective-permute-start.23 = (f32[4,2,144,128]{3,2,1,0:T(8,128)S(1)}, f32[4,2,144,128]{3,2,1,0:T(8,128)S(1)}, u32[]{:S(2)}, u32[]{:S(2)}) collective-permute-start(f32[4,2,144,128]{3,2,1,0:T(8,128)S(1)} %get-tuple-element.144), channel_id=1, source_target_pairs={{0,4},{1,5},{2,6},{3,7},{4,8},{5,9},{6,10},{7,11},{8,12},{9,13},{1... | collective-permute-start | bytes 1769480 | tf_op jit(solution)/shard_map/ppermute | solution.py:37
  78.3 9.6 %collective-permute-done.26.refs_2_ = f32[4,96,256]{2,1,0:T(8,128)} collective-permute-done((f32[4,96,256]{2,1,0:T(8,128)}, f32[4,96,256]{2,1,0:T(8,128)}, u32[]{:S(2)}, u32[]{:S(2)}) %collective-permute-start.26) | collective-permute-done | bytes 393248 | tf_op jit(solution)/shard_map/ppermute | solution.py:37
  89.3 3.9 %collective-permute-start.28 = (f32[4,2,112,128]{3,2,1,0:T(8,128)S(1)}, f32[4,2,112,128]{3,2,1,0:T(8,128)S(1)}, u32[]{:S(2)}, u32[]{:S(2)}) collective-permute-start(f32[4,2,112,128]{3,2,1,0:T(8,128)S(1)} %get-tuple-element.156), channel_id=1, source_target_pairs={{0,4},{1,5},{2,6},{3,7},{4,8},{5,9},{6,10},{7,11},{8,12},{9,13},{1... | collective-permute-start | bytes 1376264 | tf_op jit(solution)/shard_map/ppermute | solution.py:37
  94.7 3.2 %fusion.refs_13_.refs_11_.maps = f32[24,2,48,640]{3,2,1,0:T(8,128)S(1)} fusion(f32[256,640,1,1]{0,1,3,2:T(8,128)S(1)} %bitcast.41, s32[256]{0:T(256)S(1)} %bitcast.44, s32[24,2,48]{2,1,0:T(2,128)S(1)} %multiply_add_fusion), kind=kOutput, calls=%fused_computation | convolution fusion | flops 4530438144 | bytes 6563840 | tf_op jit(solution)/shard_map/dot_general | solution.py:603
  98.1 4.1 %collective-permute-done.28.below = f32[4,2,112,128]{3,2,1,0:T(8,128)S(1)} collective-permute-done((f32[4,2,112,128]{3,2,1,0:T(8,128)S(1)}, f32[4,2,112,128]{3,2,1,0:T(8,128)S(1)}, u32[]{:S(2)}, u32[]{:S(2)}) %collective-permute-start.28) | collective-permute-done | bytes 458784 | tf_op jit(solution)/shard_map/ppermute | solution.py:37
  102.2 4.3 %collective-permute-done.29.above = f32[4,2,112,128]{3,2,1,0:T(8,128)S(1)} collective-permute-done((f32[4,2,112,128]{3,2,1,0:T(8,128)S(1)}, f32[4,2,112,128]{3,2,1,0:T(8,128)S(1)}, u32[]{:S(2)}, u32[]{:S(2)}) %collective-permute-start.29) | collective-permute-done | bytes 458784 | tf_op jit(solution)/shard_map/ppermute | solution.py:37
  106.5 2.9 %shard_map.135 = (f32[24,2,48,128]{3,2,1,0:T(8,128)S(1)}, f32[24,2,48,128]{3,2,1,0:T(8,128)S(1)}, f32[24,2,48,128]{3,2,1,0:T(8,128)S(1)}, f32[24,2,48,128]{3,2,1,0:T(8,128)S(1)}, f32[16,2,32,128]{3,2,1,0:T(8,128)S(1)}) custom-call(f32[16,2,48,128]{3,2,1,0:T(8,128)S(1)} %get-tuple-element.154.log_mass, f32[16,2,48,128]{3,2,1,0:T(8,128)S(1)} %get-tuple-element.155.speed, ...), custom_call_target="tpu_custom_call" | custom-call | tf_op jit(solution)/shard_map/pallas_call | solution.py:91
  109.5 5.4 %shard_map.136 = (f32[24,2,48,128]{3,2,1,0:T(8,128)S(1)}, f32[16,2,32,128]{3,2,1,0:T(8,128)S(1)}, f32[8,2,32,128]{3,2,1,0:T(8,128)S(1)}, f32[8,2,32,128]{3,2,1,0...) custom-call(s32[10]{0:T(128)S(1)} %stack.45.place, f32[4]{0:T(128)S(1)} %bitcast.39, ...), custom_call_target="tpu_custom_call" | custom-call | tf_op jit(solution)/shard_map/pallas_call | solution.py:91
  114.9 3.6 %collective-permute-start.30 = (f32[8,2,32,128]{3,2,1,0:T(8,128)S(1)}, f32[8,2,32,128]{3,2,1,0:T(8,128)S(1)}, u32[]{:S(2)}, u32[]{:S(2)}) collective-permute-start(f32[8,2,32,128]{3,2,1,0:T(8,128)S(1)} %get-tuple-element.165), channel_id=1, source_target_pairs={{0,4},{1,5},{2,6},{3,7},{4,8},{5,9},{6,10},{7,11},{8,12},{9,13},{1... | collective-permute-start | bytes 786440 | tf_op jit(solution)/shard_map/ppermute | solution.py:37
  119.9 3.4 %collective-permute-start.32 = (f32[16,2,8,128]{3,2,1,0:T(8,128)S(1)}, f32[16,2,8,128]{3,2,1,0:T(8,128)S(1)}, u32[]{:S(2)}, u32[]{:S(2)}) collective-permute-start(f32[16,2,8,128]{3,2,1,0:T(8,128)S(1)} %get-tuple-element.167), channel_id=1, source_target_pairs={{0,1},{1,2},{2,3},{4,5},{5,6},{6,7},{8,9},{9,10},{10,11},{12,13},{... | collective-permute-start | bytes 393224 | tf_op jit(solution)/shard_map/ppermute | solution.py:37
  126.8 3.8 %collective-permute-start.34 = (f32[8,2,8,128]{3,2,1,0:T(8,128)S(1)}, f32[8,2,8,128]{3,2,1,0:T(8,128)S(1)}, u32[]{:S(2)}, u32[]{:S(2)}) collective-permute-start(f32[8,2,8,128]{3,2,1,0:T(8,128)S(1)} %get-tuple-element.169), channel_id=1, source_target_pairs={{0,1},{1,2},{2,3},{4,5},{5,6},{6,7},{8,9},{9,10},{10,11},{12,13},{... | collective-permute-start | bytes 196616 | tf_op jit(solution)/shard_map/ppermute | solution.py:37
  132.5 4.3 %collective-permute-done.35.refs_5_ = f32[8,2,8,128]{3,2,1,0:T(8,128)S(1)} collective-permute-done((f32[8,2,8,128]{3,2,1,0:T(8,128)S(1)}, f32[8,2,8,128]{3,2,1,0:T(8,128)S(1)}, u32[]{:S(2)}, u32[]{:S(2)}) %collective-permute-start.35) | collective-permute-done | bytes 65568 | tf_op jit(solution)/shard_map/ppermute | solution.py:37
  136.8 7.5 %shard_map.138 = (f32[24,2,48,128]{3,2,1,0:T(8,128)S(1)}, f32[16,2,32,128]{3,2,1,0:T(8,128)S(1)}, f32[16,2,32,128]{3,2,1,0:T(8,128)S(1)}, f32[16,2,32,128]{3,2,1...) custom-call(s32[10]{0:T(128)S(1)} %stack.45.place, ...), custom_call_target="tpu_custom_call" | custom-call | tf_op jit(solution)/shard_map/pallas_call | solution.py:91
  144.3 5.8 %collective-permute-start.36 = (f32[8,2,32,128]{3,2,1,0:T(8,128)S(1)}, f32[8,2,32,128]{3,2,1,0:T(8,128)S(1)}, u32[]{:S(2)}, u32[]{:S(2)}) collective-permute-start(f32[8,2,32,128]{3,2,1,0:T(8,128)S(1)} %get-tuple-element.176), channel_id=1, source_target_pairs={{0,4},{1,5},{2,6},{3,7},{4,8},{5,9},{6,10},{7,11},{8,12},{9,13},{1... | collective-permute-start | bytes 786440 | tf_op jit(solution)/shard_map/ppermute | solution.py:37
  163.0 4.3 %collective-permute-done.41.refs_5_ = f32[8,2,8,128]{3,2,1,0:T(8,128)S(1)} collective-permute-done((f32[8,2,8,128]{3,2,1,0:T(8,128)S(1)}, f32[8,2,8,128]{3,2,1,0:T(8,128)S(1)}, u32[]{:S(2)}, u32[]{:S(2)}) %collective-permute-start.41) | collective-permute-done | bytes 65568 | tf_op jit(solution)/shard_map/ppermute | solution.py:37
  167.3 5.2 %shard_map.140 = (f32[24,2,48,128]{3,2,1,0:T(8,128)S(1)}, f32[16,2,32,128]{3,2,1,0:T(8,128)S(1)}, f32[16,2,32,128]{3,2,1,0:T(8,128)S(1)}, f32[4,2,32,128]{3,2,1,...) custom-call(f32[16,2,32,128]{3,2,1,0:T(8,128)S(1)} %get-tuple-element.17, ...), custom_call_target="tpu_custom_call" | custom-call | tf_op jit(solution)/shard_map/pallas_call | solution.py:91
  172.6 5.5 %collective-permute-start.42 = (f32[4,2,32,128]{3,2,1,0:T(8,128)S(1)}, f32[4,2,32,128]{3,2,1,0:T(8,128)S(1)}, u32[]{:S(2)}, u32[]{:S(2)}) collective-permute-start(f32[4,2,32,128]{3,2,1,0:T(8,128)S(1)} %get-tuple-element.185), channel_id=1, source_target_pairs={{0,4},{1,5},{2,6},{3,7},{4,8},{5,9},{6,10},{7,11},{8,12},{9,13},{1... | collective-permute-start | bytes 393224 | tf_op jit(solution)/shard_map/ppermute | solution.py:37
  179.4 3.9 %collective-permute-start.44 = (f32[16,2,8,128]{3,2,1,0:T(8,128)S(1)}, f32[16,2,8,128]{3,2,1,0:T(8,128)S(1)}, u32[]{:S(2)}, u32[]{:S(2)}) collective-permute-start(f32[16,2,8,128]{3,2,1,0:T(8,128)S(1)} %get-tuple-element.187), channel_id=1, source_target_pairs={{0,1},{1,2},{2,3},{4,5},{5,6},{6,7},{8,9},{9,10},{10,11},{12,13},{... | collective-permute-start | bytes 393224 | tf_op jit(solution)/shard_map/ppermute | solution.py:37
  186.1 4.9 %collective-permute-done.45.right = f32[16,2,8,128]{3,2,1,0:T(8,128)S(1)} collective-permute-done((f32[16,2,8,128]{3,2,1,0:T(8,128)S(1)}, f32[16,2,8,128]{3,2,1,0:T(8,128)S(1)}, u32[]{:S(2)}, u32[]{:S(2)}) %collective-permute-start.45) | collective-permute-done | bytes 131104 | tf_op jit(solution)/shard_map/ppermute | solution.py:37
  197.3 7.7 %collective-permute-done.46.p1 = f32[4,32,256]{2,1,0:T(8,128)S(1)} collective-permute-done((f32[4,32,256]{2,1,0:T(8,128)S(1)}, f32[4,32,256]{2,1,0:T(8,128)S(1)}, u32[]{:S(2)}, u32[]{:S(2)}) %collective-permute-start.46) | collective-permute-done | bytes 131104 | tf_op jit(solution)/shard_map/ppermute | solution.py:37
  205.1 3.5 %collective-permute-start.50 = (f32[4,64,256]{2,1,0:T(8,128)S(1)}, f32[4,64,256]{2,1,0:T(8,128)S(1)}, u32[]{:S(2)}, u32[]{:S(2)}) collective-permute-start(f32[4,64,256]{2,1,0:T(8,128)S(1)} %get-tuple-element.207), channel_id=1, source_target_pairs={{0,2},{1,3},{2,0},{3,1},{4,6},{5,7},{6,4},{7,5},{8,10},{9,11},{10,... | collective-permute-start | bytes 786440 | tf_op jit(solution)/shard_map/ppermute | solution.py:37
  209.5 3.1 %collective-permute-done.49.p1 = f32[4,64,256]{2,1,0:T(8,128)S(1)} collective-permute-done((f32[4,64,256]{2,1,0:T(8,128)S(1)}, f32[4,64,256]{2,1,0:T(8,128)S(1)}, u32[]{:S(2)}, u32[]{:S(2)}) %collective-permute-start.49) | collective-permute-done | bytes 262176 | tf_op jit(solution)/shard_map/ppermute | solution.py:37
  212.6 3.0 %collective-permute-done.50.p2 = f32[4,64,256]{2,1,0:T(8,128)S(1)} collective-permute-done((f32[4,64,256]{2,1,0:T(8,128)S(1)}, f32[4,64,256]{2,1,0:T(8,128)S(1)}, u32[]{:S(2)}, u32[]{:S(2)}) %collective-permute-start.50) | collective-permute-done | bytes 262176 | tf_op jit(solution)/shard_map/ppermute | solution.py:37
  218.5 29.1 %collective-permute-start.55 = (f32[2,128,256]{2,1,0:T(8,128)S(1)}, f32[2,128,256]{2,1,0:T(8,128)S(1)}, u32[]{:S(2)}, u32[]{:S(2)}) collective-permute-start(f32[2,128,256]{2,1,0:T(8,128)S(1)} %get-tuple-element.222), channel_id=1, source_target_pairs={{0,80},{1,81},{2,82},{3,83},{4,84},{5,85},{6,86},{7,87},{8,88},{9,... | collective-permute-start | bytes 786440 | tf_op jit(solution)/shard_map/ppermute | solution.py:37
  247.6 5.9 %collective-permute-done.55 = f32[2,128,256]{2,1,0:T(8,128)S(1)} collective-permute-done((f32[2,128,256]{2,1,0:T(8,128)S(1)}, f32[2,128,256]{2,1,0:T(8,128)S(1)}, u32[]{:S(2)}, u32[]{:S(2)}) %collective-permute-start.55) | collective-permute-done | bytes 262176 | tf_op jit(solution)/shard_map/ppermute | solution.py:37
  254.4 3.7 %collective-permute-start.56 = (f32[4,128,256]{2,1,0:T(8,128)}, f32[4,128,256]{2,1,0:T(8,128)S(1)}, u32[]{:S(2)}, u32[]{:S(2)}) collective-permute-start(f32[4,128,256]{2,1,0:T(8,128)} %pad_maximum_fusion.1), channel_id=1, source_target_pairs={{0,80},{1,81},{2,82},{3,83},{4,84},{5,85},{6,86},{7,87},{8,88},{9,... | collective-permute-start | bytes 1572872 | tf_op jit(solution)/shard_map/ppermute | solution.py:37
  260.5 8.5 %collective-permute-done.56 = f32[4,128,256]{2,1,0:T(8,128)S(1)} collective-permute-done((f32[4,128,256]{2,1,0:T(8,128)}, f32[4,128,256]{2,1,0:T(8,128)S(1)}, u32[]{:S(2)}, u32[]{:S(2)}) %collective-permute-start.56) | collective-permute-done | bytes 524320 | tf_op jit(solution)/shard_map/ppermute | solution.py:37
  269.0 4.2 %collective-permute-done.54 = f32[4,128,256]{2,1,0:T(8,128)S(1)} collective-permute-done((f32[4,128,256]{2,1,0:T(8,128)}, f32[4,128,256]{2,1,0:T(8,128)S(1)}, u32[]{:S(2)}, u32[]{:S(2)}) %collective-permute-start.54) | collective-permute-done | bytes 524320 | tf_op jit(solution)/shard_map/ppermute | solution.py:37
  (141 shorter events, 87.0 us)
Async XLA Ops:
  2.6 16.3 %collective-permute-start.10 = (f32[4,128,256]{2,1,0:T(8,128)}, f32[4,128,256]{2,1,0:T(8,128)S(1)}, u32[]{:S(2)}, u32[]{:S(2)}) collective-permute-start(f32[4,128,256]{2,1,0:T(8,128)} %log.3), channel_id=1, source_target_pairs={{0,64},{1,65},{2,66},{3,67},{4,68},{5,69},{6,70},{7,71},{8,72},{9,... | collective-permute-start | bytes 1572872 | tf_op jit(solution)/shard_map/ppermute | solution.py:37
  4.2 16.7 %collective-permute-start.9 = (f32[4,128,256]{2,1,0:T(8,128)}, f32[4,128,256]{2,1,0:T(8,128)S(1)}, u32[]{:S(2)}, u32[]{:S(2)}) collective-permute-start(f32[4,128,256]{2,1,0:T(8,128)} %log.3), channel_id=1, source_target_pairs={{0,80},{1,81},{2,82},{3,83},{4,84},{5,85},{6,86},{7,87},{8,88},{9,... | collective-permute-start | bytes 1572872 | tf_op jit(solution)/shard_map/ppermute | solution.py:37
  9.9 20.4 %collective-permute-start.16 = (f32[4,128,256]{2,1,0:T(8,128)}, f32[4,128,256]{2,1,0:T(8,128)}, u32[]{:S(2)}, u32[]{:S(2)}) collective-permute-start(f32[4,128,256]{2,1,0:T(8,128)} %param.19), channel_id=1, source_target_pairs={{0,64},{1,65},{2,66},{3,67},{4,68},{5,69},{6,70},{7,71},{8,72},{9,... | collective-permute-start | bytes 1572872 | tf_op jit(solution)/shard_map/ppermute | solution.py:37
  10.2 24.3 %collective-permute-start.15 = (f32[4,128,256]{2,1,0:T(8,128)}, f32[4,128,256]{2,1,0:T(8,128)}, u32[]{:S(2)}, u32[]{:S(2)}) collective-permute-start(f32[4,128,256]{2,1,0:T(8,128)} %param.19), channel_id=1, source_target_pairs={{0,80},{1,81},{2,82},{3,83},{4,84},{5,85},{6,86},{7,87},{8,88},{9,... | collective-permute-start | bytes 1572872 | tf_op jit(solution)/shard_map/ppermute | solution.py:37
  19.7 16.9 %collective-permute-start.11 = (f32[2,128,256]{2,1,0:T(8,128)}, f32[2,128,256]{2,1,0:T(8,128)}, u32[]{:S(2)}, u32[]{:S(2)}) collective-permute-start(f32[2,128,256]{2,1,0:T(8,128)} %slice.40), channel_id=1, source_target_pairs={{0,64},{1,65},{2,66},{3,67},{4,68},{5,69},{6,70},{7,71},{8,72},{9,... | collective-permute-start | bytes 786440 | tf_op jit(solution)/shard_map/ppermute | solution.py:37
  22.4 15.5 %collective-permute-start.12 = (f32[2,128,256]{2,1,0:T(8,128)}, f32[2,128,256]{2,1,0:T(8,128)}, u32[]{:S(2)}, u32[]{:S(2)}) collective-permute-start(f32[2,128,256]{2,1,0:T(8,128)} %slice.41), channel_id=1, source_target_pairs={{0,80},{1,81},{2,82},{3,83},{4,84},{5,85},{6,86},{7,87},{8,88},{9,... | collective-permute-start | bytes 786440 | tf_op jit(solution)/shard_map/ppermute | solution.py:37
  28.2 22.3 %collective-permute-start.20 = (f32[4,176,256]{2,1,0:T(8,128)}, f32[4,176,256]{2,1,0:T(8,128)S(1)}, u32[]{:S(2)}, u32[]{:S(2)}) collective-permute-start(f32[4,176,256]{2,1,0:T(8,128)} %get-tuple-element.134), channel_id=1, source_target_pairs={{0,1},{1,2},{2,3},{3,0},{4,5},{5,6},{6,7},{7,4},{8,9},{9,10},{10,1... | collective-permute-start | bytes 2162696 | tf_op jit(solution)/shard_map/ppermute | solution.py:37
  30.2 31.5 %collective-permute-start.21 = (f32[4,176,256]{2,1,0:T(8,128)}, f32[4,176,256]{2,1,0:T(8,128)S(1)}, u32[]{:S(2)}, u32[]{:S(2)}) collective-permute-start(f32[4,176,256]{2,1,0:T(8,128)} %get-tuple-element.135), channel_id=1, source_target_pairs={{0,2},{1,3},{2,0},{3,1},{4,6},{5,7},{6,4},{7,5},{8,10},{9,11},{10,... | collective-permute-start | bytes 2162696 | tf_op jit(solution)/shard_map/ppermute | solution.py:37
  34.5 29.2 %collective-permute-start.22 = (f32[4,176,256]{2,1,0:T(8,128)}, f32[4,176,256]{2,1,0:T(8,128)S(1)}, u32[]{:S(2)}, u32[]{:S(2)}) collective-permute-start(f32[4,176,256]{2,1,0:T(8,128)} %copy-done.5), channel_id=1, source_target_pairs={{0,3},{1,0},{2,1},{3,2},{4,7},{5,4},{6,5},{7,6},{8,11},{9,8},{10,9... | collective-permute-start | bytes 2162696 | tf_op jit(solution)/shard_map/ppermute | solution.py:37
  66.0 12.2 %collective-permute-start.25 = (f32[4,96,256]{2,1,0:T(8,128)}, f32[4,96,256]{2,1,0:T(8,128)}, u32[]{:S(2)}, u32[]{:S(2)}) collective-permute-start(f32[4,96,256]{2,1,0:T(8,128)} %get-tuple-element.151), channel_id=1, source_target_pairs={{0,1},{1,2},{2,3},{3,0},{4,5},{5,6},{6,7},{7,4},{8,9},{9,10},{10,1... | collective-permute-start | bytes 1179656 | tf_op jit(solution)/shard_map/ppermute | solution.py:37
  67.2 20.7 %collective-permute-start.26 = (f32[4,96,256]{2,1,0:T(8,128)}, f32[4,96,256]{2,1,0:T(8,128)}, u32[]{:S(2)}, u32[]{:S(2)}) collective-permute-start(f32[4,96,256]{2,1,0:T(8,128)} %get-tuple-element.152), channel_id=1, source_target_pairs={{0,2},{1,3},{2,0},{3,1},{4,6},{5,7},{6,4},{7,5},{8,10},{9,11},{10,... | collective-permute-start | bytes 1179656 | tf_op jit(solution)/shard_map/ppermute | solution.py:37
  70.1 17.8 %collective-permute-start.27 = (f32[4,96,256]{2,1,0:T(8,128)}, f32[4,96,256]{2,1,0:T(8,128)}, u32[]{:S(2)}, u32[]{:S(2)}) collective-permute-start(f32[4,96,256]{2,1,0:T(8,128)} %get-tuple-element.153), channel_id=1, source_target_pairs={{0,3},{1,0},{2,1},{3,2},{4,7},{5,4},{6,5},{7,6},{8,11},{9,8},{10,9... | collective-permute-start | bytes 1179656 | tf_op jit(solution)/shard_map/ppermute | solution.py:37
  72.3 25.6 %collective-permute-start.23 = (f32[4,2,144,128]{3,2,1,0:T(8,128)S(1)}, f32[4,2,144,128]{3,2,1,0:T(8,128)S(1)}, u32[]{:S(2)}, u32[]{:S(2)}) collective-permute-start(f32[4,2,144,128]{3,2,1,0:T(8,128)S(1)} %get-tuple-element.144), channel_id=1, source_target_pairs={{0,4},{1,5},{2,6},{3,7},{4,8},{5,9},{6,10},{7,11},{8,12},{9,13},{1... | collective-permute-start | bytes 1769480 | tf_op jit(solution)/shard_map/ppermute | solution.py:37
  76.1 21.7 %collective-permute-start.24 = (f32[4,2,144,128]{3,2,1,0:T(8,128)S(1)}, f32[4,2,144,128]{3,2,1,0:T(8,128)S(1)}, u32[]{:S(2)}, u32[]{:S(2)}) collective-permute-start(f32[4,2,144,128]{3,2,1,0:T(8,128)S(1)} %get-tuple-element.145), channel_id=1, source_target_pairs={{4,0},{5,1},{6,2},{7,3},{8,4},{9,5},{10,6},{11,7},{12,8},{13,9},{1... | collective-permute-start | bytes 1769480 | tf_op jit(solution)/shard_map/ppermute | solution.py:37
  89.3 12.9 %collective-permute-start.28 = (f32[4,2,112,128]{3,2,1,0:T(8,128)S(1)}, f32[4,2,112,128]{3,2,1,0:T(8,128)S(1)}, u32[]{:S(2)}, u32[]{:S(2)}) collective-permute-start(f32[4,2,112,128]{3,2,1,0:T(8,128)S(1)} %get-tuple-element.156), channel_id=1, source_target_pairs={{0,4},{1,5},{2,6},{3,7},{4,8},{5,9},{6,10},{7,11},{8,12},{9,13},{1... | collective-permute-start | bytes 1376264 | tf_op jit(solution)/shard_map/ppermute | solution.py:37
  93.2 13.4 %collective-permute-start.29 = (f32[4,2,112,128]{3,2,1,0:T(8,128)S(1)}, f32[4,2,112,128]{3,2,1,0:T(8,128)S(1)}, u32[]{:S(2)}, u32[]{:S(2)}) collective-permute-start(f32[4,2,112,128]{3,2,1,0:T(8,128)S(1)} %get-tuple-element.157), channel_id=1, source_target_pairs={{4,0},{5,1},{6,2},{7,3},{8,4},{9,5},{10,6},{11,7},{12,8},{13,9},{1... | collective-permute-start | bytes 1376264 | tf_op jit(solution)/shard_map/ppermute | solution.py:37
  114.9 9.6 %collective-permute-start.30 = (f32[8,2,32,128]{3,2,1,0:T(8,128)S(1)}, f32[8,2,32,128]{3,2,1,0:T(8,128)S(1)}, u32[]{:S(2)}, u32[]{:S(2)}) collective-permute-start(f32[8,2,32,128]{3,2,1,0:T(8,128)S(1)} %get-tuple-element.165), channel_id=1, source_target_pairs={{0,4},{1,5},{2,6},{3,7},{4,8},{5,9},{6,10},{7,11},{8,12},{9,13},{1... | collective-permute-start | bytes 786440 | tf_op jit(solution)/shard_map/ppermute | solution.py:37
  118.6 8.3 %collective-permute-start.31 = (f32[8,2,32,128]{3,2,1,0:T(8,128)S(1)}, f32[8,2,32,128]{3,2,1,0:T(8,128)S(1)}, u32[]{:S(2)}, u32[]{:S(2)}) collective-permute-start(f32[8,2,32,128]{3,2,1,0:T(8,128)S(1)} %get-tuple-element.166), channel_id=1, source_target_pairs={{4,0},{5,1},{6,2},{7,3},{8,4},{9,5},{10,6},{11,7},{12,8},{13,9},{1... | collective-permute-start | bytes 786440 | tf_op jit(solution)/shard_map/ppermute | solution.py:37
  119.9 12.1 %collective-permute-start.32 = (f32[16,2,8,128]{3,2,1,0:T(8,128)S(1)}, f32[16,2,8,128]{3,2,1,0:T(8,128)S(1)}, u32[]{:S(2)}, u32[]{:S(2)}) collective-permute-start(f32[16,2,8,128]{3,2,1,0:T(8,128)S(1)} %get-tuple-element.167), channel_id=1, source_target_pairs={{0,1},{1,2},{2,3},{4,5},{5,6},{6,7},{8,9},{9,10},{10,11},{12,13},{... | collective-permute-start | bytes 393224 | tf_op jit(solution)/shard_map/ppermute | solution.py:37
  123.2 8.7 %collective-permute-start.33 = (f32[16,2,8,128]{3,2,1,0:T(8,128)S(1)}, f32[16,2,8,128]{3,2,1,0:T(8,128)S(1)}, u32[]{:S(2)}, u32[]{:S(2)}) collective-permute-start(f32[16,2,8,128]{3,2,1,0:T(8,128)S(1)} %get-tuple-element.168), channel_id=1, source_target_pairs={{1,0},{2,1},{3,2},{5,4},{6,5},{7,6},{9,8},{10,9},{11,10},{13,12},{... | collective-permute-start | bytes 393224 | tf_op jit(solution)/shard_map/ppermute | solution.py:37
  144.3 11.2 %collective-permute-start.36 = (f32[8,2,32,128]{3,2,1,0:T(8,128)S(1)}, f32[8,2,32,128]{3,2,1,0:T(8,128)S(1)}, u32[]{:S(2)}, u32[]{:S(2)}) collective-permute-start(f32[8,2,32,128]{3,2,1,0:T(8,128)S(1)} %get-tuple-element.176), channel_id=1, source_target_pairs={{0,4},{1,5},{2,6},{3,7},{4,8},{5,9},{6,10},{7,11},{8,12},{9,13},{1... | collective-permute-start | bytes 786440 | tf_op jit(solution)/shard_map/ppermute | solution.py:37
  151.4 11.0 %collective-permute-start.38 = (f32[16,2,8,128]{3,2,1,0:T(8,128)S(1)}, f32[16,2,8,128]{3,2,1,0:T(8,128)S(1)}, u32[]{:S(2)}, u32[]{:S(2)}) collective-permute-start(f32[16,2,8,128]{3,2,1,0:T(8,128)S(1)} %get-tuple-element.178), channel_id=1, source_target_pairs={{0,1},{1,2},{2,3},{4,5},{5,6},{6,7},{8,9},{9,10},{10,11},{12,13},{... | collective-permute-start | bytes 393224 | tf_op jit(solution)/shard_map/ppermute | solution.py:37
  154.2 8.3 %collective-permute-start.39 = (f32[16,2,8,128]{3,2,1,0:T(8,128)S(1)}, f32[16,2,8,128]{3,2,1,0:T(8,128)S(1)}, u32[]{:S(2)}, u32[]{:S(2)}) collective-permute-start(f32[16,2,8,128]{3,2,1,0:T(8,128)S(1)} %get-tuple-element.179), channel_id=1, source_target_pairs={{1,0},{2,1},{3,2},{5,4},{6,5},{7,6},{9,8},{10,9},{11,10},{13,12},{... | collective-permute-start | bytes 393224 | tf_op jit(solution)/shard_map/ppermute | solution.py:37
  172.6 12.1 %collective-permute-start.42 = (f32[4,2,32,128]{3,2,1,0:T(8,128)S(1)}, f32[4,2,32,128]{3,2,1,0:T(8,128)S(1)}, u32[]{:S(2)}, u32[]{:S(2)}) collective-permute-start(f32[4,2,32,128]{3,2,1,0:T(8,128)S(1)} %get-tuple-element.185), channel_id=1, source_target_pairs={{0,4},{1,5},{2,6},{3,7},{4,8},{5,9},{6,10},{7,11},{8,12},{9,13},{1... | collective-permute-start | bytes 393224 | tf_op jit(solution)/shard_map/ppermute | solution.py:37
  193.6 11.5 %collective-permute-start.46 = (f32[4,32,256]{2,1,0:T(8,128)S(1)}, f32[4,32,256]{2,1,0:T(8,128)S(1)}, u32[]{:S(2)}, u32[]{:S(2)}) collective-permute-start(f32[4,32,256]{2,1,0:T(8,128)S(1)} %get-tuple-element.194), channel_id=1, source_target_pairs={{0,1},{1,2},{2,3},{3,0},{4,5},{5,6},{6,7},{7,4},{8,9},{9,10},{10,1... | collective-permute-start | bytes 393224 | tf_op jit(solution)/shard_map/ppermute | solution.py:37
  194.6 10.5 %collective-permute-start.47 = (f32[4,32,256]{2,1,0:T(8,128)S(1)}, f32[4,32,256]{2,1,0:T(8,128)S(1)}, u32[]{:S(2)}, u32[]{:S(2)}) collective-permute-start(f32[4,32,256]{2,1,0:T(8,128)S(1)} %get-tuple-element.195), channel_id=1, source_target_pairs={{0,2},{1,3},{2,0},{3,1},{4,6},{5,7},{6,4},{7,5},{8,10},{9,11},{10,... | collective-permute-start | bytes 393224 | tf_op jit(solution)/shard_map/ppermute | solution.py:37
  194.6 10.5 %collective-permute-start.48 = (f32[4,32,256]{2,1,0:T(8,128)S(1)}, f32[4,32,256]{2,1,0:T(8,128)S(1)}, u32[]{:S(2)}, u32[]{:S(2)}) collective-permute-start(f32[4,32,256]{2,1,0:T(8,128)S(1)} %get-tuple-element.196), channel_id=1, source_target_pairs={{0,3},{1,0},{2,1},{3,2},{4,7},{5,4},{6,5},{7,6},{8,11},{9,8},{10,9... | collective-permute-start | bytes 393224 | tf_op jit(solution)/shard_map/ppermute | solution.py:37
  205.1 10.6 %collective-permute-start.50 = (f32[4,64,256]{2,1,0:T(8,128)S(1)}, f32[4,64,256]{2,1,0:T(8,128)S(1)}, u32[]{:S(2)}, u32[]{:S(2)}) collective-permute-start(f32[4,64,256]{2,1,0:T(8,128)S(1)} %get-tuple-element.207), channel_id=1, source_target_pairs={{0,2},{1,3},{2,0},{3,1},{4,6},{5,7},{6,4},{7,5},{8,10},{9,11},{10,... | collective-permute-start | bytes 786440 | tf_op jit(solution)/shard_map/ppermute | solution.py:37
  218.5 35.0 %collective-permute-start.55 = (f32[2,128,256]{2,1,0:T(8,128)S(1)}, f32[2,128,256]{2,1,0:T(8,128)S(1)}, u32[]{:S(2)}, u32[]{:S(2)}) collective-permute-start(f32[2,128,256]{2,1,0:T(8,128)S(1)} %get-tuple-element.222), channel_id=1, source_target_pairs={{0,80},{1,81},{2,82},{3,83},{4,84},{5,85},{6,86},{7,87},{8,88},{9,... | collective-permute-start | bytes 786440 | tf_op jit(solution)/shard_map/ppermute | solution.py:37
  247.6 10.5 %collective-permute-start.53 = (f32[2,128,256]{2,1,0:T(8,128)S(1)}, f32[2,128,256]{2,1,0:T(8,128)S(1)}, u32[]{:S(2)}, u32[]{:S(2)}) collective-permute-start(f32[2,128,256]{2,1,0:T(8,128)S(1)} %get-tuple-element.221), channel_id=1, source_target_pairs={{0,64},{1,65},{2,66},{3,67},{4,68},{5,69},{6,70},{7,71},{8,72},{9,... | collective-permute-start | bytes 786440 | tf_op jit(solution)/shard_map/ppermute | solution.py:37
  254.4 14.7 %collective-permute-start.56 = (f32[4,128,256]{2,1,0:T(8,128)}, f32[4,128,256]{2,1,0:T(8,128)S(1)}, u32[]{:S(2)}, u32[]{:S(2)}) collective-permute-start(f32[4,128,256]{2,1,0:T(8,128)} %pad_maximum_fusion.1), channel_id=1, source_target_pairs={{0,80},{1,81},{2,82},{3,83},{4,84},{5,85},{6,86},{7,87},{8,88},{9,... | collective-permute-start | bytes 1572872 | tf_op jit(solution)/shard_map/ppermute | solution.py:37
  259.0 14.3 %collective-permute-start.54 = (f32[4,128,256]{2,1,0:T(8,128)}, f32[4,128,256]{2,1,0:T(8,128)S(1)}, u32[]{:S(2)}, u32[]{:S(2)}) collective-permute-start(f32[4,128,256]{2,1,0:T(8,128)} %pad_maximum_fusion), channel_id=1, source_target_pairs={{0,64},{1,65},{2,66},{3,67},{4,68},{5,69},{6,70},{7,71},{8,72},{9,... | collective-permute-start | bytes 1572872 | tf_op jit(solution)/shard_map/ppermute | solution.py:37
  (31 other events, 225.8 us)
where the time goes:
time: 276 us; the launch traced here: 274 us
  starting transfers between devices  116 us (42%)
  waiting for transfers between devices  97.9 us (35%)
  Pallas kernels  32.5 us (12%)
  local copies, waits for them, and re-layouts  10.4 us (4%)
  other arithmetic  7.89 us (3%)
  between operations  5.74 us (2%)
  matrix products  3.18 us (1%)
    ppermute x48, starting transfers between devices, send(): return lax.ppermute(value, ('shot', 'sub'), pairs_by(move))  116 us
    ppermute x48, waiting for transfers between devices, send(): return lax.ppermute(value, ('shot', 'sub'), pairs_by(move))  97.9 us
    pallas_call x14, Pallas kernels, call(): pl.pallas_call(body, out_shape=tuple(outs), in_specs=specs, out_specs=tup...  32.5 us
  transfers between devices with their start and end apart: 48, of which 28 were waited for; matrix products, arithmetic and copies ran while one was open for 6% of the time, Pallas kernels for 2%

commit v1 on v0

--- a/solution.py
+++ b/solution.py
@@ -49,8 +49,30 @@
     return send(value, lambda x, c, z, y: (x, c, (z + steps) % 4, y))
 
 
-def send_y(value, steps):
-    return send(value, lambda x, c, z, y: (x, c, z, (y + steps) % 4))
+def send_column(value, turn):
+    def move(x, c, z, y):
+        column = (y + turn) % 4
+        return (x, column % 2, z, 2 * (column // 2) + c)
+
+    return send(value, move)
+
+
+def send_slab(value, turn):
+    def move(x, c, z, y):
+        return (x, y % 2, z, (2 * (y // 2) + c + turn) % 4)
+
+    return send(value, move)
+
+
+def send_outer(value):
+    def move(x, c, z, y):
+        if c == 1 and y < 2:
+            return (x, 0, z, y + 2)
+        if c == 0 and y >= 2:
+            return (x, 1, z, y - 2)
+        return None
+
+    return send(value, move)
 
 
 def next_rows(x, z, steps):
@@ -66,10 +88,6 @@
         return None if place is None else (place[0], c, place[1], y)
 
     return send(value, move)
-
-
-def send_cells(value, steps):
-    return send(value, lambda x, c, z, y: (x, c, z, y + steps) if 0 <= y + steps < 4 else None)
 
 
 def shape(*sizes):
@@ -254,43 +272,41 @@
     return near
 
 
-def fill_wide(wide, block, halo):
-    below, above, left, right, left_corners, right_corners = halo
+def cells_at(start):
+    return pl.ds(pl.multiple_of(start, 8), 8)
+
+
+def fill_wide(sides, wide, block, halo):
+    below, above, inner, outer = halo
     wide[0:8, :, 8 : 8 + CELLS, :] = below[...]
     wide[8 : 8 + ROWS, :, 8 : 8 + CELLS, :] = block[...]
     wide[8 + ROWS : 16 + ROWS, :, 8 : 8 + CELLS, :] = above[...]
-    for cells, side, corners in (
-        (slice(0, 8), left, left_corners),
-        (slice(8 + CELLS, SPAN), right, right_corners),
-    ):
-        wide[4:8, :, cells, :] = corners[0:4]
-        wide[8 : 8 + ROWS, :, cells, :] = side[...]
-        wide[8 + ROWS : 12 + ROWS, :, cells, :] = corners[4:8]
-
-
-WIDE_EDGES = [region(8, CELLS)] * 2 + [region(ROWS, 8)] * 2
+    wide[4 : 12 + ROWS, :, cells_at(sides[2]), :] = inner[...]
+    wide[4 : 12 + ROWS, :, cells_at(sides[3]), :] = outer[...]
+
+
+WIDE_EDGES = [region(8, CELLS)] * 2
 
 
 def write_wide_edges(block, edges):
-    low, high, low_cells, high_cells = edges
+    low, high = edges
     low[...] = block[0:8]
     high[...] = block[ROWS - 8 : ROWS]
-    low_cells[...] = block[:, :, 0:8, :]
-    high_cells[...] = block[:, :, CELLS - 8 : CELLS, :]
-
-
-def rim_body(below, above, low, high):
-    for out, cut in ((low, slice(0, 8)), (high, slice(CELLS - 8, CELLS))):
+
+
+def rim_body(sides, block, below, above, inner, outer):
+    for out, side in ((inner, 0), (outer, 1)):
+        cut = cells_at(sides[side])
         out[0:4] = below[4:8, :, cut, :]
-        out[4:8] = above[0:4, :, cut, :]
-
-
-def swap_wide_edges(edges):
-    low, high, low_cells, high_cells = edges
+        out[4 : 4 + ROWS] = block[:, :, cut, :]
+        out[4 + ROWS : 8 + ROWS] = above[0:4, :, cut, :]
+
+
+def swap_wide_edges(sides, block, edges):
+    low, high = edges
     below, above = send_group(high, 1), send_group(low, -1)
-    left, right = send_cells(high_cells, 1), send_cells(low_cells, -1)
-    low_corners, high_corners = call(rim_body, [region(8, 8)] * 2, 0, (below, above))
-    return below, above, left, right, send_cells(high_corners, 1), send_cells(low_corners, -1)
+    inner, outer = call(rim_body, [region(ROWS + 8, 8)] * 2, 1, (sides, block, below, above))
+    return below, above, send_core(inner), send_outer(outer)
 
 
 def cut_body(chunks, *refs, margins):
@@ -421,13 +437,13 @@
             pieces[turn][:, at : at + CELLS, 128 * half : 128 * half + 128] = block[pl.ds(slot, 4), half]
 
 
-def turn_body(place, amount, block, *refs):
-    halo, refs = refs[:6], refs[6:]
+def turn_body(place, amount, sides, block, *refs):
+    halo, refs = refs[:4], refs[4:]
     old, speed_sq, s0, s1, s2, adjoint, later, maps, near, new, adjoint_new, summed = refs[:12]
-    edges, wide = refs[12:16], refs[16]
+    edges, wide = refs[12:14], refs[14]
     model = (speed_sq, s0, s1, s2)
     lane = lanes()
-    fill_wide(wide, block, halo)
+    fill_wide(sides, wide, block, halo)
     near_step(wide, old, model, lane, near)
     add_source(place, amount[2], 0, near)
 
@@ -450,13 +466,13 @@
     write_wide_edges(adjoint_new, edges)
 
 
-def adjoint_body(block, *refs):
-    halo, refs = refs[:6], refs[6:]
+def adjoint_body(sides, block, *refs):
+    halo, refs = refs[:4], refs[4:]
     old, speed_sq, s0, s1, s2, maps, u3, u2, u1, u0, sums = refs[:11]
-    near, new, summed, low, high, low_cells, high_cells, wide = refs[11:]
+    near, new, summed, low, high, inner, outer, wide = refs[11:]
     model = (speed_sq, s0, s1, s2)
     lane = lanes()
-    fill_wide(wide, block, halo)
+    fill_wide(sides, wide, block, halo)
     near_step(wide, old, model, lane, near, injected(maps, 3, u3))
 
     def finish(row, half, cut, value):
@@ -474,19 +490,19 @@
     block_step(near, of_block(block), model, lane, finish)
     low[...] = new[0:4]
     high[...] = new[ROWS - 4 : ROWS]
-    low_cells[...] = new[:, :, 0:8, :]
-    high_cells[...] = new[:, :, CELLS - 8 : CELLS, :]
+    inner[...] = new[:, :, cells_at(sides[0]), :]
+    outer[...] = new[:, :, cells_at(sides[1]), :]
 
 
 def last_body(
-    slots, model_slots, block, below, above, left, right, old, speed_sq, s0, s1, s2, maps,
+    slots, model_slots, sides, block, below, above, inner, outer, old, speed_sq, s0, s1, s2, maps,
     u1, u0, u_before, sums, twice, u4, p0, p1, p2, p3, q0, q1, q2, q3, near, new, image,
 ):
     near[0:4, :, 8 : 8 + CELLS, :] = below[...]
     near[4 : 4 + ROWS, :, 8 : 8 + CELLS, :] = block[...]
     near[4 + ROWS : 8 + ROWS, :, 8 : 8 + CELLS, :] = above[...]
-    near[4 : 4 + ROWS, :, 0:8, :] = left[...]
-    near[4 : 4 + ROWS, :, 8 + CELLS : SPAN, :] = right[...]
+    near[4 : 4 + ROWS, :, cells_at(sides[2]), :] = inner[...]
+    near[4 : 4 + ROWS, :, cells_at(sides[3]), :] = outer[...]
     lane = lanes()
 
     def finish(row, half, cut, value):
@@ -510,8 +526,8 @@
             out[:, pl.ds(first, CELLS), :] = piece[:, CELLS * index : CELLS * index + CELLS, :]
 
 
-def sent_pieces(pieces):
-    return [pieces[0]] + [send_y(pieces[turn], turn) for turn in (1, 2, 3)]
+def sent(pieces, move):
+    return [move(piece, turn) for turn, piece in enumerate(pieces)]
 
 
 def to_slabs(pieces, chunks, count):
@@ -540,7 +556,12 @@
     y = sub % 4
     group = sub // 4
     start = aperture_start[0]
-    partner = send_core(aperture_start)
+    column = 2 * (y // 2) + core
+    own_small = (
+        jnp.concatenate([aperture_start, source_cell, receiver_cells[0]]),
+        jnp.concatenate([wavelet[0], observed.reshape(-1)]),
+    )
+    partner_small = tuple(send_core(value) for value in own_small)
 
     def wanted(first_slab):
         upper = first_slab // 4 + (y < first_slab % 4).astype(jnp.int32)
@@ -552,16 +573,29 @@
     turns = jnp.arange(4, dtype=jnp.int32)
     chunks_out = (y + turns) % 4
     chunks_in = (y - turns) % 4
-    slots_in = (y - turns - start % 4) % 4
-    slots_out = (y + turns - start % 4) % 4
 
     pieces = cut_pieces(
         [forward_now[0], forward_old[0], adjoint_now[0], adjoint_later[0]],
         (True, True, True, False),
         chunks_out,
     )
-    velocity, partner, *pieces = lax.optimization_barrier((velocity, partner, *pieces))
-    pair_core, pair_step, _ = wanted(partner[0])
+    velocity, partner_small, *pieces = lax.optimization_barrier((velocity, partner_small, *pieces))
+    pair_core, pair_step, _ = wanted(partner_small[0][0])
+    whole, amounts = (
+        jnp.where(y % 2 == core, own, partner) for own, partner in zip(own_small, partner_small)
+    )
+    skip = whole[0] % 4
+    source, receivers = whole[1], whole[2:]
+    amount, seen = amounts[:4], amounts[4:].reshape(4, -1)
+    slots_plain = (column - turns) % 4
+    slots_in = (column - turns - skip) % 4
+    slots_back = (column + turns) % 4
+    slots_out = (column + turns - skip) % 4
+    sides = jnp.where(
+        core == 0,
+        jnp.array([CELLS - 8, 0, 8 + CELLS, 0], jnp.int32),
+        jnp.array([0, CELLS - 8, 0, 8 + CELLS], jnp.int32),
+    )
 
     def gathered(slab):
         from_below = send_x(slab, 1)
@@ -584,38 +618,37 @@
 
     log_slab = gathered(jnp.log(density))
     speed_slab = gathered(velocity)
-    pieces = sent_pieces(pieces)
+    pieces = sent(pieces, send_column)
 
     def local_place(cells, rows_more, cells_more):
         rows = cells // (NY * NZ) - group * ROWS + rows_more
-        columns = (cells // NZ) % NY - y * CELLS + cells_more
+        columns = (cells // NZ) % NY - column * CELLS + cells_more
         inside = (rows >= 0) & (rows < ROWS + 2 * rows_more)
         inside = inside & (columns >= 0) & (columns < CELLS + 2 * cells_more)
         return inside, rows, (cells // 128) % 2, columns, cells % 128
 
-    inside, rows, half, columns, lane = local_place(receiver_cells[0], 4, 8)
+    inside, rows, half, columns, lane = local_place(receivers, 4, 8)
     line = jnp.where(inside, (rows * 2 + half) * SPAN + columns, -1)
     lines = (ROWS + 8) * 2 * SPAN
     on_line = (jnp.arange(lines, dtype=jnp.int32)[:, None] == line[None, :]).astype(F32)
-    weights = jnp.concatenate([jnp.ones_like(observed[0, :1]), observed[0]])
+    weights = jnp.concatenate([jnp.ones_like(seen[:1]), seen])
     hit = lane[:, None, None] == jnp.arange(128, dtype=jnp.int32)[None, None, :]
     at_lane = jnp.where(hit, weights.T[:, :, None], 0.0).reshape(-1, 5 * 128)
     maps = jnp.dot(on_line, at_lane, precision=lax.Precision.HIGHEST)
     maps = maps.reshape(ROWS + 8, 2, SPAN, 5 * 128)
 
     def source_place(rows_more, cells_more):
-        inside, rows, half, columns, lane = local_place(source_cell[0], rows_more, cells_more)
+        inside, rows, half, columns, lane = local_place(source, rows_more, cells_more)
         rows = jnp.clip(rows, 0, ROWS + 2 * rows_more - 1)
         return [inside.astype(jnp.int32), rows, half, columns, lane]
 
     place = jnp.stack(source_place(4, 8) + source_place(0, 0))
-    amount = wavelet[0]
-
-    log_slab, speed_slab = lax.optimization_barrier((log_slab, speed_slab))
+
+    log_slab, speed_slab, *pieces[:2] = lax.optimization_barrier((log_slab, speed_slab, *pieces[:2]))
     log_slab, speed_slab = turned((log_slab, speed_slab), (4 - turn_by) % 4)
     log_slab, speed_slab, *pieces = lax.optimization_barrier((log_slab, speed_slab, *pieces))
-    model_pieces = sent_pieces(cut_pieces([log_slab, speed_slab], (True, True), chunks_out))
-    now, old, adjoint, a_later, side_low, side_high = gather_blocks(pieces, chunks_in, (8, 4, 4, 0))
+    model_pieces = sent(cut_pieces([log_slab, speed_slab], (True, True), chunks_out), send_column)
+    now, old, adjoint, a_later, side_low, side_high = gather_blocks(pieces, slots_plain, (8, 4, 4, 0))
     below, above = send_group(side_high, 1), send_group(side_low, -1)
     u_wide, old_near, a_near = call(
         fields_body, [WIDE, NEAR, NEAR], 0, (now, old, adjoint, below, above)
@@ -630,43 +663,43 @@
     u1, u2, *edges = call(
         forward_body, [NEAR, BLOCK] + WIDE_EDGES, 2, (place, amount, u_wide, old_near, *model)
     )
-    halo = swap_wide_edges(edges)
+    halo = swap_wide_edges(sides, u2, edges)
     u3, u4, a3, sums, *edges = call(
         turn_body,
         [NEAR, BLOCK, BLOCK, BLOCK] + WIDE_EDGES,
-        2,
-        (place, amount, u2, *halo, u1, *model, a_near, a_later, maps),
+        3,
+        (place, amount, sides, u2, *halo, u1, *model, a_near, a_later, maps),
         (WIDE,),
     )
-    halo = swap_wide_edges(edges)
-    a2, a1, sums, side_low, side_high, low_cells, high_cells = call(
+    halo = swap_wide_edges(sides, a3, edges)
+    a2, a1, sums, side_low, side_high, inner, outer = call(
         adjoint_body,
         [NEAR, BLOCK, BLOCK] + [region(4, CELLS)] * 2 + [region(ROWS, 8)] * 2,
-        0,
-        (a3, *halo, a_near, *model, maps, u3, u2, u1, u_wide, sums),
+        1,
+        (sides, a3, *halo, a_near, *model, maps, u3, u2, u1, u_wide, sums),
         (WIDE,),
     )
     halo = (
         send_group(side_high, 1),
         send_group(side_low, -1),
-        send_cells(high_cells, 1),
-        send_cells(low_cells, -1),
+        send_core(inner),
+        send_outer(outer),
     )
     pieces = call(
         last_body,
         [shape(4, CELLS, NZ)] * 4 + [shape(4, 2 * CELLS, NZ)] * 4,
-        2,
-        (chunks_out, slots_out, a1, *halo, a2, *model, maps, u1, u_wide, old_near, sums, twice, u4),
+        3,
+        (slots_back, slots_out, sides, a1, *halo, a2, *model, maps, u1, u_wide, old_near, sums, twice, u4),
         (NEAR, BLOCK, BLOCK),
     )
-    pieces = lax.optimization_barrier((*sent_pieces(pieces[:4]), *pieces[4:]))
+    pieces = lax.optimization_barrier((*sent(pieces[:4], send_slab), *pieces[4:]))
     (image,) = to_slabs(pieces[:4], chunks_in, 1)
 
     def both(first_half, second_half):
         return jnp.concatenate([first_half, second_half])
 
     (image,) = turned((image,), turn_by)
-    image, *pieces = lax.optimization_barrier((image, *sent_pieces(pieces[4:])))
+    image, *pieces = lax.optimization_barrier((image, *sent(pieces[4:], send_slab)))
     adjoint_first, forward_last = to_slabs(pieces, chunks_in, 2)
     other = send_core(image)
 

time: 276 us -> 303 us (1.098); the launches traced: 274 us -> 309 us
  waiting for transfers between devices: 97.9 us -> 72.7 us
  local copies, waits for them, and re-layouts: 10.4 us -> 32.8 us
  starting transfers between devices: 116 us -> 136 us
  Pallas kernels: 32.5 us -> 39.5 us
  other arithmetic: 7.89 us -> 12.9 us
  between operations: 5.74 us -> 9.28 us
    ppermute x48 -> x49, waiting for transfers between devices: 97.9 us -> 72.7 us  [send(): return lax.ppermute(value, ('shot', 'sub'), pairs_by(move))]
    unnamed x32 -> x105, local copies, waits for them, and re-layouts: 3.9 us -> 26.1 us
    ppermute x48 -> x49, starting transfers between devices: 116 us -> 136 us  [send(): return lax.ppermute(value, ('shot', 'sub'), pairs_by(move))]
    pallas_call x14, Pallas kernels: 32.5 us -> 39.5 us  [call(): pl.pallas_call(body, out_shape=tuple(outs), in_specs=specs, out_specs=tup...]
  transfers between devices with their start and end apart: 48 -> 49, of which waited for: 28 -> 21; matrix products, arithmetic and copies ran while one was open for 6% -> 7% of each run, Pallas kernels for 2% -> 3%
where the time goes in v1:
time: 303 us; the launch traced here: 309 us
  starting transfers between devices  136 us (45%)
  waiting for transfers between devices  72.7 us (24%)
  Pallas kernels  39.5 us (13%)
  local copies, waits for them, and re-layouts  32.8 us (11%)
  other arithmetic  12.9 us (4%)
  between operations  9.28 us (3%)
  matrix products  5.97 us (2%)
    ppermute x49, starting transfers between devices, send(): return lax.ppermute(value, ('shot', 'sub'), pairs_by(move))  136 us
    ppermute x49, waiting for transfers between devices, send(): return lax.ppermute(value, ('shot', 'sub'), pairs_by(move))  72.7 us
    pallas_call x14, Pallas kernels, call(): pl.pallas_call(body, out_shape=tuple(outs), in_specs=specs, out_specs=tup...  39.5 us
    unnamed x105, local copies, waits for them, and re-layouts  26.1 us
  transfers between devices with their start and end apart: 49, of which 21 were waited for; matrix products, arithmetic and copies ran while one was open for 7% of the time, Pallas kernels for 3%

profile of v1, /device:TPU:0, one launch (start us, length us, event | category | flops | bytes accessed | tf_op | source)
XLA Modules:
  0.0 309.2 jit_solution(16915844435946573001)
XLA Ops:
  15.6 2.9 collective-permute-start.16
  28.3 3.3 %collective-permute-start.14 = (f32[2,128,256]{2,1,0:T(8,128)S(1)}, f32[2,128,256]{2,1,0:T(8,128)S(1)}, u32[]{:S(2)}, u32[]{:S(2)}) collective-permute-start(f32[2,128,256]{2,1,0:T(8,128)S(1)} %slice.66), channel_id=1, source_target_pairs={{0,80},{1,81},{2,82},{3,83},{4,84},{5,85},{6,86},{7,87},{8,88},{9,... | collective-permute-start | bytes 786440 | tf_op jit(solution)/shard_map/ppermute | solution.py:37
  33.5 3.0 collective-permute-start.23
  37.3 3.7 %collective-permute-start.19 = (f32[2,128,256]{2,1,0:T(8,128)S(1)}, f32[2,128,256]{2,1,0:T(8,128)S(1)}, u32[]{:S(2)}, u32[]{:S(2)}) collective-permute-start(f32[2,128,256]{2,1,0:T(8,128)S(1)} %slice.68), channel_id=1, source_target_pairs={{0,80},{1,81},{2,82},{3,83},{4,84},{5,85},{6,86},{7,87},{8,88},{9,... | collective-permute-start | bytes 786440 | tf_op jit(solution)/shard_map/ppermute | solution.py:37
  42.4 3.0 collective-permute-done.18
  55.6 6.2 %collective-permute-done.24.refs_3_ = f32[4,176,256]{2,1,0:T(8,128)S(1)} collective-permute-done((f32[4,176,256]{2,1,0:T(8,128)S(1)}, f32[4,176,256]{2,1,0:T(8,128)S(1)}, u32[]{:S(2)}, u32[]{:S(2)}) %collective-permute-start.24) | collective-permute-done | bytes 720928 | tf_op jit(solution)/shard_map/ppermute | solution.py:37
  66.7 6.1 %collective-permute-start.28 = (f32[4,96,256]{2,1,0:T(8,128)}, f32[4,96,256]{2,1,0:T(8,128)}, u32[]{:S(2)}, u32[]{:S(2)}) collective-permute-start(f32[4,96,256]{2,1,0:T(8,128)} %get-tuple-element.157), channel_id=1, source_target_pairs={{0,32},{1,2},{2,34},{3,0},{4,36},{5,6},{6,38},{7,4},{8,40},{9,10},... | collective-permute-start | bytes 1179656 | tf_op jit(solution)/shard_map/ppermute | solution.py:37
  82.6 3.8 %collective-permute-start.25 = (f32[4,2,144,128]{3,2,1,0:T(8,128)}, f32[4,2,144,128]{3,2,1,0:T(8,128)S(1)}, u32[]{:S(2)}, u32[]{:S(2)}) collective-permute-start(f32[4,2,144,128]{3,2,1,0:T(8,128)} %get-tuple-element.150), channel_id=1, source_target_pairs={{0,4},{1,5},{2,6},{3,7},{4,8},{5,9},{6,10},{7,11},{8,12},{9,13},{1... | collective-permute-start | bytes 1769480 | tf_op jit(solution)/shard_map/ppermute | solution.py:37
  88.5 3.6 %collective-permute-done.30.refs_3_ = f32[4,96,256]{2,1,0:T(8,128)} collective-permute-done((f32[4,96,256]{2,1,0:T(8,128)}, f32[4,96,256]{2,1,0:T(8,128)}, u32[]{:S(2)}, u32[]{:S(2)}) %collective-permute-start.30) | collective-permute-done | bytes 393248 | tf_op jit(solution)/shard_map/ppermute | solution.py:37
  97.2 4.7 %collective-permute-start.31 = (f32[4,2,112,128]{3,2,1,0:T(8,128)}, f32[4,2,112,128]{3,2,1,0:T(8,128)}, u32[]{:S(2)}, u32[]{:S(2)}) collective-permute-start(f32[4,2,112,128]{3,2,1,0:T(8,128)} %get-tuple-element.162), channel_id=1, source_target_pairs={{0,4},{1,5},{2,6},{3,7},{4,8},{5,9},{6,10},{7,11},{8,12},{9,13},{1... | collective-permute-start | bytes 1376264 | tf_op jit(solution)/shard_map/ppermute | solution.py:37
  107.5 6.0 %fusion.refs_11_.refs_9_.maps = f32[24,2,48,640]{3,2,1,0:T(8,128)} fusion(f32[256,640,1,1]{0,1,3,2:T(8,128)} %bitcast.38, s32[256]{0:T(256)S(1)} %get-tuple-element.227, s32[24,2,48]{2,1,0:T(2,128)} %multiply_add_fusion), kind=kOutput, calls=%fused_computation | convolution fusion | flops 4530438144 | bytes 6563840 | tf_op jit(solution)/shard_map/dot_general | solution.py:637
  117.6 4.1 %shard_map.153 = (f32[24,2,48,128]{3,2,1,0:T(8,128)S(1)}, f32[24,2,48,128]{3,2,1,0:T(8,128)S(1)}, f32[24,2,48,128]{3,2,1,0:T(8,128)S(1)}, f32[24,2,48,128]{3,2,1,0:T(8,128)S(1)}, f32[16,2,32,128]{3,2,1,0:T(8,128)S(1)}) custom-call(f32[16,2,48,128]{3,2,1,0:T(8,128)S(1)} %copy-done.18, f32[16,2,48,128]{3,2,1,0:T(8,128)S(1)} %copy-done.20, ...), custom_call_target="tpu_custom_call" | custom-call | tf_op jit(solution)/shard_map/pallas_call | solution.py:109
  122.5 6.2 %shard_map.154 = (f32[24,2,48,128]{3,2,1,0:T(8,128)S(1)}, f32[16,2,32,128]{3,2,1,0:T(8,128)S(1)}, f32[8,2,32,128]{3,2,1,0:T(8,128)}, f32[8,2,32,128]{3,2,1,0:T(8,128)}) custom-call(s32[10]{0:T(128)S(1)} %stack.45.place, f32[4]{0:T(128)S(1)} %slice.64.amount, f32[32,2,48,128]{3,2,1,0:T(8,128)S(1)} %get-tuple-element.152.wide.refs_13_.u0, ...), custom_call_target="tpu_custom_call" | custom-call | tf_op jit(solution)/shard_map/pallas_call | solution.py:109
  130.8 3.7 %collective-permute-start.33 = (f32[8,2,32,128]{3,2,1,0:T(8,128)}, f32[8,2,32,128]{3,2,1,0:T(8,128)}, u32[]{:S(2)}, u32[]{:S(2)}) collective-permute-start(f32[8,2,32,128]{3,2,1,0:T(8,128)} %get-tuple-element.171), channel_id=1, source_target_pairs={{0,4},{1,5},{2,6},{3,7},{4,8},{5,9},{6,10},{7,11},{8,12},{9,13},{1... | collective-permute-start | bytes 786440 | tf_op jit(solution)/shard_map/ppermute | solution.py:37
  135.9 4.1 %collective-permute-done.33.below.refs_0_ = f32[8,2,32,128]{3,2,1,0:T(8,128)} collective-permute-done((f32[8,2,32,128]{3,2,1,0:T(8,128)}, f32[8,2,32,128]{3,2,1,0:T(8,128)}, u32[]{:S(2)}, u32[]{:S(2)}) %collective-permute-start.33) | collective-permute-done | bytes 262176 | tf_op jit(solution)/shard_map/ppermute | solution.py:37
  140.0 4.8 %collective-permute-done.34.above.refs_1_ = f32[8,2,32,128]{3,2,1,0:T(8,128)} collective-permute-done((f32[8,2,32,128]{3,2,1,0:T(8,128)}, f32[8,2,32,128]{3,2,1,0:T(8,128)}, u32[]{:S(2)}, u32[]{:S(2)}) %collective-permute-start.34) | collective-permute-done | bytes 262176 | tf_op jit(solution)/shard_map/ppermute | solution.py:37
  156.5 7.8 %shard_map.156 = (f32[24,2,48,128]{3,2,1,0:T(8,128)S(1)}, f32[16,2,32,128]{3,2,1,0:T(8,128)S(1)}, f32[16,2,32,128]{3,2,1,0:T(8,128)S(1)}, f32[16,2,32,128]{3,2,1...) custom-call(s32[10]{0:T(128)S(1)} %stack.45.place, f32[4]{0:T(128)S(1)} %slice.64.amount, ...), custom_call_target="tpu_custom_call" | custom-call | tf_op jit(solution)/shard_map/pallas_call | solution.py:109
  164.3 5.3 %collective-permute-start.37 = (f32[8,2,32,128]{3,2,1,0:T(8,128)S(1)}, f32[8,2,32,128]{3,2,1,0:T(8,128)S(1)}, u32[]{:S(2)}, u32[]{:S(2)}) collective-permute-start(f32[8,2,32,128]{3,2,1,0:T(8,128)S(1)} %get-tuple-element.180), channel_id=1, source_target_pairs={{0,4},{1,5},{2,6},{3,7},{4,8},{5,9},{6,10},{7,11},{8,12},{9,13},{1... | collective-permute-start | bytes 786440 | tf_op jit(solution)/shard_map/ppermute | solution.py:37
  173.5 4.4 %collective-permute-done.38.above.refs_1_ = f32[8,2,32,128]{3,2,1,0:T(8,128)S(1)} collective-permute-done((f32[8,2,32,128]{3,2,1,0:T(8,128)S(1)}, f32[8,2,32,128]{3,2,1,0:T(8,128)S(1)}, u32[]{:S(2)}, u32[]{:S(2)}) %collective-permute-start.38) | collective-permute-done | bytes 262176 | tf_op jit(solution)/shard_map/ppermute | solution.py:37
  178.5 6.2 %collective-permute-start.39 = (f32[24,2,8,128]{3,2,1,0:T(8,128)S(1)}, f32[24,2,8,128]{3,2,1,0:T(8,128)S(1)}, u32[]{:S(2)}, u32[]{:S(2)}) collective-permute-start(f32[24,2,8,128]{3,2,1,0:T(8,128)S(1)} %get-tuple-element.182), channel_id=1, source_target_pairs={{0,32},{1,33},{2,34},{3,35},{4,36},{5,37},{6,38},{7,39},{8,40},{9,... | collective-permute-start | bytes 589832 | tf_op jit(solution)/shard_map/ppermute | solution.py:37
  185.8 5.6 %shard_map.158 = (f32[24,2,48,128]{3,2,1,0:T(8,128)S(1)}, f32[16,2,32,128]{3,2,1,0:T(8,128)S(1)}, f32[16,2,32,128]{3,2,1,0:T(8,128)S(1)}, f32[4,2,32,128]{3,2,1,...) custom-call(s32[4]{0:T(128)S(1)} %broadcast_select_fusion.2.sides, ...), custom_call_target="tpu_custom_call" | custom-call | tf_op jit(solution)/shard_map/pallas_call | solution.py:109
  191.5 6.7 %collective-permute-start.41 = (f32[4,2,32,128]{3,2,1,0:T(8,128)S(1)}, f32[4,2,32,128]{3,2,1,0:T(8,128)S(1)}, u32[]{:S(2)}, u32[]{:S(2)}) collective-permute-start(f32[4,2,32,128]{3,2,1,0:T(8,128)S(1)} %get-tuple-element.187), channel_id=1, source_target_pairs={{0,4},{1,5},{2,6},{3,7},{4,8},{5,9},{6,10},{7,11},{8,12},{9,13},{1... | collective-permute-start | bytes 393224 | tf_op jit(solution)/shard_map/ppermute | solution.py:37
  199.5 7.2 %collective-permute-start.43 = (f32[16,2,8,128]{3,2,1,0:T(8,128)S(1)}, f32[16,2,8,128]{3,2,1,0:T(8,128)S(1)}, u32[]{:S(2)}, u32[]{:S(2)}) collective-permute-start(f32[16,2,8,128]{3,2,1,0:T(8,128)S(1)} %get-tuple-element.189), channel_id=1, source_target_pairs={{0,32},{1,33},{2,34},{3,35},{4,36},{5,37},{6,38},{7,39},{8,40},{9,... | collective-permute-start | bytes 393224 | tf_op jit(solution)/shard_map/ppermute | solution.py:37
  207.7 3.4 %shard_map.159 = (f32[4,32,256]{2,1,0:T(8,128)S(1)}, f32[4,32,256]{2,1,0:T(8,128)S(1)}, f32[4,32,256]{2,1,0:T(8,128)S(1)}, f32[4,32,256]{2,1,0:T(8,128)S(1)}, f3...) custom-call(s32[4]{0:T(128)S(1)} %and_select_fusion.11.slots, ...), custom_call_target="tpu_custom_call" | custom-call | tf_op jit(solution)/shard_map/pallas_call | solution.py:109
  211.7 9.7 %collective-permute-start.46 = (f32[4,32,256]{2,1,0:T(8,128)S(1)}, f32[4,32,256]{2,1,0:T(8,128)S(1)}, u32[]{:S(2)}, u32[]{:S(2)}) collective-permute-start(f32[4,32,256]{2,1,0:T(8,128)S(1)} %get-tuple-element.196), channel_id=1, source_target_pairs={{0,1},{1,33},{2,3},{3,35},{4,5},{5,37},{6,7},{7,39},{8,9},{9,41},{... | collective-permute-start | bytes 393224 | tf_op jit(solution)/shard_map/ppermute | solution.py:37
  224.1 4.9 %collective-permute-done.46.p1 = f32[4,32,256]{2,1,0:T(8,128)S(1)} collective-permute-done((f32[4,32,256]{2,1,0:T(8,128)S(1)}, f32[4,32,256]{2,1,0:T(8,128)S(1)}, u32[]{:S(2)}, u32[]{:S(2)}) %collective-permute-start.46) | collective-permute-done | bytes 131104 | tf_op jit(solution)/shard_map/ppermute | solution.py:37
  236.4 10.3 %collective-permute-done.50.p1 = f32[4,64,256]{2,1,0:T(8,128)S(1)} collective-permute-done((f32[4,64,256]{2,1,0:T(8,128)}, f32[4,64,256]{2,1,0:T(8,128)S(1)}, u32[]{:S(2)}, u32[]{:S(2)}) %collective-permute-start.50) | collective-permute-done | bytes 262176 | tf_op jit(solution)/shard_map/ppermute | solution.py:37
  249.7 32.0 %collective-permute-start.56 = (f32[2,128,256]{2,1,0:T(8,128)S(1)}, f32[2,128,256]{2,1,0:T(8,128)S(1)}, u32[]{:S(2)}, u32[]{:S(2)}) collective-permute-start(f32[2,128,256]{2,1,0:T(8,128)S(1)} %get-tuple-element.224), channel_id=1, source_target_pairs={{0,80},{1,81},{2,82},{3,83},{4,84},{5,85},{6,86},{7,87},{8,88},{9,... | collective-permute-start | bytes 786440 | tf_op jit(solution)/shard_map/ppermute | solution.py:37
  281.6 5.9 %collective-permute-done.56 = f32[2,128,256]{2,1,0:T(8,128)S(1)} collective-permute-done((f32[2,128,256]{2,1,0:T(8,128)S(1)}, f32[2,128,256]{2,1,0:T(8,128)S(1)}, u32[]{:S(2)}, u32[]{:S(2)}) %collective-permute-start.56) | collective-permute-done | bytes 262176 | tf_op jit(solution)/shard_map/ppermute | solution.py:37
  288.4 3.7 %collective-permute-start.57 = (f32[4,128,256]{2,1,0:T(8,128)}, f32[4,128,256]{2,1,0:T(8,128)}, u32[]{:S(2)}, u32[]{:S(2)}) collective-permute-start(f32[4,128,256]{2,1,0:T(8,128)} %pad_maximum_fusion.1), channel_id=1, source_target_pairs={{0,80},{1,81},{2,82},{3,83},{4,84},{5,85},{6,86},{7,87},{8,88},{9,... | collective-permute-start | bytes 1572872 | tf_op jit(solution)/shard_map/ppermute | solution.py:37
  294.6 8.5 %collective-permute-done.57 = f32[4,128,256]{2,1,0:T(8,128)} collective-permute-done((f32[4,128,256]{2,1,0:T(8,128)}, f32[4,128,256]{2,1,0:T(8,128)}, u32[]{:S(2)}, u32[]{:S(2)}) %collective-permute-start.57) | collective-permute-done | bytes 524320 | tf_op jit(solution)/shard_map/ppermute | solution.py:37
  303.0 4.2 %collective-permute-done.55 = f32[4,128,256]{2,1,0:T(8,128)S(1)} collective-permute-done((f32[4,128,256]{2,1,0:T(8,128)}, f32[4,128,256]{2,1,0:T(8,128)S(1)}, u32[]{:S(2)}, u32[]{:S(2)}) %collective-permute-start.55) | collective-permute-done | bytes 524320 | tf_op jit(solution)/shard_map/ppermute | solution.py:37
  (228 shorter events, 105.0 us)
Async XLA Ops:
  2.6 15.9 %collective-permute-start.12 = (f32[4,128,256]{2,1,0:T(8,128)}, f32[4,128,256]{2,1,0:T(8,128)}, u32[]{:S(2)}, u32[]{:S(2)}) collective-permute-start(f32[4,128,256]{2,1,0:T(8,128)} %log.3), channel_id=1, source_target_pairs={{0,64},{1,65},{2,66},{3,67},{4,68},{5,69},{6,70},{7,71},{8,72},{9,... | collective-permute-start | bytes 1572872 | tf_op jit(solution)/shard_map/ppermute | solution.py:37
  4.2 23.1 %collective-permute-start.11 = (f32[4,128,256]{2,1,0:T(8,128)}, f32[4,128,256]{2,1,0:T(8,128)}, u32[]{:S(2)}, u32[]{:S(2)}) collective-permute-start(f32[4,128,256]{2,1,0:T(8,128)} %log.3), channel_id=1, source_target_pairs={{0,80},{1,81},{2,82},{3,83},{4,84},{5,85},{6,86},{7,87},{8,88},{9,... | collective-permute-start | bytes 1572872 | tf_op jit(solution)/shard_map/ppermute | solution.py:37
  15.1 16.5 %collective-permute-start.17 = (f32[4,128,256]{2,1,0:T(8,128)}, f32[4,128,256]{2,1,0:T(8,128)S(1)}, u32[]{:S(2)}, u32[]{:S(2)}) collective-permute-start(f32[4,128,256]{2,1,0:T(8,128)} %param.21), channel_id=1, source_target_pairs={{0,64},{1,65},{2,66},{3,67},{4,68},{5,69},{6,70},{7,71},{8,72},{9,... | collective-permute-start | bytes 1572872 | tf_op jit(solution)/shard_map/ppermute | solution.py:37
  15.6 17.9 %collective-permute-start.16 = (f32[4,128,256]{2,1,0:T(8,128)}, f32[4,128,256]{2,1,0:T(8,128)S(1)}, u32[]{:S(2)}, u32[]{:S(2)}) collective-permute-start(f32[4,128,256]{2,1,0:T(8,128)} %param.21), channel_id=1, source_target_pairs={{0,80},{1,81},{2,82},{3,83},{4,84},{5,85},{6,86},{7,87},{8,88},{9,... | collective-permute-start | bytes 1572872 | tf_op jit(solution)/shard_map/ppermute | solution.py:37
  20.2 16.3 %collective-permute-start.13 = (f32[2,128,256]{2,1,0:T(8,128)}, f32[2,128,256]{2,1,0:T(8,128)S(1)}, u32[]{:S(2)}, u32[]{:S(2)}) collective-permute-start(f32[2,128,256]{2,1,0:T(8,128)} %slice.65), channel_id=1, source_target_pairs={{0,64},{1,65},{2,66},{3,67},{4,68},{5,69},{6,70},{7,71},{8,72},{9,... | collective-permute-start | bytes 786440 | tf_op jit(solution)/shard_map/ppermute | solution.py:37
  25.5 29.2 %collective-permute-start.21 = (f32[4,176,256]{2,1,0:T(8,128)}, f32[4,176,256]{2,1,0:T(8,128)S(1)}, u32[]{:S(2)}, u32[]{:S(2)}) collective-permute-start(f32[4,176,256]{2,1,0:T(8,128)} %copy-done.38), channel_id=1, source_target_pairs={{0,0},{1,32},{2,2},{3,34},{4,4},{5,36},{6,6},{7,38},{8,8},{9,40},{... | collective-permute-start | bytes 2162696 | tf_op jit(solution)/shard_map/ppermute | solution.py:37
  31.7 23.0 %collective-permute-start.22 = (f32[4,176,256]{2,1,0:T(8,128)}, f32[4,176,256]{2,1,0:T(8,128)S(1)}, u32[]{:S(2)}, u32[]{:S(2)}) collective-permute-start(f32[4,176,256]{2,1,0:T(8,128)} %get-tuple-element.134), channel_id=1, source_target_pairs={{0,32},{1,2},{2,34},{3,0},{4,36},{5,6},{6,38},{7,4},{8,40},{9,10},... | collective-permute-start | bytes 2162696 | tf_op jit(solution)/shard_map/ppermute | solution.py:37
  33.5 22.1 %collective-permute-start.23 = (f32[4,176,256]{2,1,0:T(8,128)}, f32[4,176,256]{2,1,0:T(8,128)S(1)}, u32[]{:S(2)}, u32[]{:S(2)}) collective-permute-start(f32[4,176,256]{2,1,0:T(8,128)} %copy-done.37), channel_id=1, source_target_pairs={{0,2},{1,34},{2,0},{3,32},{4,6},{5,38},{6,4},{7,36},{8,10},{9,42},... | collective-permute-start | bytes 2162696 | tf_op jit(solution)/shard_map/ppermute | solution.py:37
  37.3 10.3 %collective-permute-start.19 = (f32[2,128,256]{2,1,0:T(8,128)S(1)}, f32[2,128,256]{2,1,0:T(8,128)S(1)}, u32[]{:S(2)}, u32[]{:S(2)}) collective-permute-start(f32[2,128,256]{2,1,0:T(8,128)S(1)} %slice.68), channel_id=1, source_target_pairs={{0,80},{1,81},{2,82},{3,83},{4,84},{5,85},{6,86},{7,87},{8,88},{9,... | collective-permute-start | bytes 786440 | tf_op jit(solution)/shard_map/ppermute | solution.py:37
  47.6 14.2 %collective-permute-start.24 = (f32[4,176,256]{2,1,0:T(8,128)S(1)}, f32[4,176,256]{2,1,0:T(8,128)S(1)}, u32[]{:S(2)}, u32[]{:S(2)}) collective-permute-start(f32[4,176,256]{2,1,0:T(8,128)S(1)} %get-tuple-element.142), channel_id=1, source_target_pairs={{0,34},{1,0},{2,32},{3,2},{4,38},{5,4},{6,36},{7,6},{8,42},{9,8},{... | collective-permute-start | bytes 2162696 | tf_op jit(solution)/shard_map/ppermute | solution.py:37
  65.1 21.4 %collective-permute-start.27 = (f32[4,96,256]{2,1,0:T(8,128)}, f32[4,96,256]{2,1,0:T(8,128)S(1)}, u32[]{:S(2)}, u32[]{:S(2)}) collective-permute-start(f32[4,96,256]{2,1,0:T(8,128)} %get-tuple-element.156), channel_id=1, source_target_pairs={{0,0},{1,32},{2,2},{3,34},{4,4},{5,36},{6,6},{7,38},{8,8},{9,40},{... | collective-permute-start | bytes 1179656 | tf_op jit(solution)/shard_map/ppermute | solution.py:37
  66.7 21.8 %collective-permute-start.28 = (f32[4,96,256]{2,1,0:T(8,128)}, f32[4,96,256]{2,1,0:T(8,128)}, u32[]{:S(2)}, u32[]{:S(2)}) collective-permute-start(f32[4,96,256]{2,1,0:T(8,128)} %get-tuple-element.157), channel_id=1, source_target_pairs={{0,32},{1,2},{2,34},{3,0},{4,36},{5,6},{6,38},{7,4},{8,40},{9,10},... | collective-permute-start | bytes 1179656 | tf_op jit(solution)/shard_map/ppermute | solution.py:37
  72.8 15.7 %collective-permute-start.29 = (f32[4,96,256]{2,1,0:T(8,128)}, f32[4,96,256]{2,1,0:T(8,128)}, u32[]{:S(2)}, u32[]{:S(2)}) collective-permute-start(f32[4,96,256]{2,1,0:T(8,128)} %get-tuple-element.158), channel_id=1, source_target_pairs={{0,2},{1,34},{2,0},{3,32},{4,6},{5,38},{6,4},{7,36},{8,10},{9,42},... | collective-permute-start | bytes 1179656 | tf_op jit(solution)/shard_map/ppermute | solution.py:37
  74.9 17.3 %collective-permute-start.30 = (f32[4,96,256]{2,1,0:T(8,128)}, f32[4,96,256]{2,1,0:T(8,128)}, u32[]{:S(2)}, u32[]{:S(2)}) collective-permute-start(f32[4,96,256]{2,1,0:T(8,128)} %get-tuple-element.159), channel_id=1, source_target_pairs={{0,34},{1,0},{2,32},{3,2},{4,38},{5,4},{6,36},{7,6},{8,42},{9,8},{... | collective-permute-start | bytes 1179656 | tf_op jit(solution)/shard_map/ppermute | solution.py:37
  82.6 30.9 %collective-permute-start.25 = (f32[4,2,144,128]{3,2,1,0:T(8,128)}, f32[4,2,144,128]{3,2,1,0:T(8,128)S(1)}, u32[]{:S(2)}, u32[]{:S(2)}) collective-permute-start(f32[4,2,144,128]{3,2,1,0:T(8,128)} %get-tuple-element.150), channel_id=1, source_target_pairs={{0,4},{1,5},{2,6},{3,7},{4,8},{5,9},{6,10},{7,11},{8,12},{9,13},{1... | collective-permute-start | bytes 1769480 | tf_op jit(solution)/shard_map/ppermute | solution.py:37
  87.2 26.3 %collective-permute-start.26 = (f32[4,2,144,128]{3,2,1,0:T(8,128)}, f32[4,2,144,128]{3,2,1,0:T(8,128)S(1)}, u32[]{:S(2)}, u32[]{:S(2)}) collective-permute-start(f32[4,2,144,128]{3,2,1,0:T(8,128)} %get-tuple-element.151), channel_id=1, source_target_pairs={{4,0},{5,1},{6,2},{7,3},{8,4},{9,5},{10,6},{11,7},{12,8},{13,9},{1... | collective-permute-start | bytes 1769480 | tf_op jit(solution)/shard_map/ppermute | solution.py:37
  97.2 17.6 %collective-permute-start.31 = (f32[4,2,112,128]{3,2,1,0:T(8,128)}, f32[4,2,112,128]{3,2,1,0:T(8,128)}, u32[]{:S(2)}, u32[]{:S(2)}) collective-permute-start(f32[4,2,112,128]{3,2,1,0:T(8,128)} %get-tuple-element.162), channel_id=1, source_target_pairs={{0,4},{1,5},{2,6},{3,7},{4,8},{5,9},{6,10},{7,11},{8,12},{9,13},{1... | collective-permute-start | bytes 1376264 | tf_op jit(solution)/shard_map/ppermute | solution.py:37
  101.9 15.7 %collective-permute-start.32 = (f32[4,2,112,128]{3,2,1,0:T(8,128)}, f32[4,2,112,128]{3,2,1,0:T(8,128)}, u32[]{:S(2)}, u32[]{:S(2)}) collective-permute-start(f32[4,2,112,128]{3,2,1,0:T(8,128)} %get-tuple-element.163), channel_id=1, source_target_pairs={{4,0},{5,1},{6,2},{7,3},{8,4},{9,5},{10,6},{11,7},{12,8},{13,9},{1... | collective-permute-start | bytes 1376264 | tf_op jit(solution)/shard_map/ppermute | solution.py:37
  130.8 9.2 %collective-permute-start.33 = (f32[8,2,32,128]{3,2,1,0:T(8,128)}, f32[8,2,32,128]{3,2,1,0:T(8,128)}, u32[]{:S(2)}, u32[]{:S(2)}) collective-permute-start(f32[8,2,32,128]{3,2,1,0:T(8,128)} %get-tuple-element.171), channel_id=1, source_target_pairs={{0,4},{1,5},{2,6},{3,7},{4,8},{5,9},{6,10},{7,11},{8,12},{9,13},{1... | collective-permute-start | bytes 786440 | tf_op jit(solution)/shard_map/ppermute | solution.py:37
  134.6 10.2 %collective-permute-start.34 = (f32[8,2,32,128]{3,2,1,0:T(8,128)}, f32[8,2,32,128]{3,2,1,0:T(8,128)}, u32[]{:S(2)}, u32[]{:S(2)}) collective-permute-start(f32[8,2,32,128]{3,2,1,0:T(8,128)} %get-tuple-element.172), channel_id=1, source_target_pairs={{4,0},{5,1},{6,2},{7,3},{8,4},{9,5},{10,6},{11,7},{12,8},{13,9},{1... | collective-permute-start | bytes 786440 | tf_op jit(solution)/shard_map/ppermute | solution.py:37
  164.3 9.2 %collective-permute-start.37 = (f32[8,2,32,128]{3,2,1,0:T(8,128)S(1)}, f32[8,2,32,128]{3,2,1,0:T(8,128)S(1)}, u32[]{:S(2)}, u32[]{:S(2)}) collective-permute-start(f32[8,2,32,128]{3,2,1,0:T(8,128)S(1)} %get-tuple-element.180), channel_id=1, source_target_pairs={{0,4},{1,5},{2,6},{3,7},{4,8},{5,9},{6,10},{7,11},{8,12},{9,13},{1... | collective-permute-start | bytes 786440 | tf_op jit(solution)/shard_map/ppermute | solution.py:37
  191.5 15.9 %collective-permute-start.41 = (f32[4,2,32,128]{3,2,1,0:T(8,128)S(1)}, f32[4,2,32,128]{3,2,1,0:T(8,128)S(1)}, u32[]{:S(2)}, u32[]{:S(2)}) collective-permute-start(f32[4,2,32,128]{3,2,1,0:T(8,128)S(1)} %get-tuple-element.187), channel_id=1, source_target_pairs={{0,4},{1,5},{2,6},{3,7},{4,8},{5,9},{6,10},{7,11},{8,12},{9,13},{1... | collective-permute-start | bytes 393224 | tf_op jit(solution)/shard_map/ppermute | solution.py:37
  198.2 9.2 %collective-permute-start.42 = (f32[4,2,32,128]{3,2,1,0:T(8,128)S(1)}, f32[4,2,32,128]{3,2,1,0:T(8,128)S(1)}, u32[]{:S(2)}, u32[]{:S(2)}) collective-permute-start(f32[4,2,32,128]{3,2,1,0:T(8,128)S(1)} %get-tuple-element.188), channel_id=1, source_target_pairs={{4,0},{5,1},{6,2},{7,3},{8,4},{9,5},{10,6},{11,7},{12,8},{13,9},{1... | collective-permute-start | bytes 393224 | tf_op jit(solution)/shard_map/ppermute | solution.py:37
  211.1 13.0 %collective-permute-start.45 = (f32[4,32,256]{2,1,0:T(8,128)S(1)}, f32[4,32,256]{2,1,0:T(8,128)S(1)}, u32[]{:S(2)}, u32[]{:S(2)}) collective-permute-start(f32[4,32,256]{2,1,0:T(8,128)S(1)} %get-tuple-element.195), channel_id=1, source_target_pairs={{0,0},{1,32},{2,2},{3,34},{4,4},{5,36},{6,6},{7,38},{8,8},{9,40},{... | collective-permute-start | bytes 393224 | tf_op jit(solution)/shard_map/ppermute | solution.py:37
  211.7 17.2 %collective-permute-start.46 = (f32[4,32,256]{2,1,0:T(8,128)S(1)}, f32[4,32,256]{2,1,0:T(8,128)S(1)}, u32[]{:S(2)}, u32[]{:S(2)}) collective-permute-start(f32[4,32,256]{2,1,0:T(8,128)S(1)} %get-tuple-element.196), channel_id=1, source_target_pairs={{0,1},{1,33},{2,3},{3,35},{4,5},{5,37},{6,7},{7,39},{8,9},{9,41},{... | collective-permute-start | bytes 393224 | tf_op jit(solution)/shard_map/ppermute | solution.py:37
  231.2 15.5 %collective-permute-start.50 = (f32[4,64,256]{2,1,0:T(8,128)}, f32[4,64,256]{2,1,0:T(8,128)S(1)}, u32[]{:S(2)}, u32[]{:S(2)}) collective-permute-start(f32[4,64,256]{2,1,0:T(8,128)} %get-tuple-element.208), channel_id=1, source_target_pairs={{0,1},{1,33},{2,3},{3,35},{4,5},{5,37},{6,7},{7,39},{8,9},{9,41},{... | collective-permute-start | bytes 786440 | tf_op jit(solution)/shard_map/ppermute | solution.py:37
  233.3 14.2 %collective-permute-start.51 = (f32[4,64,256]{2,1,0:T(8,128)S(1)}, f32[4,64,256]{2,1,0:T(8,128)S(1)}, u32[]{:S(2)}, u32[]{:S(2)}) collective-permute-start(f32[4,64,256]{2,1,0:T(8,128)S(1)} %get-tuple-element.209), channel_id=1, source_target_pairs={{0,2},{1,34},{2,0},{3,32},{4,6},{5,38},{6,4},{7,36},{8,10},{9,42},... | collective-permute-start | bytes 786440 | tf_op jit(solution)/shard_map/ppermute | solution.py:37
  235.2 12.3 %collective-permute-start.52 = (f32[4,64,256]{2,1,0:T(8,128)S(1)}, f32[4,64,256]{2,1,0:T(8,128)S(1)}, u32[]{:S(2)}, u32[]{:S(2)}) collective-permute-start(f32[4,64,256]{2,1,0:T(8,128)S(1)} %get-tuple-element.210), channel_id=1, source_target_pairs={{0,3},{1,35},{2,1},{3,33},{4,7},{5,39},{6,5},{7,37},{8,11},{9,43},... | collective-permute-start | bytes 786440 | tf_op jit(solution)/shard_map/ppermute | solution.py:37
  249.7 37.8 %collective-permute-start.56 = (f32[2,128,256]{2,1,0:T(8,128)S(1)}, f32[2,128,256]{2,1,0:T(8,128)S(1)}, u32[]{:S(2)}, u32[]{:S(2)}) collective-permute-start(f32[2,128,256]{2,1,0:T(8,128)S(1)} %get-tuple-element.224), channel_id=1, source_target_pairs={{0,80},{1,81},{2,82},{3,83},{4,84},{5,85},{6,86},{7,87},{8,88},{9,... | collective-permute-start | bytes 786440 | tf_op jit(solution)/shard_map/ppermute | solution.py:37
  281.6 10.5 %collective-permute-start.54 = (f32[2,128,256]{2,1,0:T(8,128)S(1)}, f32[2,128,256]{2,1,0:T(8,128)S(1)}, u32[]{:S(2)}, u32[]{:S(2)}) collective-permute-start(f32[2,128,256]{2,1,0:T(8,128)S(1)} %get-tuple-element.223), channel_id=1, source_target_pairs={{0,64},{1,65},{2,66},{3,67},{4,68},{5,69},{6,70},{7,71},{8,72},{9,... | collective-permute-start | bytes 786440 | tf_op jit(solution)/shard_map/ppermute | solution.py:37
  288.4 14.7 %collective-permute-start.57 = (f32[4,128,256]{2,1,0:T(8,128)}, f32[4,128,256]{2,1,0:T(8,128)}, u32[]{:S(2)}, u32[]{:S(2)}) collective-permute-start(f32[4,128,256]{2,1,0:T(8,128)} %pad_maximum_fusion.1), channel_id=1, source_target_pairs={{0,80},{1,81},{2,82},{3,83},{4,84},{5,85},{6,86},{7,87},{8,88},{9,... | collective-permute-start | bytes 1572872 | tf_op jit(solution)/shard_map/ppermute | solution.py:37
  293.0 14.3 %collective-permute-start.55 = (f32[4,128,256]{2,1,0:T(8,128)}, f32[4,128,256]{2,1,0:T(8,128)S(1)}, u32[]{:S(2)}, u32[]{:S(2)}) collective-permute-start(f32[4,128,256]{2,1,0:T(8,128)} %pad_maximum_fusion), channel_id=1, source_target_pairs={{0,64},{1,65},{2,66},{3,67},{4,68},{5,69},{6,70},{7,71},{8,72},{9,... | collective-permute-start | bytes 1572872 | tf_op jit(solution)/shard_map/ppermute | solution.py:37
  (68 other events, 572.6 us)

commit v2 on v0

--- a/solution.py
+++ b/solution.py
@@ -380,9 +380,9 @@
     stack_near(adjoint_near, below, adjoint, above, SPAN + 2 * CELLS)
 
 
-def model_body(log_mass, speed, below, above, speed_sq, s0, s1, s2, twice, wide, speed_near):
-    stack_wide(wide, below, log_mass, above, 0)
-    stack_near(speed_near, below, speed, above, SPAN + CELLS)
+def model_body(log_mass, speed, log_below, log_above, below, above, speed_sq, s0, s1, s2, twice, wide, speed_near):
+    stack_wide(wide, log_below, log_mass, log_above, 0)
+    stack_near(speed_near, below, speed, above, 0)
     twice[...] = 2.0 / speed[:, :, 8 : 8 + CELLS, :]
     lane = lanes()
 
@@ -563,10 +563,11 @@
     velocity, partner, *pieces = lax.optimization_barrier((velocity, partner, *pieces))
     pair_core, pair_step, _ = wanted(partner[0])
 
-    def gathered(slab):
+    def gathered(slab, *others):
         from_below = send_x(slab, 1)
         from_above = send_x(slab, -1)
         far = jnp.concatenate([send_x(from_below[0:2], 1), send_x(from_above[2:4], -1)])
+        far, *others = lax.optimization_barrier((far, *others))
 
         def pick(step):
             return jnp.where(
@@ -574,7 +575,7 @@
             )
 
         other = send_core(pick(pair_step))
-        return jnp.where(own_core == core, pick(own_step), other)
+        return jnp.where(own_core == core, pick(own_step), other), *others
 
     def turned(arrays, steps):
         def branch(count):
@@ -582,9 +583,8 @@
 
         return lax.switch(steps, [branch(count) for count in (0, 1, 2, -1)], *arrays)
 
-    log_slab = gathered(jnp.log(density))
-    speed_slab = gathered(velocity)
-    pieces = sent_pieces(pieces)
+    log_slab, *pieces = gathered(jnp.log(density), *sent_pieces(pieces))
+    (speed_slab,) = gathered(velocity)
 
     def local_place(cells, rows_more, cells_more):
         rows = cells // (NY * NZ) - group * ROWS + rows_more
@@ -611,20 +611,27 @@
     place = jnp.stack(source_place(4, 8) + source_place(0, 0))
     amount = wavelet[0]
 
+    steps = (4 - turn_by) % 4
     log_slab, speed_slab = lax.optimization_barrier((log_slab, speed_slab))
-    log_slab, speed_slab = turned((log_slab, speed_slab), (4 - turn_by) % 4)
-    log_slab, speed_slab, *pieces = lax.optimization_barrier((log_slab, speed_slab, *pieces))
-    model_pieces = sent_pieces(cut_pieces([log_slab, speed_slab], (True, True), chunks_out))
+    (log_slab,) = turned((log_slab,), steps)
+    log_pieces = cut_pieces([log_slab], (True,), chunks_out)
+    speed_slab, *log_pieces = lax.optimization_barrier((speed_slab, *log_pieces))
+    log_pieces = sent_pieces(log_pieces)
+    (speed_slab,) = turned((speed_slab,), steps)
+    speed_slab, *log_pieces = lax.optimization_barrier((speed_slab, *log_pieces))
+    speed_pieces = sent_pieces(cut_pieces([speed_slab], (True,), chunks_out))
+    log_mass, side_low, side_high = gather_blocks(log_pieces, slots_in, (8,))
+    log_halo = send_group(side_high, 1), send_group(side_low, -1)
     now, old, adjoint, a_later, side_low, side_high = gather_blocks(pieces, chunks_in, (8, 4, 4, 0))
     below, above = send_group(side_high, 1), send_group(side_low, -1)
     u_wide, old_near, a_near = call(
         fields_body, [WIDE, NEAR, NEAR], 0, (now, old, adjoint, below, above)
     )
-    log_mass, speed, side_low, side_high = gather_blocks(model_pieces, slots_in, (8, 4))
+    speed, side_low, side_high = gather_blocks(speed_pieces, slots_in, (4,))
     below, above = send_group(side_high, 1), send_group(side_low, -1)
     below, above, maps = lax.optimization_barrier((below, above, maps))
     *model, twice = call(
-        model_body, [NEAR] * 4 + [BLOCK], 0, (log_mass, speed, below, above), (WIDE, NEAR)
+        model_body, [NEAR] * 4 + [BLOCK], 0, (log_mass, speed, *log_halo, below, above), (WIDE, NEAR)
     )
 
     u1, u2, *edges = call(

time: 276 us -> 300 us (1.087)
  starting transfers between devices: 116 us -> 135 us
  waiting for transfers between devices: 97.9 us -> 84.7 us
  other arithmetic: 7.89 us -> 14.7 us
  Pallas kernels: 32.5 us -> 38.1 us
    ppermute x48 -> x53, starting transfers between devices: 116 us -> 135 us  [send(): return lax.ppermute(value, ('shot', 'sub'), pairs_by(move))]
    ppermute x48 -> x53, waiting for transfers between devices: 97.9 us -> 84.7 us  [send(): return lax.ppermute(value, ('shot', 'sub'), pairs_by(move))]
    pallas_call x14 -> x16, Pallas kernels: 32.5 us -> 38.1 us  [call(): pl.pallas_call(body, out_shape=tuple(outs), in_specs=specs, out_specs=tup...]
  transfers between devices with their start and end apart: 48 -> 53, of which waited for: 28 -> 29; matrix products, arithmetic and copies ran while one was open for 6% -> 8% of each run, Pallas kernels for 2% -> 5%
where the time goes in v2:
time: 300 us; the launch traced here: 295 us
  starting transfers between devices  135 us (45%)
  waiting for transfers between devices  84.7 us (28%)
  Pallas kernels  38.1 us (13%)
  other arithmetic  14.7 us (5%)
  local copies, waits for them, and re-layouts  12.4 us (4%)
  between operations  5.63 us (2%)
  matrix products  4.96 us (2%)
    ppermute x53, starting transfers between devices, send(): return lax.ppermute(value, ('shot', 'sub'), pairs_by(move))  135 us
    ppermute x53, waiting for transfers between devices, send(): return lax.ppermute(value, ('shot', 'sub'), pairs_by(move))  84.7 us
    pallas_call x16, Pallas kernels, call(): pl.pallas_call(body, out_shape=tuple(outs), in_specs=specs, out_specs=tup...  38.1 us
  transfers between devices with their start and end apart: 53, of which 29 were waited for; matrix products, arithmetic and copies ran while one was open for 8% of the time, Pallas kernels for 5%

profile of v2, /device:TPU:0, one launch (start us, length us, event | category | flops | bytes accessed | tf_op | source)
XLA Modules:
  0.0 295.3 jit_solution(16898670887316505560)
XLA Ops:
  1.9 2.9 collective-permute-start.11
  13.8 3.3 %collective-permute-done.11 = f32[4,128,256]{2,1,0:T(8,128)} collective-permute-done((f32[4,128,256]{2,1,0:T(8,128)S(1)}, f32[4,128,256]{2,1,0:T(8,128)}, u32[]{:S(2)}, u32[]{:S(2)}) %collective-permute-start.11) | collective-permute-done | bytes 524320 | tf_op jit(solution)/shard_map/ppermute | solution.py:37
  17.1 3.2 %collective-permute-start.15 = (f32[4,176,256]{2,1,0:T(8,128)}, f32[4,176,256]{2,1,0:T(8,128)S(1)}, u32[]{:S(2)}, u32[]{:S(2)}) collective-permute-start(f32[4,176,256]{2,1,0:T(8,128)} %get-tuple-element.142), channel_id=1, source_target_pairs={{0,2},{1,3},{2,0},{3,1},{4,6},{5,7},{6,4},{7,5},{8,10},{9,11},{10,... | collective-permute-start | bytes 2162696 | tf_op jit(solution)/shard_map/ppermute | solution.py:37
  20.9 3.0 %collective-permute-start.16 = (f32[4,176,256]{2,1,0:T(8,128)}, f32[4,176,256]{2,1,0:T(8,128)S(1)}, u32[]{:S(2)}, u32[]{:S(2)}) collective-permute-start(f32[4,176,256]{2,1,0:T(8,128)} %get-tuple-element.143), channel_id=1, source_target_pairs={{0,3},{1,0},{2,1},{3,2},{4,7},{5,4},{6,5},{7,6},{8,11},{9,8},{10,9... | collective-permute-start | bytes 2162696 | tf_op jit(solution)/shard_map/ppermute | solution.py:37
  42.2 6.4 %collective-permute-done.15.refs_2_ = f32[4,176,256]{2,1,0:T(8,128)S(1)} collective-permute-done((f32[4,176,256]{2,1,0:T(8,128)}, f32[4,176,256]{2,1,0:T(8,128)S(1)}, u32[]{:S(2)}, u32[]{:S(2)}) %collective-permute-start.15) | collective-permute-done | bytes 720928 | tf_op jit(solution)/shard_map/ppermute | solution.py:37
  56.9 4.7 %collective-permute-start.17 = (f32[4,2,144,128]{3,2,1,0:T(8,128)}, f32[4,2,144,128]{3,2,1,0:T(8,128)}, u32[]{:S(2)}, u32[]{:S(2)}) collective-permute-start(f32[4,2,144,128]{3,2,1,0:T(8,128)} %get-tuple-element.151), channel_id=1, source_target_pairs={{0,4},{1,5},{2,6},{3,7},{4,8},{5,9},{6,10},{7,11},{8,12},{9,13},{1... | collective-permute-start | bytes 1769480 | tf_op jit(solution)/shard_map/ppermute | solution.py:37
  75.9 4.9 %collective-permute-done.26.refs_2_ = f32[4,48,256]{2,1,0:T(8,128)S(1)} collective-permute-done((f32[4,48,256]{2,1,0:T(8,128)S(1)}, f32[4,48,256]{2,1,0:T(8,128)S(1)}, u32[]{:S(2)}, u32[]{:S(2)}) %collective-permute-start.26) | collective-permute-done | bytes 196640 | tf_op jit(solution)/shard_map/ppermute | solution.py:37
  89.4 3.0 %collective-permute-start.31 = (f32[4,2,80,128]{3,2,1,0:T(8,128)}, f32[4,2,80,128]{3,2,1,0:T(8,128)S(1)}, u32[]{:S(2)}, u32[]{:S(2)}) collective-permute-start(f32[4,2,80,128]{3,2,1,0:T(8,128)} %get-tuple-element.180), channel_id=1, source_target_pairs={{0,4},{1,5},{2,6},{3,7},{4,8},{5,9},{6,10},{7,11},{8,12},{9,13},{1... | collective-permute-start | bytes 983048 | tf_op jit(solution)/shard_map/ppermute | solution.py:37
  97.3 5.2 %collective-permute-start.33 = (f32[4,2,32,128]{3,2,1,0:T(8,128)}, f32[4,2,32,128]{3,2,1,0:T(8,128)}, u32[]{:S(2)}, u32[]{:S(2)}) collective-permute-start(f32[4,2,32,128]{3,2,1,0:T(8,128)} %get-tuple-element.182), channel_id=1, source_target_pairs={{0,4},{1,5},{2,6},{3,7},{4,8},{5,9},{6,10},{7,11},{8,12},{9,13},{1... | collective-permute-start | bytes 393224 | tf_op jit(solution)/shard_map/ppermute | solution.py:37
  103.8 5.0 %fusion.refs_13_.refs_11_.maps = f32[24,2,48,640]{3,2,1,0:T(8,128)} fusion(f32[256,640,1,1]{0,1,3,2:T(8,128)S(1)} %bitcast.43, s32[256]{0:T(256)S(1)} %bitcast.46, s32[24,2,48]{2,1,0:T(2,128)S(1)} %copy-done.23), kind=kOutput, calls=%fused_computation | convolution fusion | flops 4530438144 | bytes 6563840 | tf_op jit(solution)/shard_map/dot_general | solution.py:603
  112.5 4.0 %shard_map.137 = (f32[24,2,48,128]{3,2,1,0:T(8,128)S(1)}, f32[24,2,48,128]{3,2,1,0:T(8,128)S(1)}, f32[24,2,48,128]{3,2,1,0:T(8,128)S(1)}, f32[24,2,48,128]{3,2,1,0:T(8,128)S(1)}, f32[16,2,32,128]{3,2,1,0:T(8,128)S(1)}) custom-call(f32[16,2,48,128]{3,2,1,0:T(8,128)S(1)} %get-tuple-element.173.log_mass, f32[16,2,48,128]{3,2,1,0:T(8,128)S(1)} %copy-done.1, ...), custom_call_target="tpu_custom_call" | custom-call | tf_op jit(solution)/shard_map/pallas_call | solution.py:91
  116.5 5.5 %shard_map.138 = (f32[24,2,48,128]{3,2,1,0:T(8,128)S(1)}, f32[16,2,32,128]{3,2,1,0:T(8,128)S(1)}, f32[8,2,32,128]{3,2,1,0:T(8,128)S(1)}, f32[8,2,32,128]{3,2,1,0...) custom-call(s32[10]{0:T(128)S(1)} %stack.45.place, f32[4]{0:T(128)S(1)} %bitcast.41, ...), custom_call_target="tpu_custom_call" | custom-call | tf_op jit(solution)/shard_map/pallas_call | solution.py:91
  122.1 4.6 %collective-permute-start.35 = (f32[8,2,32,128]{3,2,1,0:T(8,128)S(1)}, f32[8,2,32,128]{3,2,1,0:T(8,128)S(1)}, u32[]{:S(2)}, u32[]{:S(2)}) collective-permute-start(f32[8,2,32,128]{3,2,1,0:T(8,128)S(1)} %get-tuple-element.191), channel_id=1, source_target_pairs={{0,4},{1,5},{2,6},{3,7},{4,8},{5,9},{6,10},{7,11},{8,12},{9,13},{1... | collective-permute-start | bytes 786440 | tf_op jit(solution)/shard_map/ppermute | solution.py:37
  130.7 4.2 %collective-permute-done.36.above.refs_1_ = f32[8,2,32,128]{3,2,1,0:T(8,128)S(1)} collective-permute-done((f32[8,2,32,128]{3,2,1,0:T(8,128)S(1)}, f32[8,2,32,128]{3,2,1,0:T(8,128)S(1)}, u32[]{:S(2)}, u32[]{:S(2)}) %collective-permute-start.36) | collective-permute-done | bytes 262176 | tf_op jit(solution)/shard_map/ppermute | solution.py:37
  138.2 4.3 %collective-permute-done.40.refs_5_ = f32[8,2,8,128]{3,2,1,0:T(8,128)S(1)} collective-permute-done((f32[8,2,8,128]{3,2,1,0:T(8,128)S(1)}, f32[8,2,8,128]{3,2,1,0:T(8,128)S(1)}, u32[]{:S(2)}, u32[]{:S(2)}) %collective-permute-start.40) | collective-permute-done | bytes 65568 | tf_op jit(solution)/shard_map/ppermute | solution.py:37
  142.4 7.4 %shard_map.140 = (f32[24,2,48,128]{3,2,1,0:T(8,128)S(1)}, f32[16,2,32,128]{3,2,1,0:T(8,128)S(1)}, f32[16,2,32,128]{3,2,1,0:T(8,128)S(1)}, f32[16,2,32,128]{3,2,1...) custom-call(s32[10]{0:T(128)S(1)} %stack.45.place, ...), custom_call_target="tpu_custom_call" | custom-call | tf_op jit(solution)/shard_map/pallas_call | solution.py:91
  149.8 7.2 %collective-permute-start.41 = (f32[8,2,32,128]{3,2,1,0:T(8,128)S(1)}, f32[8,2,32,128]{3,2,1,0:T(8,128)S(1)}, u32[]{:S(2)}, u32[]{:S(2)}) collective-permute-start(f32[8,2,32,128]{3,2,1,0:T(8,128)S(1)} %get-tuple-element.202), channel_id=1, source_target_pairs={{0,4},{1,5},{2,6},{3,7},{4,8},{5,9},{6,10},{7,11},{8,12},{9,13},{1... | collective-permute-start | bytes 786440 | tf_op jit(solution)/shard_map/ppermute | solution.py:37
  162.1 5.5 %collective-permute-done.42.above.refs_1_ = f32[8,2,32,128]{3,2,1,0:T(8,128)S(1)} collective-permute-done((f32[8,2,32,128]{3,2,1,0:T(8,128)S(1)}, f32[8,2,32,128]{3,2,1,0:T(8,128)S(1)}, u32[]{:S(2)}, u32[]{:S(2)}) %collective-permute-start.42) | collective-permute-done | bytes 262176 | tf_op jit(solution)/shard_map/ppermute | solution.py:37
  172.0 4.3 %collective-permute-done.46.refs_5_ = f32[8,2,8,128]{3,2,1,0:T(8,128)S(1)} collective-permute-done((f32[8,2,8,128]{3,2,1,0:T(8,128)S(1)}, f32[8,2,8,128]{3,2,1,0:T(8,128)S(1)}, u32[]{:S(2)}, u32[]{:S(2)}) %collective-permute-start.46) | collective-permute-done | bytes 65568 | tf_op jit(solution)/shard_map/ppermute | solution.py:37
  176.3 5.2 %shard_map.142 = (f32[24,2,48,128]{3,2,1,0:T(8,128)S(1)}, f32[16,2,32,128]{3,2,1,0:T(8,128)S(1)}, f32[16,2,32,128]{3,2,1,0:T(8,128)S(1)}, f32[4,2,32,128]{3,2,1,...) custom-call(f32[16,2,32,128]{3,2,1,0:T(8,128)S(1)} %get-tuple-element.20, ...), custom_call_target="tpu_custom_call" | custom-call | tf_op jit(solution)/shard_map/pallas_call | solution.py:91
  181.5 7.4 %collective-permute-start.47 = (f32[4,2,32,128]{3,2,1,0:T(8,128)S(1)}, f32[4,2,32,128]{3,2,1,0:T(8,128)S(1)}, u32[]{:S(2)}, u32[]{:S(2)}) collective-permute-start(f32[4,2,32,128]{3,2,1,0:T(8,128)S(1)} %get-tuple-element.211), channel_id=1, source_target_pairs={{0,4},{1,5},{2,6},{3,7},{4,8},{5,9},{6,10},{7,11},{8,12},{9,13},{1... | collective-permute-start | bytes 393224 | tf_op jit(solution)/shard_map/ppermute | solution.py:37
  190.2 3.7 %collective-permute-start.49 = (f32[16,2,8,128]{3,2,1,0:T(8,128)S(1)}, f32[16,2,8,128]{3,2,1,0:T(8,128)S(1)}, u32[]{:S(2)}, u32[]{:S(2)}) collective-permute-start(f32[16,2,8,128]{3,2,1,0:T(8,128)S(1)} %get-tuple-element.213), channel_id=1, source_target_pairs={{0,1},{1,2},{2,3},{4,5},{5,6},{6,7},{8,9},{9,10},{10,11},{12,13},{... | collective-permute-start | bytes 393224 | tf_op jit(solution)/shard_map/ppermute | solution.py:37
  197.8 4.5 %collective-permute-done.50.right = f32[16,2,8,128]{3,2,1,0:T(8,128)S(1)} collective-permute-done((f32[16,2,8,128]{3,2,1,0:T(8,128)S(1)}, f32[16,2,8,128]{3,2,1,0:T(8,128)S(1)}, u32[]{:S(2)}, u32[]{:S(2)}) %collective-permute-start.50) | collective-permute-done | bytes 131104 | tf_op jit(solution)/shard_map/ppermute | solution.py:37
  208.2 6.6 %collective-permute-done.51.p1 = f32[4,32,256]{2,1,0:T(8,128)S(1)} collective-permute-done((f32[4,32,256]{2,1,0:T(8,128)S(1)}, f32[4,32,256]{2,1,0:T(8,128)S(1)}, u32[]{:S(2)}, u32[]{:S(2)}) %collective-permute-start.51) | collective-permute-done | bytes 131104 | tf_op jit(solution)/shard_map/ppermute | solution.py:37
  215.5 3.3 %collective-permute-start.55 = (f32[4,64,256]{2,1,0:T(8,128)S(1)}, f32[4,64,256]{2,1,0:T(8,128)S(1)}, u32[]{:S(2)}, u32[]{:S(2)}) collective-permute-start(f32[4,64,256]{2,1,0:T(8,128)S(1)} %get-tuple-element.233), channel_id=1, source_target_pairs={{0,2},{1,3},{2,0},{3,1},{4,6},{5,7},{6,4},{7,5},{8,10},{9,11},{10,... | collective-permute-start | bytes 786440 | tf_op jit(solution)/shard_map/ppermute | solution.py:37
  219.4 3.4 %collective-permute-done.54.p1 = f32[4,64,256]{2,1,0:T(8,128)S(1)} collective-permute-done((f32[4,64,256]{2,1,0:T(8,128)S(1)}, f32[4,64,256]{2,1,0:T(8,128)S(1)}, u32[]{:S(2)}, u32[]{:S(2)}) %collective-permute-start.54) | collective-permute-done | bytes 262176 | tf_op jit(solution)/shard_map/ppermute | solution.py:37
  222.8 3.1 %collective-permute-done.55.p2 = f32[4,64,256]{2,1,0:T(8,128)S(1)} collective-permute-done((f32[4,64,256]{2,1,0:T(8,128)S(1)}, f32[4,64,256]{2,1,0:T(8,128)S(1)}, u32[]{:S(2)}, u32[]{:S(2)}) %collective-permute-start.55) | collective-permute-done | bytes 262176 | tf_op jit(solution)/shard_map/ppermute | solution.py:37
  228.7 39.1 %collective-permute-start.60 = (f32[2,128,256]{2,1,0:T(8,128)S(1)}, f32[2,128,256]{2,1,0:T(8,128)S(1)}, u32[]{:S(2)}, u32[]{:S(2)}) collective-permute-start(f32[2,128,256]{2,1,0:T(8,128)S(1)} %get-tuple-element.248), channel_id=1, source_target_pairs={{0,80},{1,81},{2,82},{3,83},{4,84},{5,85},{6,86},{7,87},{8,88},{9,... | collective-permute-start | bytes 786440 | tf_op jit(solution)/shard_map/ppermute | solution.py:37
  267.7 5.9 %collective-permute-done.60 = f32[2,128,256]{2,1,0:T(8,128)S(1)} collective-permute-done((f32[2,128,256]{2,1,0:T(8,128)S(1)}, f32[2,128,256]{2,1,0:T(8,128)S(1)}, u32[]{:S(2)}, u32[]{:S(2)}) %collective-permute-start.60) | collective-permute-done | bytes 262176 | tf_op jit(solution)/shard_map/ppermute | solution.py:37
  274.5 3.7 %collective-permute-start.61 = (f32[4,128,256]{2,1,0:T(8,128)}, f32[4,128,256]{2,1,0:T(8,128)}, u32[]{:S(2)}, u32[]{:S(2)}) collective-permute-start(f32[4,128,256]{2,1,0:T(8,128)} %pad_maximum_fusion.3), channel_id=1, source_target_pairs={{0,80},{1,81},{2,82},{3,83},{4,84},{5,85},{6,86},{7,87},{8,88},{9,... | collective-permute-start | bytes 1572872 | tf_op jit(solution)/shard_map/ppermute | solution.py:37
  280.7 8.5 %collective-permute-done.61 = f32[4,128,256]{2,1,0:T(8,128)} collective-permute-done((f32[4,128,256]{2,1,0:T(8,128)}, f32[4,128,256]{2,1,0:T(8,128)}, u32[]{:S(2)}, u32[]{:S(2)}) %collective-permute-start.61) | collective-permute-done | bytes 524320 | tf_op jit(solution)/shard_map/ppermute | solution.py:37
  289.2 4.2 %collective-permute-done.59 = f32[4,128,256]{2,1,0:T(8,128)S(1)} collective-permute-done((f32[4,128,256]{2,1,0:T(8,128)}, f32[4,128,256]{2,1,0:T(8,128)S(1)}, u32[]{:S(2)}, u32[]{:S(2)}) %collective-permute-start.59) | collective-permute-done | bytes 524320 | tf_op jit(solution)/shard_map/ppermute | solution.py:37
  (179 shorter events, 102.7 us)
Async XLA Ops:
  1.9 15.2 %collective-permute-start.11 = (f32[4,128,256]{2,1,0:T(8,128)S(1)}, f32[4,128,256]{2,1,0:T(8,128)}, u32[]{:S(2)}, u32[]{:S(2)}) collective-permute-start(f32[4,128,256]{2,1,0:T(8,128)S(1)} %log.3), channel_id=1, source_target_pairs={{0,80},{1,81},{2,82},{3,83},{4,84},{5,85},{6,86},{7,87},{8,88},{9,... | collective-permute-start | bytes 1572872 | tf_op jit(solution)/shard_map/ppermute | solution.py:37
  4.8 16.2 %collective-permute-start.9 = (f32[4,128,256]{2,1,0:T(8,128)S(1)}, f32[4,128,256]{2,1,0:T(8,128)}, u32[]{:S(2)}, u32[]{:S(2)}) collective-permute-start(f32[4,128,256]{2,1,0:T(8,128)S(1)} %log.3), channel_id=1, source_target_pairs={{0,64},{1,65},{2,66},{3,67},{4,68},{5,69},{6,70},{7,71},{8,72},{9,... | collective-permute-start | bytes 1572872 | tf_op jit(solution)/shard_map/ppermute | solution.py:37
  8.9 21.8 %collective-permute-start.21 = (f32[4,128,256]{2,1,0:T(8,128)}, f32[4,128,256]{2,1,0:T(8,128)}, u32[]{:S(2)}, u32[]{:S(2)}) collective-permute-start(f32[4,128,256]{2,1,0:T(8,128)} %param.23), channel_id=1, source_target_pairs={{0,64},{1,65},{2,66},{3,67},{4,68},{5,69},{6,70},{7,71},{8,72},{9,... | collective-permute-start | bytes 1572872 | tf_op jit(solution)/shard_map/ppermute | solution.py:37
  9.7 21.0 %collective-permute-start.20 = (f32[4,128,256]{2,1,0:T(8,128)}, f32[4,128,256]{2,1,0:T(8,128)}, u32[]{:S(2)}, u32[]{:S(2)}) collective-permute-start(f32[4,128,256]{2,1,0:T(8,128)} %param.23), channel_id=1, source_target_pairs={{0,80},{1,81},{2,82},{3,83},{4,84},{5,85},{6,86},{7,87},{8,88},{9,... | collective-permute-start | bytes 1572872 | tf_op jit(solution)/shard_map/ppermute | solution.py:37
  12.2 30.0 %collective-permute-start.14 = (f32[4,176,256]{2,1,0:T(8,128)}, f32[4,176,256]{2,1,0:T(8,128)S(1)}, u32[]{:S(2)}, u32[]{:S(2)}) collective-permute-start(f32[4,176,256]{2,1,0:T(8,128)} %get-tuple-element.141), channel_id=1, source_target_pairs={{0,1},{1,2},{2,3},{3,0},{4,5},{5,6},{6,7},{7,4},{8,9},{9,10},{10,1... | collective-permute-start | bytes 2162696 | tf_op jit(solution)/shard_map/ppermute | solution.py:37
  17.1 31.5 %collective-permute-start.15 = (f32[4,176,256]{2,1,0:T(8,128)}, f32[4,176,256]{2,1,0:T(8,128)S(1)}, u32[]{:S(2)}, u32[]{:S(2)}) collective-permute-start(f32[4,176,256]{2,1,0:T(8,128)} %get-tuple-element.142), channel_id=1, source_target_pairs={{0,2},{1,3},{2,0},{3,1},{4,6},{5,7},{6,4},{7,5},{8,10},{9,11},{10,... | collective-permute-start | bytes 2162696 | tf_op jit(solution)/shard_map/ppermute | solution.py:37
  20.9 29.6 %collective-permute-start.16 = (f32[4,176,256]{2,1,0:T(8,128)}, f32[4,176,256]{2,1,0:T(8,128)S(1)}, u32[]{:S(2)}, u32[]{:S(2)}) collective-permute-start(f32[4,176,256]{2,1,0:T(8,128)} %get-tuple-element.143), channel_id=1, source_target_pairs={{0,3},{1,0},{2,1},{3,2},{4,7},{5,4},{6,5},{7,6},{8,11},{9,8},{10,9... | collective-permute-start | bytes 2162696 | tf_op jit(solution)/shard_map/ppermute | solution.py:37
  37.9 14.5 %collective-permute-start.22 = (f32[2,128,256]{2,1,0:T(8,128)S(1)}, f32[2,128,256]{2,1,0:T(8,128)S(1)}, u32[]{:S(2)}, u32[]{:S(2)}) collective-permute-start(f32[2,128,256]{2,1,0:T(8,128)S(1)} %slice.42), channel_id=1, source_target_pairs={{0,64},{1,65},{2,66},{3,67},{4,68},{5,69},{6,70},{7,71},{8,72},{9,... | collective-permute-start | bytes 786440 | tf_op jit(solution)/shard_map/ppermute | solution.py:37
  38.9 13.5 %collective-permute-start.23 = (f32[2,128,256]{2,1,0:T(8,128)S(1)}, f32[2,128,256]{2,1,0:T(8,128)S(1)}, u32[]{:S(2)}, u32[]{:S(2)}) collective-permute-start(f32[2,128,256]{2,1,0:T(8,128)S(1)} %slice.43), channel_id=1, source_target_pairs={{0,80},{1,81},{2,82},{3,83},{4,84},{5,85},{6,86},{7,87},{8,88},{9,... | collective-permute-start | bytes 786440 | tf_op jit(solution)/shard_map/ppermute | solution.py:37
  52.3 9.2 %collective-permute-start.19 = (f32[4,128,256]{2,1,0:T(8,128)S(1)}, f32[4,128,256]{2,1,0:T(8,128)S(1)}, u32[]{:S(2)}, u32[]{:S(2)}) collective-permute-start(f32[4,128,256]{2,1,0:T(8,128)S(1)} %select_select_fusion.2), channel_id=1, source_target_pairs={{0,32},{1,33},{2,34},{3,35},{4,36},{5,37},{6,38},{7,39},{8,40},{9,... | collective-permute-start | bytes 1572872 | tf_op jit(solution)/shard_map/ppermute | solution.py:37
  56.9 45.7 %collective-permute-start.17 = (f32[4,2,144,128]{3,2,1,0:T(8,128)}, f32[4,2,144,128]{3,2,1,0:T(8,128)}, u32[]{:S(2)}, u32[]{:S(2)}) collective-permute-start(f32[4,2,144,128]{3,2,1,0:T(8,128)} %get-tuple-element.151), channel_id=1, source_target_pairs={{0,4},{1,5},{2,6},{3,7},{4,8},{5,9},{6,10},{7,11},{8,12},{9,13},{1... | collective-permute-start | bytes 1769480 | tf_op jit(solution)/shard_map/ppermute | solution.py:37
  68.8 12.0 %collective-permute-start.26 = (f32[4,48,256]{2,1,0:T(8,128)S(1)}, f32[4,48,256]{2,1,0:T(8,128)S(1)}, u32[]{:S(2)}, u32[]{:S(2)}) collective-permute-start(f32[4,48,256]{2,1,0:T(8,128)S(1)} %get-tuple-element.167), channel_id=1, source_target_pairs={{0,2},{1,3},{2,0},{3,1},{4,6},{5,7},{6,4},{7,5},{8,10},{9,11},{10,... | collective-permute-start | bytes 589832 | tf_op jit(solution)/shard_map/ppermute | solution.py:37
  73.7 36.0 %collective-permute-start.18 = (f32[4,2,144,128]{3,2,1,0:T(8,128)}, f32[4,2,144,128]{3,2,1,0:T(8,128)}, u32[]{:S(2)}, u32[]{:S(2)}) collective-permute-start(f32[4,2,144,128]{3,2,1,0:T(8,128)} %copy-done.19), channel_id=1, source_target_pairs={{4,0},{5,1},{6,2},{7,3},{8,4},{9,5},{10,6},{11,7},{12,8},{13,9},{1... | collective-permute-start | bytes 1769480 | tf_op jit(solution)/shard_map/ppermute | solution.py:37
  82.8 11.9 %collective-permute-start.29 = (f32[4,48,256]{2,1,0:T(8,128)S(1)}, f32[4,48,256]{2,1,0:T(8,128)S(1)}, u32[]{:S(2)}, u32[]{:S(2)}) collective-permute-start(f32[4,48,256]{2,1,0:T(8,128)S(1)} %get-tuple-element.177), channel_id=1, source_target_pairs={{0,2},{1,3},{2,0},{3,1},{4,6},{5,7},{6,4},{7,5},{8,10},{9,11},{10,... | collective-permute-start | bytes 589832 | tf_op jit(solution)/shard_map/ppermute | solution.py:37
  85.7 10.3 %collective-permute-start.30 = (f32[4,48,256]{2,1,0:T(8,128)S(1)}, f32[4,48,256]{2,1,0:T(8,128)S(1)}, u32[]{:S(2)}, u32[]{:S(2)}) collective-permute-start(f32[4,48,256]{2,1,0:T(8,128)S(1)} %get-tuple-element.178), channel_id=1, source_target_pairs={{0,3},{1,0},{2,1},{3,2},{4,7},{5,4},{6,5},{7,6},{8,11},{9,8},{10,9... | collective-permute-start | bytes 589832 | tf_op jit(solution)/shard_map/ppermute | solution.py:37
  89.4 21.9 %collective-permute-start.31 = (f32[4,2,80,128]{3,2,1,0:T(8,128)}, f32[4,2,80,128]{3,2,1,0:T(8,128)S(1)}, u32[]{:S(2)}, u32[]{:S(2)}) collective-permute-start(f32[4,2,80,128]{3,2,1,0:T(8,128)} %get-tuple-element.180), channel_id=1, source_target_pairs={{0,4},{1,5},{2,6},{3,7},{4,8},{5,9},{6,10},{7,11},{8,12},{9,13},{1... | collective-permute-start | bytes 983048 | tf_op jit(solution)/shard_map/ppermute | solution.py:37
  94.7 16.7 %collective-permute-start.32 = (f32[4,2,80,128]{3,2,1,0:T(8,128)}, f32[4,2,80,128]{3,2,1,0:T(8,128)}, u32[]{:S(2)}, u32[]{:S(2)}) collective-permute-start(f32[4,2,80,128]{3,2,1,0:T(8,128)} %get-tuple-element.181), channel_id=1, source_target_pairs={{4,0},{5,1},{6,2},{7,3},{8,4},{9,5},{10,6},{11,7},{12,8},{13,9},{1... | collective-permute-start | bytes 983048 | tf_op jit(solution)/shard_map/ppermute | solution.py:37
  97.3 14.0 %collective-permute-start.33 = (f32[4,2,32,128]{3,2,1,0:T(8,128)}, f32[4,2,32,128]{3,2,1,0:T(8,128)}, u32[]{:S(2)}, u32[]{:S(2)}) collective-permute-start(f32[4,2,32,128]{3,2,1,0:T(8,128)} %get-tuple-element.182), channel_id=1, source_target_pairs={{0,4},{1,5},{2,6},{3,7},{4,8},{5,9},{6,10},{7,11},{8,12},{9,13},{1... | collective-permute-start | bytes 393224 | tf_op jit(solution)/shard_map/ppermute | solution.py:37
  127.9 9.6 %collective-permute-start.37 = (f32[16,2,8,128]{3,2,1,0:T(8,128)S(1)}, f32[16,2,8,128]{3,2,1,0:T(8,128)S(1)}, u32[]{:S(2)}, u32[]{:S(2)}) collective-permute-start(f32[16,2,8,128]{3,2,1,0:T(8,128)S(1)} %get-tuple-element.193), channel_id=1, source_target_pairs={{0,1},{1,2},{2,3},{4,5},{5,6},{6,7},{8,9},{9,10},{10,11},{12,13},{... | collective-permute-start | bytes 393224 | tf_op jit(solution)/shard_map/ppermute | solution.py:37
  149.8 12.3 %collective-permute-start.41 = (f32[8,2,32,128]{3,2,1,0:T(8,128)S(1)}, f32[8,2,32,128]{3,2,1,0:T(8,128)S(1)}, u32[]{:S(2)}, u32[]{:S(2)}) collective-permute-start(f32[8,2,32,128]{3,2,1,0:T(8,128)S(1)} %get-tuple-element.202), channel_id=1, source_target_pairs={{0,4},{1,5},{2,6},{3,7},{4,8},{5,9},{6,10},{7,11},{8,12},{9,13},{1... | collective-permute-start | bytes 786440 | tf_op jit(solution)/shard_map/ppermute | solution.py:37
  157.0 10.5 %collective-permute-start.42 = (f32[8,2,32,128]{3,2,1,0:T(8,128)S(1)}, f32[8,2,32,128]{3,2,1,0:T(8,128)S(1)}, u32[]{:S(2)}, u32[]{:S(2)}) collective-permute-start(f32[8,2,32,128]{3,2,1,0:T(8,128)S(1)} %get-tuple-element.203), channel_id=1, source_target_pairs={{4,0},{5,1},{6,2},{7,3},{8,4},{9,5},{10,6},{11,7},{12,8},{13,9},{1... | collective-permute-start | bytes 786440 | tf_op jit(solution)/shard_map/ppermute | solution.py:37
  158.3 13.1 %collective-permute-start.43 = (f32[16,2,8,128]{3,2,1,0:T(8,128)S(1)}, f32[16,2,8,128]{3,2,1,0:T(8,128)S(1)}, u32[]{:S(2)}, u32[]{:S(2)}) collective-permute-start(f32[16,2,8,128]{3,2,1,0:T(8,128)S(1)} %get-tuple-element.204), channel_id=1, source_target_pairs={{0,1},{1,2},{2,3},{4,5},{5,6},{6,7},{8,9},{9,10},{10,11},{12,13},{... | collective-permute-start | bytes 393224 | tf_op jit(solution)/shard_map/ppermute | solution.py:37
  160.8 10.7 %collective-permute-start.44 = (f32[16,2,8,128]{3,2,1,0:T(8,128)S(1)}, f32[16,2,8,128]{3,2,1,0:T(8,128)S(1)}, u32[]{:S(2)}, u32[]{:S(2)}) collective-permute-start(f32[16,2,8,128]{3,2,1,0:T(8,128)S(1)} %get-tuple-element.205), channel_id=1, source_target_pairs={{1,0},{2,1},{3,2},{5,4},{6,5},{7,6},{9,8},{10,9},{11,10},{13,12},{... | collective-permute-start | bytes 393224 | tf_op jit(solution)/shard_map/ppermute | solution.py:37
  181.5 13.8 %collective-permute-start.47 = (f32[4,2,32,128]{3,2,1,0:T(8,128)S(1)}, f32[4,2,32,128]{3,2,1,0:T(8,128)S(1)}, u32[]{:S(2)}, u32[]{:S(2)}) collective-permute-start(f32[4,2,32,128]{3,2,1,0:T(8,128)S(1)} %get-tuple-element.211), channel_id=1, source_target_pairs={{0,4},{1,5},{2,6},{3,7},{4,8},{5,9},{6,10},{7,11},{8,12},{9,13},{1... | collective-permute-start | bytes 393224 | tf_op jit(solution)/shard_map/ppermute | solution.py:37
  204.9 9.9 %collective-permute-start.51 = (f32[4,32,256]{2,1,0:T(8,128)S(1)}, f32[4,32,256]{2,1,0:T(8,128)S(1)}, u32[]{:S(2)}, u32[]{:S(2)}) collective-permute-start(f32[4,32,256]{2,1,0:T(8,128)S(1)} %get-tuple-element.220), channel_id=1, source_target_pairs={{0,1},{1,2},{2,3},{3,0},{4,5},{5,6},{6,7},{7,4},{8,9},{9,10},{10,1... | collective-permute-start | bytes 393224 | tf_op jit(solution)/shard_map/ppermute | solution.py:37
  205.4 9.5 %collective-permute-start.52 = (f32[4,32,256]{2,1,0:T(8,128)S(1)}, f32[4,32,256]{2,1,0:T(8,128)S(1)}, u32[]{:S(2)}, u32[]{:S(2)}) collective-permute-start(f32[4,32,256]{2,1,0:T(8,128)S(1)} %get-tuple-element.221), channel_id=1, source_target_pairs={{0,2},{1,3},{2,0},{3,1},{4,6},{5,7},{6,4},{7,5},{8,10},{9,11},{10,... | collective-permute-start | bytes 393224 | tf_op jit(solution)/shard_map/ppermute | solution.py:37
  205.4 9.8 %collective-permute-start.53 = (f32[4,32,256]{2,1,0:T(8,128)S(1)}, f32[4,32,256]{2,1,0:T(8,128)S(1)}, u32[]{:S(2)}, u32[]{:S(2)}) collective-permute-start(f32[4,32,256]{2,1,0:T(8,128)S(1)} %get-tuple-element.222), channel_id=1, source_target_pairs={{0,3},{1,0},{2,1},{3,2},{4,7},{5,4},{6,5},{7,6},{8,11},{9,8},{10,9... | collective-permute-start | bytes 393224 | tf_op jit(solution)/shard_map/ppermute | solution.py:37
  215.5 10.5 %collective-permute-start.55 = (f32[4,64,256]{2,1,0:T(8,128)S(1)}, f32[4,64,256]{2,1,0:T(8,128)S(1)}, u32[]{:S(2)}, u32[]{:S(2)}) collective-permute-start(f32[4,64,256]{2,1,0:T(8,128)S(1)} %get-tuple-element.233), channel_id=1, source_target_pairs={{0,2},{1,3},{2,0},{3,1},{4,6},{5,7},{6,4},{7,5},{8,10},{9,11},{10,... | collective-permute-start | bytes 786440 | tf_op jit(solution)/shard_map/ppermute | solution.py:37
  228.7 45.0 %collective-permute-start.60 = (f32[2,128,256]{2,1,0:T(8,128)S(1)}, f32[2,128,256]{2,1,0:T(8,128)S(1)}, u32[]{:S(2)}, u32[]{:S(2)}) collective-permute-start(f32[2,128,256]{2,1,0:T(8,128)S(1)} %get-tuple-element.248), channel_id=1, source_target_pairs={{0,80},{1,81},{2,82},{3,83},{4,84},{5,85},{6,86},{7,87},{8,88},{9,... | collective-permute-start | bytes 786440 | tf_op jit(solution)/shard_map/ppermute | solution.py:37
  267.7 10.5 %collective-permute-start.58 = (f32[2,128,256]{2,1,0:T(8,128)S(1)}, f32[2,128,256]{2,1,0:T(8,128)S(1)}, u32[]{:S(2)}, u32[]{:S(2)}) collective-permute-start(f32[2,128,256]{2,1,0:T(8,128)S(1)} %get-tuple-element.247), channel_id=1, source_target_pairs={{0,64},{1,65},{2,66},{3,67},{4,68},{5,69},{6,70},{7,71},{8,72},{9,... | collective-permute-start | bytes 786440 | tf_op jit(solution)/shard_map/ppermute | solution.py:37
  274.5 14.7 %collective-permute-start.61 = (f32[4,128,256]{2,1,0:T(8,128)}, f32[4,128,256]{2,1,0:T(8,128)}, u32[]{:S(2)}, u32[]{:S(2)}) collective-permute-start(f32[4,128,256]{2,1,0:T(8,128)} %pad_maximum_fusion.3), channel_id=1, source_target_pairs={{0,80},{1,81},{2,82},{3,83},{4,84},{5,85},{6,86},{7,87},{8,88},{9,... | collective-permute-start | bytes 1572872 | tf_op jit(solution)/shard_map/ppermute | solution.py:37
  279.1 14.3 %collective-permute-start.59 = (f32[4,128,256]{2,1,0:T(8,128)}, f32[4,128,256]{2,1,0:T(8,128)S(1)}, u32[]{:S(2)}, u32[]{:S(2)}) collective-permute-start(f32[4,128,256]{2,1,0:T(8,128)} %pad_maximum_fusion.2), channel_id=1, source_target_pairs={{0,64},{1,65},{2,66},{3,67},{4,68},{5,69},{6,70},{7,71},{8,72},{9,... | collective-permute-start | bytes 1572872 | tf_op jit(solution)/shard_map/ppermute | solution.py:37
  (49 other events, 406.4 us)

commit v3 on v0

--- a/solution.py
+++ b/solution.py
@@ -560,13 +560,18 @@
         (True, True, True, False),
         chunks_out,
     )
-    velocity, partner, *pieces = lax.optimization_barrier((velocity, partner, *pieces))
     pair_core, pair_step, _ = wanted(partner[0])
 
-    def gathered(slab):
+    def gathered(slab, *others):
         from_below = send_x(slab, 1)
         from_above = send_x(slab, -1)
-        far = jnp.concatenate([send_x(from_below[0:2], 1), send_x(from_above[2:4], -1)])
+        passing = from_below[0:2], from_above[2:4]
+        if others:
+            first, second, from_below, from_above, *others = lax.optimization_barrier(
+                (*passing, from_below, from_above, *others)
+            )
+            passing = first, second
+        far = jnp.concatenate([send_x(passing[0], 1), send_x(passing[1], -1)])
 
         def pick(step):
             return jnp.where(
@@ -574,7 +579,7 @@
             )
 
         other = send_core(pick(pair_step))
-        return jnp.where(own_core == core, pick(own_step), other)
+        return jnp.where(own_core == core, pick(own_step), other), *others
 
     def turned(arrays, steps):
         def branch(count):
@@ -582,8 +587,8 @@
 
         return lax.switch(steps, [branch(count) for count in (0, 1, 2, -1)], *arrays)
 
-    log_slab = gathered(jnp.log(density))
-    speed_slab = gathered(velocity)
+    log_slab, *pieces = gathered(jnp.log(density), *pieces)
+    (speed_slab,) = gathered(velocity)
     pieces = sent_pieces(pieces)
 
     def local_place(cells, rows_more, cells_more):

time: 276 us -> 263 us (0.953)
  starting transfers between devices: 116 us -> 99.1 us
  waiting for transfers between devices: 97.9 us -> 101 us
    ppermute x48, starting transfers between devices: 116 us -> 99.1 us  [send(): return lax.ppermute(value, ('shot', 'sub'), pairs_by(move))]
    ppermute x48, waiting for transfers between devices: 97.9 us -> 101 us  [send(): return lax.ppermute(value, ('shot', 'sub'), pairs_by(move))]
  transfers between devices with their start and end apart: 48 -> 48, of which waited for: 28 -> 25; matrix products, arithmetic and copies ran while one was open for 6% -> 7% of each run, Pallas kernels for 2% -> 3%
where the time goes in v3:
time: 263 us; the launch traced here: 261 us
  waiting for transfers between devices  101 us (38%)
  starting transfers between devices  99.1 us (38%)
  Pallas kernels  32.6 us (12%)
  local copies, waits for them, and re-layouts  9.76 us (4%)
  other arithmetic  9.37 us (4%)
  between operations  5.5 us (2%)
  matrix products  3.18 us (1%)
    ppermute x48, waiting for transfers between devices, send(): return lax.ppermute(value, ('shot', 'sub'), pairs_by(move))  101 us
    ppermute x48, starting transfers between devices, send(): return lax.ppermute(value, ('shot', 'sub'), pairs_by(move))  99.1 us
    pallas_call x14, Pallas kernels, call(): pl.pallas_call(body, out_shape=tuple(outs), in_specs=specs, out_specs=tup...  32.6 us
  transfers between devices with their start and end apart: 48, of which 25 were waited for; matrix products, arithmetic and copies ran while one was open for 7% of the time, Pallas kernels for 3%

profile of v3, /device:TPU:0, one launch (start us, length us, event | category | flops | bytes accessed | tf_op | source)
XLA Modules:
  0.0 261.2 jit_solution(4766818227680420902)
XLA Ops:
  8.6 8.4 %collective-permute-done.16 = f32[4,128,256]{2,1,0:T(8,128)S(1)} collective-permute-done((f32[4,128,256]{2,1,0:T(8,128)}, f32[4,128,256]{2,1,0:T(8,128)S(1)}, u32[]{:S(2)}, u32[]{:S(2)}) %collective-permute-start.16) | collective-permute-done | bytes 524320 | tf_op jit(solution)/shard_map/ppermute | solution.py:37
  35.4 2.9 %collective-permute-start.21 = (f32[4,176,256]{2,1,0:T(8,128)}, f32[4,176,256]{2,1,0:T(8,128)S(1)}, u32[]{:S(2)}, u32[]{:S(2)}) collective-permute-start(f32[4,176,256]{2,1,0:T(8,128)} %get-tuple-element.139), channel_id=1, source_target_pairs={{0,2},{1,3},{2,0},{3,1},{4,6},{5,7},{6,4},{7,5},{8,10},{9,11},{10,... | collective-permute-start | bytes 2162696 | tf_op jit(solution)/shard_map/ppermute | solution.py:37
  49.4 3.8 %collective-permute-done.20.refs_1_ = f32[4,176,256]{2,1,0:T(8,128)S(1)} collective-permute-done((f32[4,176,256]{2,1,0:T(8,128)}, f32[4,176,256]{2,1,0:T(8,128)S(1)}, u32[]{:S(2)}, u32[]{:S(2)}) %collective-permute-start.20) | collective-permute-done | bytes 720928 | tf_op jit(solution)/shard_map/ppermute | solution.py:37
  53.2 13.5 %collective-permute-done.21.refs_2_ = f32[4,176,256]{2,1,0:T(8,128)S(1)} collective-permute-done((f32[4,176,256]{2,1,0:T(8,128)}, f32[4,176,256]{2,1,0:T(8,128)S(1)}, u32[]{:S(2)}, u32[]{:S(2)}) %collective-permute-start.21) | collective-permute-done | bytes 720928 | tf_op jit(solution)/shard_map/ppermute | solution.py:37
  75.9 3.9 %collective-permute-start.23 = (f32[4,2,144,128]{3,2,1,0:T(8,128)S(1)}, f32[4,2,144,128]{3,2,1,0:T(8,128)S(1)}, u32[]{:S(2)}, u32[]{:S(2)}) collective-permute-start(f32[4,2,144,128]{3,2,1,0:T(8,128)S(1)} %get-tuple-element.148), channel_id=1, source_target_pairs={{0,4},{1,5},{2,6},{3,7},{4,8},{5,9},{6,10},{7,11},{8,12},{9,13},{1... | collective-permute-start | bytes 1769480 | tf_op jit(solution)/shard_map/ppermute | solution.py:37
  82.0 9.6 %collective-permute-done.26.refs_2_ = f32[4,96,256]{2,1,0:T(8,128)} collective-permute-done((f32[4,96,256]{2,1,0:T(8,128)}, f32[4,96,256]{2,1,0:T(8,128)}, u32[]{:S(2)}, u32[]{:S(2)}) %collective-permute-start.26) | collective-permute-done | bytes 393248 | tf_op jit(solution)/shard_map/ppermute | solution.py:37
  93.0 3.8 %collective-permute-start.28 = (f32[4,2,112,128]{3,2,1,0:T(8,128)S(1)}, f32[4,2,112,128]{3,2,1,0:T(8,128)S(1)}, u32[]{:S(2)}, u32[]{:S(2)}) collective-permute-start(f32[4,2,112,128]{3,2,1,0:T(8,128)S(1)} %get-tuple-element.160), channel_id=1, source_target_pairs={{0,4},{1,5},{2,6},{3,7},{4,8},{5,9},{6,10},{7,11},{8,12},{9,13},{1... | collective-permute-start | bytes 1376264 | tf_op jit(solution)/shard_map/ppermute | solution.py:37
  98.3 3.2 %fusion.refs_13_.refs_11_.maps = f32[24,2,48,640]{3,2,1,0:T(8,128)S(1)} fusion(f32[256,640,1,1]{0,1,3,2:T(8,128)S(1)} %bitcast.41, s32[256]{0:T(256)S(1)} %bitcast.44, s32[24,2,48]{2,1,0:T(2,128)S(1)} %multiply_add_fusion), kind=kOutput, calls=%fused_computation | convolution fusion | flops 4530438144 | bytes 6563840 | tf_op jit(solution)/shard_map/dot_general | solution.py:608
  101.8 4.1 %collective-permute-done.28.below = f32[4,2,112,128]{3,2,1,0:T(8,128)S(1)} collective-permute-done((f32[4,2,112,128]{3,2,1,0:T(8,128)S(1)}, f32[4,2,112,128]{3,2,1,0:T(8,128)S(1)}, u32[]{:S(2)}, u32[]{:S(2)}) %collective-permute-start.28) | collective-permute-done | bytes 458784 | tf_op jit(solution)/shard_map/ppermute | solution.py:37
  105.9 4.3 %collective-permute-done.29.above = f32[4,2,112,128]{3,2,1,0:T(8,128)S(1)} collective-permute-done((f32[4,2,112,128]{3,2,1,0:T(8,128)S(1)}, f32[4,2,112,128]{3,2,1,0:T(8,128)S(1)}, u32[]{:S(2)}, u32[]{:S(2)}) %collective-permute-start.29) | collective-permute-done | bytes 458784 | tf_op jit(solution)/shard_map/ppermute | solution.py:37
  110.2 2.9 %shard_map.135 = (f32[24,2,48,128]{3,2,1,0:T(8,128)S(1)}, f32[24,2,48,128]{3,2,1,0:T(8,128)S(1)}, f32[24,2,48,128]{3,2,1,0:T(8,128)S(1)}, f32[24,2,48,128]{3,2,1,0:T(8,128)S(1)}, f32[16,2,32,128]{3,2,1,0:T(8,128)S(1)}) custom-call(f32[16,2,48,128]{3,2,1,0:T(8,128)S(1)} %get-tuple-element.158.log_mass, f32[16,2,48,128]{3,2,1,0:T(8,128)S(1)} %get-tuple-element.159.speed, ...), custom_call_target="tpu_custom_call" | custom-call | tf_op jit(solution)/shard_map/pallas_call | solution.py:91
  113.2 5.4 %shard_map.136 = (f32[24,2,48,128]{3,2,1,0:T(8,128)S(1)}, f32[16,2,32,128]{3,2,1,0:T(8,128)S(1)}, f32[8,2,32,128]{3,2,1,0:T(8,128)S(1)}, f32[8,2,32,128]{3,2,1,0...) custom-call(s32[10]{0:T(128)S(1)} %stack.45.place, f32[4]{0:T(128)S(1)} %bitcast.39, ...), custom_call_target="tpu_custom_call" | custom-call | tf_op jit(solution)/shard_map/pallas_call | solution.py:91
  118.6 3.7 %collective-permute-start.30 = (f32[8,2,32,128]{3,2,1,0:T(8,128)S(1)}, f32[8,2,32,128]{3,2,1,0:T(8,128)S(1)}, u32[]{:S(2)}, u32[]{:S(2)}) collective-permute-start(f32[8,2,32,128]{3,2,1,0:T(8,128)S(1)} %get-tuple-element.169), channel_id=1, source_target_pairs={{0,4},{1,5},{2,6},{3,7},{4,8},{5,9},{6,10},{7,11},{8,12},{9,13},{1... | collective-permute-start | bytes 786440 | tf_op jit(solution)/shard_map/ppermute | solution.py:37
  123.5 3.4 %collective-permute-start.32 = (f32[16,2,8,128]{3,2,1,0:T(8,128)S(1)}, f32[16,2,8,128]{3,2,1,0:T(8,128)S(1)}, u32[]{:S(2)}, u32[]{:S(2)}) collective-permute-start(f32[16,2,8,128]{3,2,1,0:T(8,128)S(1)} %get-tuple-element.171), channel_id=1, source_target_pairs={{0,1},{1,2},{2,3},{4,5},{5,6},{6,7},{8,9},{9,10},{10,11},{12,13},{... | collective-permute-start | bytes 393224 | tf_op jit(solution)/shard_map/ppermute | solution.py:37
  130.5 3.8 %collective-permute-start.34 = (f32[8,2,8,128]{3,2,1,0:T(8,128)S(1)}, f32[8,2,8,128]{3,2,1,0:T(8,128)S(1)}, u32[]{:S(2)}, u32[]{:S(2)}) collective-permute-start(f32[8,2,8,128]{3,2,1,0:T(8,128)S(1)} %get-tuple-element.173), channel_id=1, source_target_pairs={{0,1},{1,2},{2,3},{4,5},{5,6},{6,7},{8,9},{9,10},{10,11},{12,13},{... | collective-permute-start | bytes 196616 | tf_op jit(solution)/shard_map/ppermute | solution.py:37
  136.2 4.3 %collective-permute-done.35.refs_5_ = f32[8,2,8,128]{3,2,1,0:T(8,128)S(1)} collective-permute-done((f32[8,2,8,128]{3,2,1,0:T(8,128)S(1)}, f32[8,2,8,128]{3,2,1,0:T(8,128)S(1)}, u32[]{:S(2)}, u32[]{:S(2)}) %collective-permute-start.35) | collective-permute-done | bytes 65568 | tf_op jit(solution)/shard_map/ppermute | solution.py:37
  140.5 7.4 %shard_map.138 = (f32[24,2,48,128]{3,2,1,0:T(8,128)S(1)}, f32[16,2,32,128]{3,2,1,0:T(8,128)S(1)}, f32[16,2,32,128]{3,2,1,0:T(8,128)S(1)}, f32[16,2,32,128]{3,2,1...) custom-call(s32[10]{0:T(128)S(1)} %stack.45.place, ...), custom_call_target="tpu_custom_call" | custom-call | tf_op jit(solution)/shard_map/pallas_call | solution.py:91
  147.9 5.9 %collective-permute-start.36 = (f32[8,2,32,128]{3,2,1,0:T(8,128)S(1)}, f32[8,2,32,128]{3,2,1,0:T(8,128)S(1)}, u32[]{:S(2)}, u32[]{:S(2)}) collective-permute-start(f32[8,2,32,128]{3,2,1,0:T(8,128)S(1)} %get-tuple-element.180), channel_id=1, source_target_pairs={{0,4},{1,5},{2,6},{3,7},{4,8},{5,9},{6,10},{7,11},{8,12},{9,13},{1... | collective-permute-start | bytes 786440 | tf_op jit(solution)/shard_map/ppermute | solution.py:37
  166.7 4.3 %collective-permute-done.41.refs_5_ = f32[8,2,8,128]{3,2,1,0:T(8,128)S(1)} collective-permute-done((f32[8,2,8,128]{3,2,1,0:T(8,128)S(1)}, f32[8,2,8,128]{3,2,1,0:T(8,128)S(1)}, u32[]{:S(2)}, u32[]{:S(2)}) %collective-permute-start.41) | collective-permute-done | bytes 65568 | tf_op jit(solution)/shard_map/ppermute | solution.py:37
  171.0 5.2 %shard_map.140 = (f32[24,2,48,128]{3,2,1,0:T(8,128)S(1)}, f32[16,2,32,128]{3,2,1,0:T(8,128)S(1)}, f32[16,2,32,128]{3,2,1,0:T(8,128)S(1)}, f32[4,2,32,128]{3,2,1,...) custom-call(f32[16,2,32,128]{3,2,1,0:T(8,128)S(1)} %get-tuple-element.17, ...), custom_call_target="tpu_custom_call" | custom-call | tf_op jit(solution)/shard_map/pallas_call | solution.py:91
  176.2 5.5 %collective-permute-start.42 = (f32[4,2,32,128]{3,2,1,0:T(8,128)S(1)}, f32[4,2,32,128]{3,2,1,0:T(8,128)S(1)}, u32[]{:S(2)}, u32[]{:S(2)}) collective-permute-start(f32[4,2,32,128]{3,2,1,0:T(8,128)S(1)} %get-tuple-element.189), channel_id=1, source_target_pairs={{0,4},{1,5},{2,6},{3,7},{4,8},{5,9},{6,10},{7,11},{8,12},{9,13},{1... | collective-permute-start | bytes 393224 | tf_op jit(solution)/shard_map/ppermute | solution.py:37
  183.1 3.9 %collective-permute-start.44 = (f32[16,2,8,128]{3,2,1,0:T(8,128)S(1)}, f32[16,2,8,128]{3,2,1,0:T(8,128)S(1)}, u32[]{:S(2)}, u32[]{:S(2)}) collective-permute-start(f32[16,2,8,128]{3,2,1,0:T(8,128)S(1)} %get-tuple-element.191), channel_id=1, source_target_pairs={{0,1},{1,2},{2,3},{4,5},{5,6},{6,7},{8,9},{9,10},{10,11},{12,13},{... | collective-permute-start | bytes 393224 | tf_op jit(solution)/shard_map/ppermute | solution.py:37
  189.7 4.9 %collective-permute-done.45.right = f32[16,2,8,128]{3,2,1,0:T(8,128)S(1)} collective-permute-done((f32[16,2,8,128]{3,2,1,0:T(8,128)S(1)}, f32[16,2,8,128]{3,2,1,0:T(8,128)S(1)}, u32[]{:S(2)}, u32[]{:S(2)}) %collective-permute-start.45) | collective-permute-done | bytes 131104 | tf_op jit(solution)/shard_map/ppermute | solution.py:37
  201.0 7.7 %collective-permute-done.46.p1 = f32[4,32,256]{2,1,0:T(8,128)S(1)} collective-permute-done((f32[4,32,256]{2,1,0:T(8,128)S(1)}, f32[4,32,256]{2,1,0:T(8,128)S(1)}, u32[]{:S(2)}, u32[]{:S(2)}) %collective-permute-start.46) | collective-permute-done | bytes 131104 | tf_op jit(solution)/shard_map/ppermute | solution.py:37
  208.7 3.5 %collective-permute-start.50 = (f32[4,64,256]{2,1,0:T(8,128)S(1)}, f32[4,64,256]{2,1,0:T(8,128)S(1)}, u32[]{:S(2)}, u32[]{:S(2)}) collective-permute-start(f32[4,64,256]{2,1,0:T(8,128)S(1)} %get-tuple-element.211), channel_id=1, source_target_pairs={{0,2},{1,3},{2,0},{3,1},{4,6},{5,7},{6,4},{7,5},{8,10},{9,11},{10,... | collective-permute-start | bytes 786440 | tf_op jit(solution)/shard_map/ppermute | solution.py:37
  213.2 3.1 %collective-permute-done.49.p1 = f32[4,64,256]{2,1,0:T(8,128)S(1)} collective-permute-done((f32[4,64,256]{2,1,0:T(8,128)S(1)}, f32[4,64,256]{2,1,0:T(8,128)S(1)}, u32[]{:S(2)}, u32[]{:S(2)}) %collective-permute-start.49) | collective-permute-done | bytes 262176 | tf_op jit(solution)/shard_map/ppermute | solution.py:37
  216.3 3.0 %collective-permute-done.50.p2 = f32[4,64,256]{2,1,0:T(8,128)S(1)} collective-permute-done((f32[4,64,256]{2,1,0:T(8,128)S(1)}, f32[4,64,256]{2,1,0:T(8,128)S(1)}, u32[]{:S(2)}, u32[]{:S(2)}) %collective-permute-start.50) | collective-permute-done | bytes 262176 | tf_op jit(solution)/shard_map/ppermute | solution.py:37
  222.2 12.5 %collective-permute-start.55 = (f32[2,128,256]{2,1,0:T(8,128)S(1)}, f32[2,128,256]{2,1,0:T(8,128)S(1)}, u32[]{:S(2)}, u32[]{:S(2)}) collective-permute-start(f32[2,128,256]{2,1,0:T(8,128)S(1)} %get-tuple-element.226), channel_id=1, source_target_pairs={{0,80},{1,81},{2,82},{3,83},{4,84},{5,85},{6,86},{7,87},{8,88},{9,... | collective-permute-start | bytes 786440 | tf_op jit(solution)/shard_map/ppermute | solution.py:37
  234.7 5.9 %collective-permute-done.55 = f32[2,128,256]{2,1,0:T(8,128)S(1)} collective-permute-done((f32[2,128,256]{2,1,0:T(8,128)S(1)}, f32[2,128,256]{2,1,0:T(8,128)S(1)}, u32[]{:S(2)}, u32[]{:S(2)}) %collective-permute-start.55) | collective-permute-done | bytes 262176 | tf_op jit(solution)/shard_map/ppermute | solution.py:37
  241.4 3.7 %collective-permute-start.56 = (f32[4,128,256]{2,1,0:T(8,128)}, f32[4,128,256]{2,1,0:T(8,128)S(1)}, u32[]{:S(2)}, u32[]{:S(2)}) collective-permute-start(f32[4,128,256]{2,1,0:T(8,128)} %pad_maximum_fusion.1), channel_id=1, source_target_pairs={{0,80},{1,81},{2,82},{3,83},{4,84},{5,85},{6,86},{7,87},{8,88},{9,... | collective-permute-start | bytes 1572872 | tf_op jit(solution)/shard_map/ppermute | solution.py:37
  247.6 8.5 %collective-permute-done.56 = f32[4,128,256]{2,1,0:T(8,128)S(1)} collective-permute-done((f32[4,128,256]{2,1,0:T(8,128)}, f32[4,128,256]{2,1,0:T(8,128)S(1)}, u32[]{:S(2)}, u32[]{:S(2)}) %collective-permute-start.56) | collective-permute-done | bytes 524320 | tf_op jit(solution)/shard_map/ppermute | solution.py:37
  256.1 4.2 %collective-permute-done.54 = f32[4,128,256]{2,1,0:T(8,128)S(1)} collective-permute-done((f32[4,128,256]{2,1,0:T(8,128)}, f32[4,128,256]{2,1,0:T(8,128)S(1)}, u32[]{:S(2)}, u32[]{:S(2)}) %collective-permute-start.54) | collective-permute-done | bytes 524320 | tf_op jit(solution)/shard_map/ppermute | solution.py:37
  (133 shorter events, 85.6 us)
Async XLA Ops:
  0.7 16.3 %collective-permute-start.16 = (f32[4,128,256]{2,1,0:T(8,128)}, f32[4,128,256]{2,1,0:T(8,128)S(1)}, u32[]{:S(2)}, u32[]{:S(2)}) collective-permute-start(f32[4,128,256]{2,1,0:T(8,128)} %param.19), channel_id=1, source_target_pairs={{0,64},{1,65},{2,66},{3,67},{4,68},{5,69},{6,70},{7,71},{8,72},{9,... | collective-permute-start | bytes 1572872 | tf_op jit(solution)/shard_map/ppermute | solution.py:37
  2.3 19.7 %collective-permute-start.15 = (f32[4,128,256]{2,1,0:T(8,128)}, f32[4,128,256]{2,1,0:T(8,128)}, u32[]{:S(2)}, u32[]{:S(2)}) collective-permute-start(f32[4,128,256]{2,1,0:T(8,128)} %param.19), channel_id=1, source_target_pairs={{0,80},{1,81},{2,82},{3,83},{4,84},{5,85},{6,86},{7,87},{8,88},{9,... | collective-permute-start | bytes 1572872 | tf_op jit(solution)/shard_map/ppermute | solution.py:37
  5.9 23.4 %collective-permute-start.10 = (f32[4,128,256]{2,1,0:T(8,128)}, f32[4,128,256]{2,1,0:T(8,128)S(1)}, u32[]{:S(2)}, u32[]{:S(2)}) collective-permute-start(f32[4,128,256]{2,1,0:T(8,128)} %log.3), channel_id=1, source_target_pairs={{0,80},{1,81},{2,82},{3,83},{4,84},{5,85},{6,86},{7,87},{8,88},{9,... | collective-permute-start | bytes 1572872 | tf_op jit(solution)/shard_map/ppermute | solution.py:37
  7.5 21.8 %collective-permute-start.9 = (f32[4,128,256]{2,1,0:T(8,128)}, f32[4,128,256]{2,1,0:T(8,128)}, u32[]{:S(2)}, u32[]{:S(2)}) collective-permute-start(f32[4,128,256]{2,1,0:T(8,128)} %log.3), channel_id=1, source_target_pairs={{0,64},{1,65},{2,66},{3,67},{4,68},{5,69},{6,70},{7,71},{8,72},{9,... | collective-permute-start | bytes 1572872 | tf_op jit(solution)/shard_map/ppermute | solution.py:37
  7.9 18.7 %collective-permute-start.13 = (s32[1]{0:T(128)}, s32[1]{0:T(128)}, u32[]{:S(2)}, u32[]{:S(2)}) collective-permute-start(s32[1]{0:T(128)} %param.21), channel_id=1, source_target_pairs={{0,32},{1,33},{2,34},{3,35},{4,36},{5,37},{6,38},{7,39},{8,40},{9,... | collective-permute-start | bytes 20 | tf_op jit(solution)/shard_map/ppermute | solution.py:37
  17.7 17.7 %collective-permute-start.17 = (f32[2,128,256]{2,1,0:T(8,128)}, f32[2,128,256]{2,1,0:T(8,128)}, u32[]{:S(2)}, u32[]{:S(2)}) collective-permute-start(f32[2,128,256]{2,1,0:T(8,128)} %slice.42), channel_id=1, source_target_pairs={{0,64},{1,65},{2,66},{3,67},{4,68},{5,69},{6,70},{7,71},{8,72},{9,... | collective-permute-start | bytes 786440 | tf_op jit(solution)/shard_map/ppermute | solution.py:37
  23.7 15.6 %collective-permute-start.18 = (f32[2,128,256]{2,1,0:T(8,128)}, f32[2,128,256]{2,1,0:T(8,128)}, u32[]{:S(2)}, u32[]{:S(2)}) collective-permute-start(f32[2,128,256]{2,1,0:T(8,128)} %slice.43), channel_id=1, source_target_pairs={{0,80},{1,81},{2,82},{3,83},{4,84},{5,85},{6,86},{7,87},{8,88},{9,... | collective-permute-start | bytes 786440 | tf_op jit(solution)/shard_map/ppermute | solution.py:37
  30.4 12.6 %collective-permute-start.11 = (f32[2,128,256]{2,1,0:T(8,128)S(1)}, f32[2,128,256]{2,1,0:T(8,128)S(1)}, u32[]{:S(2)}, u32[]{:S(2)}) collective-permute-start(f32[2,128,256]{2,1,0:T(8,128)S(1)} %slice.40), channel_id=1, source_target_pairs={{0,64},{1,65},{2,66},{3,67},{4,68},{5,69},{6,70},{7,71},{8,72},{9,... | collective-permute-start | bytes 786440 | tf_op jit(solution)/shard_map/ppermute | solution.py:37
  31.3 11.8 %collective-permute-start.12 = (f32[2,128,256]{2,1,0:T(8,128)S(1)}, f32[2,128,256]{2,1,0:T(8,128)S(1)}, u32[]{:S(2)}, u32[]{:S(2)}) collective-permute-start(f32[2,128,256]{2,1,0:T(8,128)S(1)} %slice.41), channel_id=1, source_target_pairs={{0,80},{1,81},{2,82},{3,83},{4,84},{5,85},{6,86},{7,87},{8,88},{9,... | collective-permute-start | bytes 786440 | tf_op jit(solution)/shard_map/ppermute | solution.py:37
  33.7 19.4 %collective-permute-start.20 = (f32[4,176,256]{2,1,0:T(8,128)}, f32[4,176,256]{2,1,0:T(8,128)S(1)}, u32[]{:S(2)}, u32[]{:S(2)}) collective-permute-start(f32[4,176,256]{2,1,0:T(8,128)} %get-tuple-element.138), channel_id=1, source_target_pairs={{0,1},{1,2},{2,3},{3,0},{4,5},{5,6},{6,7},{7,4},{8,9},{9,10},{10,1... | collective-permute-start | bytes 2162696 | tf_op jit(solution)/shard_map/ppermute | solution.py:37
  35.4 31.3 %collective-permute-start.21 = (f32[4,176,256]{2,1,0:T(8,128)}, f32[4,176,256]{2,1,0:T(8,128)S(1)}, u32[]{:S(2)}, u32[]{:S(2)}) collective-permute-start(f32[4,176,256]{2,1,0:T(8,128)} %get-tuple-element.139), channel_id=1, source_target_pairs={{0,2},{1,3},{2,0},{3,1},{4,6},{5,7},{6,4},{7,5},{8,10},{9,11},{10,... | collective-permute-start | bytes 2162696 | tf_op jit(solution)/shard_map/ppermute | solution.py:37
  39.3 28.1 %collective-permute-start.22 = (f32[4,176,256]{2,1,0:T(8,128)}, f32[4,176,256]{2,1,0:T(8,128)S(1)}, u32[]{:S(2)}, u32[]{:S(2)}) collective-permute-start(f32[4,176,256]{2,1,0:T(8,128)} %get-tuple-element.140), channel_id=1, source_target_pairs={{0,3},{1,0},{2,1},{3,2},{4,7},{5,4},{6,5},{7,6},{8,11},{9,8},{10,9... | collective-permute-start | bytes 2162696 | tf_op jit(solution)/shard_map/ppermute | solution.py:37
  69.7 12.2 %collective-permute-start.25 = (f32[4,96,256]{2,1,0:T(8,128)}, f32[4,96,256]{2,1,0:T(8,128)}, u32[]{:S(2)}, u32[]{:S(2)}) collective-permute-start(f32[4,96,256]{2,1,0:T(8,128)} %get-tuple-element.155), channel_id=1, source_target_pairs={{0,1},{1,2},{2,3},{3,0},{4,5},{5,6},{6,7},{7,4},{8,9},{9,10},{10,1... | collective-permute-start | bytes 1179656 | tf_op jit(solution)/shard_map/ppermute | solution.py:37
  70.9 20.7 %collective-permute-start.26 = (f32[4,96,256]{2,1,0:T(8,128)}, f32[4,96,256]{2,1,0:T(8,128)}, u32[]{:S(2)}, u32[]{:S(2)}) collective-permute-start(f32[4,96,256]{2,1,0:T(8,128)} %get-tuple-element.156), channel_id=1, source_target_pairs={{0,2},{1,3},{2,0},{3,1},{4,6},{5,7},{6,4},{7,5},{8,10},{9,11},{10,... | collective-permute-start | bytes 1179656 | tf_op jit(solution)/shard_map/ppermute | solution.py:37
  73.8 17.8 %collective-permute-start.27 = (f32[4,96,256]{2,1,0:T(8,128)}, f32[4,96,256]{2,1,0:T(8,128)}, u32[]{:S(2)}, u32[]{:S(2)}) collective-permute-start(f32[4,96,256]{2,1,0:T(8,128)} %get-tuple-element.157), channel_id=1, source_target_pairs={{0,3},{1,0},{2,1},{3,2},{4,7},{5,4},{6,5},{7,6},{8,11},{9,8},{10,9... | collective-permute-start | bytes 1179656 | tf_op jit(solution)/shard_map/ppermute | solution.py:37
  75.9 25.6 %collective-permute-start.23 = (f32[4,2,144,128]{3,2,1,0:T(8,128)S(1)}, f32[4,2,144,128]{3,2,1,0:T(8,128)S(1)}, u32[]{:S(2)}, u32[]{:S(2)}) collective-permute-start(f32[4,2,144,128]{3,2,1,0:T(8,128)S(1)} %get-tuple-element.148), channel_id=1, source_target_pairs={{0,4},{1,5},{2,6},{3,7},{4,8},{5,9},{6,10},{7,11},{8,12},{9,13},{1... | collective-permute-start | bytes 1769480 | tf_op jit(solution)/shard_map/ppermute | solution.py:37
  79.8 21.7 %collective-permute-start.24 = (f32[4,2,144,128]{3,2,1,0:T(8,128)S(1)}, f32[4,2,144,128]{3,2,1,0:T(8,128)S(1)}, u32[]{:S(2)}, u32[]{:S(2)}) collective-permute-start(f32[4,2,144,128]{3,2,1,0:T(8,128)S(1)} %get-tuple-element.149), channel_id=1, source_target_pairs={{4,0},{5,1},{6,2},{7,3},{8,4},{9,5},{10,6},{11,7},{12,8},{13,9},{1... | collective-permute-start | bytes 1769480 | tf_op jit(solution)/shard_map/ppermute | solution.py:37
  93.0 12.9 %collective-permute-start.28 = (f32[4,2,112,128]{3,2,1,0:T(8,128)S(1)}, f32[4,2,112,128]{3,2,1,0:T(8,128)S(1)}, u32[]{:S(2)}, u32[]{:S(2)}) collective-permute-start(f32[4,2,112,128]{3,2,1,0:T(8,128)S(1)} %get-tuple-element.160), channel_id=1, source_target_pairs={{0,4},{1,5},{2,6},{3,7},{4,8},{5,9},{6,10},{7,11},{8,12},{9,13},{1... | collective-permute-start | bytes 1376264 | tf_op jit(solution)/shard_map/ppermute | solution.py:37
  96.8 13.4 %collective-permute-start.29 = (f32[4,2,112,128]{3,2,1,0:T(8,128)S(1)}, f32[4,2,112,128]{3,2,1,0:T(8,128)S(1)}, u32[]{:S(2)}, u32[]{:S(2)}) collective-permute-start(f32[4,2,112,128]{3,2,1,0:T(8,128)S(1)} %get-tuple-element.161), channel_id=1, source_target_pairs={{4,0},{5,1},{6,2},{7,3},{8,4},{9,5},{10,6},{11,7},{12,8},{13,9},{1... | collective-permute-start | bytes 1376264 | tf_op jit(solution)/shard_map/ppermute | solution.py:37
  118.6 9.7 %collective-permute-start.30 = (f32[8,2,32,128]{3,2,1,0:T(8,128)S(1)}, f32[8,2,32,128]{3,2,1,0:T(8,128)S(1)}, u32[]{:S(2)}, u32[]{:S(2)}) collective-permute-start(f32[8,2,32,128]{3,2,1,0:T(8,128)S(1)} %get-tuple-element.169), channel_id=1, source_target_pairs={{0,4},{1,5},{2,6},{3,7},{4,8},{5,9},{6,10},{7,11},{8,12},{9,13},{1... | collective-permute-start | bytes 786440 | tf_op jit(solution)/shard_map/ppermute | solution.py:37
  123.5 12.1 %collective-permute-start.32 = (f32[16,2,8,128]{3,2,1,0:T(8,128)S(1)}, f32[16,2,8,128]{3,2,1,0:T(8,128)S(1)}, u32[]{:S(2)}, u32[]{:S(2)}) collective-permute-start(f32[16,2,8,128]{3,2,1,0:T(8,128)S(1)} %get-tuple-element.171), channel_id=1, source_target_pairs={{0,1},{1,2},{2,3},{4,5},{5,6},{6,7},{8,9},{9,10},{10,11},{12,13},{... | collective-permute-start | bytes 393224 | tf_op jit(solution)/shard_map/ppermute | solution.py:37
  147.9 11.2 %collective-permute-start.36 = (f32[8,2,32,128]{3,2,1,0:T(8,128)S(1)}, f32[8,2,32,128]{3,2,1,0:T(8,128)S(1)}, u32[]{:S(2)}, u32[]{:S(2)}) collective-permute-start(f32[8,2,32,128]{3,2,1,0:T(8,128)S(1)} %get-tuple-element.180), channel_id=1, source_target_pairs={{0,4},{1,5},{2,6},{3,7},{4,8},{5,9},{6,10},{7,11},{8,12},{9,13},{1... | collective-permute-start | bytes 786440 | tf_op jit(solution)/shard_map/ppermute | solution.py:37
  155.1 11.0 %collective-permute-start.38 = (f32[16,2,8,128]{3,2,1,0:T(8,128)S(1)}, f32[16,2,8,128]{3,2,1,0:T(8,128)S(1)}, u32[]{:S(2)}, u32[]{:S(2)}) collective-permute-start(f32[16,2,8,128]{3,2,1,0:T(8,128)S(1)} %get-tuple-element.182), channel_id=1, source_target_pairs={{0,1},{1,2},{2,3},{4,5},{5,6},{6,7},{8,9},{9,10},{10,11},{12,13},{... | collective-permute-start | bytes 393224 | tf_op jit(solution)/shard_map/ppermute | solution.py:37
  176.2 12.1 %collective-permute-start.42 = (f32[4,2,32,128]{3,2,1,0:T(8,128)S(1)}, f32[4,2,32,128]{3,2,1,0:T(8,128)S(1)}, u32[]{:S(2)}, u32[]{:S(2)}) collective-permute-start(f32[4,2,32,128]{3,2,1,0:T(8,128)S(1)} %get-tuple-element.189), channel_id=1, source_target_pairs={{0,4},{1,5},{2,6},{3,7},{4,8},{5,9},{6,10},{7,11},{8,12},{9,13},{1... | collective-permute-start | bytes 393224 | tf_op jit(solution)/shard_map/ppermute | solution.py:37
  197.3 11.5 %collective-permute-start.46 = (f32[4,32,256]{2,1,0:T(8,128)S(1)}, f32[4,32,256]{2,1,0:T(8,128)S(1)}, u32[]{:S(2)}, u32[]{:S(2)}) collective-permute-start(f32[4,32,256]{2,1,0:T(8,128)S(1)} %get-tuple-element.198), channel_id=1, source_target_pairs={{0,1},{1,2},{2,3},{3,0},{4,5},{5,6},{6,7},{7,4},{8,9},{9,10},{10,1... | collective-permute-start | bytes 393224 | tf_op jit(solution)/shard_map/ppermute | solution.py:37
  198.3 10.5 %collective-permute-start.47 = (f32[4,32,256]{2,1,0:T(8,128)S(1)}, f32[4,32,256]{2,1,0:T(8,128)S(1)}, u32[]{:S(2)}, u32[]{:S(2)}) collective-permute-start(f32[4,32,256]{2,1,0:T(8,128)S(1)} %get-tuple-element.199), channel_id=1, source_target_pairs={{0,2},{1,3},{2,0},{3,1},{4,6},{5,7},{6,4},{7,5},{8,10},{9,11},{10,... | collective-permute-start | bytes 393224 | tf_op jit(solution)/shard_map/ppermute | solution.py:37
  198.3 10.5 %collective-permute-start.48 = (f32[4,32,256]{2,1,0:T(8,128)S(1)}, f32[4,32,256]{2,1,0:T(8,128)S(1)}, u32[]{:S(2)}, u32[]{:S(2)}) collective-permute-start(f32[4,32,256]{2,1,0:T(8,128)S(1)} %get-tuple-element.200), channel_id=1, source_target_pairs={{0,3},{1,0},{2,1},{3,2},{4,7},{5,4},{6,5},{7,6},{8,11},{9,8},{10,9... | collective-permute-start | bytes 393224 | tf_op jit(solution)/shard_map/ppermute | solution.py:37
  208.7 10.6 %collective-permute-start.50 = (f32[4,64,256]{2,1,0:T(8,128)S(1)}, f32[4,64,256]{2,1,0:T(8,128)S(1)}, u32[]{:S(2)}, u32[]{:S(2)}) collective-permute-start(f32[4,64,256]{2,1,0:T(8,128)S(1)} %get-tuple-element.211), channel_id=1, source_target_pairs={{0,2},{1,3},{2,0},{3,1},{4,6},{5,7},{6,4},{7,5},{8,10},{9,11},{10,... | collective-permute-start | bytes 786440 | tf_op jit(solution)/shard_map/ppermute | solution.py:37
  222.2 18.4 %collective-permute-start.55 = (f32[2,128,256]{2,1,0:T(8,128)S(1)}, f32[2,128,256]{2,1,0:T(8,128)S(1)}, u32[]{:S(2)}, u32[]{:S(2)}) collective-permute-start(f32[2,128,256]{2,1,0:T(8,128)S(1)} %get-tuple-element.226), channel_id=1, source_target_pairs={{0,80},{1,81},{2,82},{3,83},{4,84},{5,85},{6,86},{7,87},{8,88},{9,... | collective-permute-start | bytes 786440 | tf_op jit(solution)/shard_map/ppermute | solution.py:37
  234.7 10.5 %collective-permute-start.53 = (f32[2,128,256]{2,1,0:T(8,128)S(1)}, f32[2,128,256]{2,1,0:T(8,128)S(1)}, u32[]{:S(2)}, u32[]{:S(2)}) collective-permute-start(f32[2,128,256]{2,1,0:T(8,128)S(1)} %get-tuple-element.225), channel_id=1, source_target_pairs={{0,64},{1,65},{2,66},{3,67},{4,68},{5,69},{6,70},{7,71},{8,72},{9,... | collective-permute-start | bytes 786440 | tf_op jit(solution)/shard_map/ppermute | solution.py:37
  241.4 14.7 %collective-permute-start.56 = (f32[4,128,256]{2,1,0:T(8,128)}, f32[4,128,256]{2,1,0:T(8,128)S(1)}, u32[]{:S(2)}, u32[]{:S(2)}) collective-permute-start(f32[4,128,256]{2,1,0:T(8,128)} %pad_maximum_fusion.1), channel_id=1, source_target_pairs={{0,80},{1,81},{2,82},{3,83},{4,84},{5,85},{6,86},{7,87},{8,88},{9,... | collective-permute-start | bytes 1572872 | tf_op jit(solution)/shard_map/ppermute | solution.py:37
  246.0 14.3 %collective-permute-start.54 = (f32[4,128,256]{2,1,0:T(8,128)}, f32[4,128,256]{2,1,0:T(8,128)S(1)}, u32[]{:S(2)}, u32[]{:S(2)}) collective-permute-start(f32[4,128,256]{2,1,0:T(8,128)} %pad_maximum_fusion), channel_id=1, source_target_pairs={{0,64},{1,65},{2,66},{3,67},{4,68},{5,69},{6,70},{7,71},{8,72},{9,... | collective-permute-start | bytes 1572872 | tf_op jit(solution)/shard_map/ppermute | solution.py:37
  (27 other events, 197.5 us)

commit v4 on v3

--- a/solution.py
+++ b/solution.py
@@ -581,9 +581,9 @@
         other = send_core(pick(pair_step))
         return jnp.where(own_core == core, pick(own_step), other), *others
 
-    def turned(arrays, steps):
+    def turned(arrays, steps, then=tuple):
         def branch(count):
-            return lambda *values: tuple(send_z(value, count) if count else value for value in values)
+            return lambda *values: then([send_z(value, count) if count else value for value in values])
 
         return lax.switch(steps, [branch(count) for count in (0, 1, 2, -1)], *arrays)
 
@@ -617,9 +617,13 @@
     amount = wavelet[0]
 
     log_slab, speed_slab = lax.optimization_barrier((log_slab, speed_slab))
-    log_slab, speed_slab = turned((log_slab, speed_slab), (4 - turn_by) % 4)
-    log_slab, speed_slab, *pieces = lax.optimization_barrier((log_slab, speed_slab, *pieces))
-    model_pieces = sent_pieces(cut_pieces([log_slab, speed_slab], (True, True), chunks_out))
+    model_pieces = turned(
+        (log_slab, speed_slab),
+        (4 - turn_by) % 4,
+        lambda slabs: tuple(cut_pieces(slabs, (True, True), chunks_out)),
+    )
+    rest = lax.optimization_barrier((*model_pieces, *pieces))
+    model_pieces, pieces = sent_pieces(rest[:4]), rest[4:]
     now, old, adjoint, a_later, side_low, side_high = gather_blocks(pieces, chunks_in, (8, 4, 4, 0))
     below, above = send_group(side_high, 1), send_group(side_low, -1)
     u_wide, old_near, a_near = call(

time: 263 us -> 261 us (level)
  no operation moved by 1% of the time
where the time goes in v4:
time: 261 us; the launch traced here: 260 us
  starting transfers between devices  100 us (38%)
  waiting for transfers between devices  100 us (38%)
  Pallas kernels  32.2 us (12%)
  local copies, waits for them, and re-layouts  9.79 us (4%)
  other arithmetic  8.46 us (3%)
  between operations  5.17 us (2%)
  matrix products  3.17 us (1%)
    ppermute x48, waiting for transfers between devices, send(): return lax.ppermute(value, ('shot', 'sub'), pairs_by(move))  100 us
    ppermute x48, starting transfers between devices, send(): return lax.ppermute(value, ('shot', 'sub'), pairs_by(move))  100 us
    pallas_call x14, Pallas kernels, call(): pl.pallas_call(body, out_shape=tuple(outs), in_specs=specs, out_specs=tup...  32.2 us
  transfers between devices with their start and end apart: 48, of which 25 were waited for; matrix products, arithmetic and copies ran while one was open for 7% of the time, Pallas kernels for 3%

profile of v4, /device:TPU:0, one launch (start us, length us, event | category | flops | bytes accessed | tf_op | source)
XLA Modules:
  0.0 259.8 jit_solution(4599464614030707692)
XLA Ops:
  8.6 8.4 %collective-permute-done.16 = f32[4,128,256]{2,1,0:T(8,128)S(1)} collective-permute-done((f32[4,128,256]{2,1,0:T(8,128)}, f32[4,128,256]{2,1,0:T(8,128)S(1)}, u32[]{:S(2)}, u32[]{:S(2)}) %collective-permute-start.16) | collective-permute-done | bytes 524320 | tf_op jit(solution)/shard_map/ppermute | solution.py:37
  35.1 2.9 %collective-permute-start.21 = (f32[4,176,256]{2,1,0:T(8,128)}, f32[4,176,256]{2,1,0:T(8,128)S(1)}, u32[]{:S(2)}, u32[]{:S(2)}) collective-permute-start(f32[4,176,256]{2,1,0:T(8,128)} %get-tuple-element.159), channel_id=1, source_target_pairs={{0,2},{1,3},{2,0},{3,1},{4,6},{5,7},{6,4},{7,5},{8,10},{9,11},{10,... | collective-permute-start | bytes 2162696 | tf_op jit(solution)/shard_map/ppermute | solution.py:37
  52.8 13.5 %collective-permute-done.21.refs_2_ = f32[4,176,256]{2,1,0:T(8,128)S(1)} collective-permute-done((f32[4,176,256]{2,1,0:T(8,128)}, f32[4,176,256]{2,1,0:T(8,128)S(1)}, u32[]{:S(2)}, u32[]{:S(2)}) %collective-permute-start.21) | collective-permute-done | bytes 720928 | tf_op jit(solution)/shard_map/ppermute | solution.py:37
  68.6 2.9 %collective-permute-start.26 = (f32[4,96,256]{2,1,0:T(8,128)}, f32[4,96,256]{2,1,0:T(8,128)}, u32[]{:S(2)}, u32[]{:S(2)}) collective-permute-start(f32[4,96,256]{2,1,0:T(8,128)} %get-tuple-element.174), channel_id=1, source_target_pairs={{0,2},{1,3},{2,0},{3,1},{4,6},{5,7},{6,4},{7,5},{8,10},{9,11},{10,... | collective-permute-start | bytes 1179656 | tf_op jit(solution)/shard_map/ppermute | solution.py:37
  73.6 3.9 %collective-permute-start.23 = (f32[4,2,144,128]{3,2,1,0:T(8,128)S(1)}, f32[4,2,144,128]{3,2,1,0:T(8,128)S(1)}, u32[]{:S(2)}, u32[]{:S(2)}) collective-permute-start(f32[4,2,144,128]{3,2,1,0:T(8,128)S(1)} %get-tuple-element.168), channel_id=1, source_target_pairs={{0,4},{1,5},{2,6},{3,7},{4,8},{5,9},{6,10},{7,11},{8,12},{9,13},{1... | collective-permute-start | bytes 1769480 | tf_op jit(solution)/shard_map/ppermute | solution.py:37
  79.5 9.7 %collective-permute-done.26.refs_2_ = f32[4,96,256]{2,1,0:T(8,128)} collective-permute-done((f32[4,96,256]{2,1,0:T(8,128)}, f32[4,96,256]{2,1,0:T(8,128)}, u32[]{:S(2)}, u32[]{:S(2)}) %collective-permute-start.26) | collective-permute-done | bytes 393248 | tf_op jit(solution)/shard_map/ppermute | solution.py:37
  90.6 3.8 %collective-permute-start.28 = (f32[4,2,112,128]{3,2,1,0:T(8,128)S(1)}, f32[4,2,112,128]{3,2,1,0:T(8,128)S(1)}, u32[]{:S(2)}, u32[]{:S(2)}) collective-permute-start(f32[4,2,112,128]{3,2,1,0:T(8,128)S(1)} %get-tuple-element.178), channel_id=1, source_target_pairs={{0,4},{1,5},{2,6},{3,7},{4,8},{5,9},{6,10},{7,11},{8,12},{9,13},{1... | collective-permute-start | bytes 1376264 | tf_op jit(solution)/shard_map/ppermute | solution.py:37
  95.9 3.2 %fusion.refs_13_.refs_11_.maps = f32[24,2,48,640]{3,2,1,0:T(8,128)S(1)} fusion(f32[256,640,1,1]{0,1,3,2:T(8,128)S(1)} %bitcast.41, s32[256]{0:T(256)S(1)} %bitcast.44, s32[24,2,48]{2,1,0:T(2,128)S(1)} %multiply_add_fusion), kind=kOutput, calls=%fused_computation | convolution fusion | flops 4530438144 | bytes 6563840 | tf_op jit(solution)/shard_map/dot_general | solution.py:608
  99.4 4.1 %collective-permute-done.28.below = f32[4,2,112,128]{3,2,1,0:T(8,128)S(1)} collective-permute-done((f32[4,2,112,128]{3,2,1,0:T(8,128)S(1)}, f32[4,2,112,128]{3,2,1,0:T(8,128)S(1)}, u32[]{:S(2)}, u32[]{:S(2)}) %collective-permute-start.28) | collective-permute-done | bytes 458784 | tf_op jit(solution)/shard_map/ppermute | solution.py:37
  103.5 4.3 %collective-permute-done.29.above = f32[4,2,112,128]{3,2,1,0:T(8,128)S(1)} collective-permute-done((f32[4,2,112,128]{3,2,1,0:T(8,128)S(1)}, f32[4,2,112,128]{3,2,1,0:T(8,128)S(1)}, u32[]{:S(2)}, u32[]{:S(2)}) %collective-permute-start.29) | collective-permute-done | bytes 458784 | tf_op jit(solution)/shard_map/ppermute | solution.py:37
  107.8 2.9 %shard_map.134 = (f32[24,2,48,128]{3,2,1,0:T(8,128)S(1)}, f32[24,2,48,128]{3,2,1,0:T(8,128)S(1)}, f32[24,2,48,128]{3,2,1,0:T(8,128)S(1)}, f32[24,2,48,128]{3,2,1,0:T(8,128)S(1)}, f32[16,2,32,128]{3,2,1,0:T(8,128)S(1)}) custom-call(f32[16,2,48,128]{3,2,1,0:T(8,128)S(1)} %get-tuple-element.176.log_mass, f32[16,2,48,128]{3,2,1,0:T(8,128)S(1)} %get-tuple-element.177.speed, ...), custom_call_target="tpu_custom_call" | custom-call | tf_op jit(solution)/shard_map/pallas_call | solution.py:91
  110.7 5.3 %shard_map.135 = (f32[24,2,48,128]{3,2,1,0:T(8,128)S(1)}, f32[16,2,32,128]{3,2,1,0:T(8,128)S(1)}, f32[8,2,32,128]{3,2,1,0:T(8,128)S(1)}, f32[8,2,32,128]{3,2,1,0...) custom-call(s32[10]{0:T(128)S(1)} %stack.45.place, f32[4]{0:T(128)S(1)} %bitcast.39, ...), custom_call_target="tpu_custom_call" | custom-call | tf_op jit(solution)/shard_map/pallas_call | solution.py:91
  116.1 3.6 %collective-permute-start.30 = (f32[8,2,32,128]{3,2,1,0:T(8,128)S(1)}, f32[8,2,32,128]{3,2,1,0:T(8,128)S(1)}, u32[]{:S(2)}, u32[]{:S(2)}) collective-permute-start(f32[8,2,32,128]{3,2,1,0:T(8,128)S(1)} %get-tuple-element.187), channel_id=1, source_target_pairs={{0,4},{1,5},{2,6},{3,7},{4,8},{5,9},{6,10},{7,11},{8,12},{9,13},{1... | collective-permute-start | bytes 786440 | tf_op jit(solution)/shard_map/ppermute | solution.py:37
  121.0 3.4 %collective-permute-start.32 = (f32[16,2,8,128]{3,2,1,0:T(8,128)S(1)}, f32[16,2,8,128]{3,2,1,0:T(8,128)S(1)}, u32[]{:S(2)}, u32[]{:S(2)}) collective-permute-start(f32[16,2,8,128]{3,2,1,0:T(8,128)S(1)} %get-tuple-element.189), channel_id=1, source_target_pairs={{0,1},{1,2},{2,3},{4,5},{5,6},{6,7},{8,9},{9,10},{10,11},{12,13},{... | collective-permute-start | bytes 393224 | tf_op jit(solution)/shard_map/ppermute | solution.py:37
  128.0 3.8 %collective-permute-start.34 = (f32[8,2,8,128]{3,2,1,0:T(8,128)S(1)}, f32[8,2,8,128]{3,2,1,0:T(8,128)S(1)}, u32[]{:S(2)}, u32[]{:S(2)}) collective-permute-start(f32[8,2,8,128]{3,2,1,0:T(8,128)S(1)} %get-tuple-element.191), channel_id=1, source_target_pairs={{0,1},{1,2},{2,3},{4,5},{5,6},{6,7},{8,9},{9,10},{10,11},{12,13},{... | collective-permute-start | bytes 196616 | tf_op jit(solution)/shard_map/ppermute | solution.py:37
  133.7 4.3 %collective-permute-done.35.refs_5_ = f32[8,2,8,128]{3,2,1,0:T(8,128)S(1)} collective-permute-done((f32[8,2,8,128]{3,2,1,0:T(8,128)S(1)}, f32[8,2,8,128]{3,2,1,0:T(8,128)S(1)}, u32[]{:S(2)}, u32[]{:S(2)}) %collective-permute-start.35) | collective-permute-done | bytes 65568 | tf_op jit(solution)/shard_map/ppermute | solution.py:37
  138.0 7.4 %shard_map.137 = (f32[24,2,48,128]{3,2,1,0:T(8,128)S(1)}, f32[16,2,32,128]{3,2,1,0:T(8,128)S(1)}, f32[16,2,32,128]{3,2,1,0:T(8,128)S(1)}, f32[16,2,32,128]{3,2,1...) custom-call(s32[10]{0:T(128)S(1)} %stack.45.place, ...), custom_call_target="tpu_custom_call" | custom-call | tf_op jit(solution)/shard_map/pallas_call | solution.py:91
  145.4 5.8 %collective-permute-start.36 = (f32[8,2,32,128]{3,2,1,0:T(8,128)S(1)}, f32[8,2,32,128]{3,2,1,0:T(8,128)S(1)}, u32[]{:S(2)}, u32[]{:S(2)}) collective-permute-start(f32[8,2,32,128]{3,2,1,0:T(8,128)S(1)} %get-tuple-element.198), channel_id=1, source_target_pairs={{0,4},{1,5},{2,6},{3,7},{4,8},{5,9},{6,10},{7,11},{8,12},{9,13},{1... | collective-permute-start | bytes 786440 | tf_op jit(solution)/shard_map/ppermute | solution.py:37
  164.2 4.3 %collective-permute-done.41.refs_5_ = f32[8,2,8,128]{3,2,1,0:T(8,128)S(1)} collective-permute-done((f32[8,2,8,128]{3,2,1,0:T(8,128)S(1)}, f32[8,2,8,128]{3,2,1,0:T(8,128)S(1)}, u32[]{:S(2)}, u32[]{:S(2)}) %collective-permute-start.41) | collective-permute-done | bytes 65568 | tf_op jit(solution)/shard_map/ppermute | solution.py:37
  168.4 5.2 %shard_map.139 = (f32[24,2,48,128]{3,2,1,0:T(8,128)S(1)}, f32[16,2,32,128]{3,2,1,0:T(8,128)S(1)}, f32[16,2,32,128]{3,2,1,0:T(8,128)S(1)}, f32[4,2,32,128]{3,2,1,...) custom-call(f32[16,2,32,128]{3,2,1,0:T(8,128)S(1)} %get-tuple-element.19, ...), custom_call_target="tpu_custom_call" | custom-call | tf_op jit(solution)/shard_map/pallas_call | solution.py:91
  173.6 5.5 %collective-permute-start.42 = (f32[4,2,32,128]{3,2,1,0:T(8,128)S(1)}, f32[4,2,32,128]{3,2,1,0:T(8,128)S(1)}, u32[]{:S(2)}, u32[]{:S(2)}) collective-permute-start(f32[4,2,32,128]{3,2,1,0:T(8,128)S(1)} %get-tuple-element.207), channel_id=1, source_target_pairs={{0,4},{1,5},{2,6},{3,7},{4,8},{5,9},{6,10},{7,11},{8,12},{9,13},{1... | collective-permute-start | bytes 393224 | tf_op jit(solution)/shard_map/ppermute | solution.py:37
  180.4 3.9 %collective-permute-start.44 = (f32[16,2,8,128]{3,2,1,0:T(8,128)S(1)}, f32[16,2,8,128]{3,2,1,0:T(8,128)S(1)}, u32[]{:S(2)}, u32[]{:S(2)}) collective-permute-start(f32[16,2,8,128]{3,2,1,0:T(8,128)S(1)} %get-tuple-element.209), channel_id=1, source_target_pairs={{0,1},{1,2},{2,3},{4,5},{5,6},{6,7},{8,9},{9,10},{10,11},{12,13},{... | collective-permute-start | bytes 393224 | tf_op jit(solution)/shard_map/ppermute | solution.py:37
  187.1 4.9 %collective-permute-done.45.right = f32[16,2,8,128]{3,2,1,0:T(8,128)S(1)} collective-permute-done((f32[16,2,8,128]{3,2,1,0:T(8,128)S(1)}, f32[16,2,8,128]{3,2,1,0:T(8,128)S(1)}, u32[]{:S(2)}, u32[]{:S(2)}) %collective-permute-start.45) | collective-permute-done | bytes 131104 | tf_op jit(solution)/shard_map/ppermute | solution.py:37
  198.4 7.7 %collective-permute-done.46.p1 = f32[4,32,256]{2,1,0:T(8,128)S(1)} collective-permute-done((f32[4,32,256]{2,1,0:T(8,128)S(1)}, f32[4,32,256]{2,1,0:T(8,128)S(1)}, u32[]{:S(2)}, u32[]{:S(2)}) %collective-permute-start.46) | collective-permute-done | bytes 131104 | tf_op jit(solution)/shard_map/ppermute | solution.py:37
  206.1 3.5 %collective-permute-start.50 = (f32[4,64,256]{2,1,0:T(8,128)S(1)}, f32[4,64,256]{2,1,0:T(8,128)S(1)}, u32[]{:S(2)}, u32[]{:S(2)}) collective-permute-start(f32[4,64,256]{2,1,0:T(8,128)S(1)} %get-tuple-element.229), channel_id=1, source_target_pairs={{0,2},{1,3},{2,0},{3,1},{4,6},{5,7},{6,4},{7,5},{8,10},{9,11},{10,... | collective-permute-start | bytes 786440 | tf_op jit(solution)/shard_map/ppermute | solution.py:37
  210.6 3.1 %collective-permute-done.49.p1 = f32[4,64,256]{2,1,0:T(8,128)S(1)} collective-permute-done((f32[4,64,256]{2,1,0:T(8,128)S(1)}, f32[4,64,256]{2,1,0:T(8,128)S(1)}, u32[]{:S(2)}, u32[]{:S(2)}) %collective-permute-start.49) | collective-permute-done | bytes 262176 | tf_op jit(solution)/shard_map/ppermute | solution.py:37
  213.7 3.0 %collective-permute-done.50.p2 = f32[4,64,256]{2,1,0:T(8,128)S(1)} collective-permute-done((f32[4,64,256]{2,1,0:T(8,128)S(1)}, f32[4,64,256]{2,1,0:T(8,128)S(1)}, u32[]{:S(2)}, u32[]{:S(2)}) %collective-permute-start.50) | collective-permute-done | bytes 262176 | tf_op jit(solution)/shard_map/ppermute | solution.py:37
  219.6 13.7 %collective-permute-start.55 = (f32[2,128,256]{2,1,0:T(8,128)S(1)}, f32[2,128,256]{2,1,0:T(8,128)S(1)}, u32[]{:S(2)}, u32[]{:S(2)}) collective-permute-start(f32[2,128,256]{2,1,0:T(8,128)S(1)} %get-tuple-element.244), channel_id=1, source_target_pairs={{0,80},{1,81},{2,82},{3,83},{4,84},{5,85},{6,86},{7,87},{8,88},{9,... | collective-permute-start | bytes 786440 | tf_op jit(solution)/shard_map/ppermute | solution.py:37
  233.2 5.9 %collective-permute-done.55 = f32[2,128,256]{2,1,0:T(8,128)S(1)} collective-permute-done((f32[2,128,256]{2,1,0:T(8,128)S(1)}, f32[2,128,256]{2,1,0:T(8,128)S(1)}, u32[]{:S(2)}, u32[]{:S(2)}) %collective-permute-start.55) | collective-permute-done | bytes 262176 | tf_op jit(solution)/shard_map/ppermute | solution.py:37
  240.0 3.7 %collective-permute-start.56 = (f32[4,128,256]{2,1,0:T(8,128)}, f32[4,128,256]{2,1,0:T(8,128)S(1)}, u32[]{:S(2)}, u32[]{:S(2)}) collective-permute-start(f32[4,128,256]{2,1,0:T(8,128)} %pad_maximum_fusion.1), channel_id=1, source_target_pairs={{0,80},{1,81},{2,82},{3,83},{4,84},{5,85},{6,86},{7,87},{8,88},{9,... | collective-permute-start | bytes 1572872 | tf_op jit(solution)/shard_map/ppermute | solution.py:37
  246.2 8.5 %collective-permute-done.56 = f32[4,128,256]{2,1,0:T(8,128)S(1)} collective-permute-done((f32[4,128,256]{2,1,0:T(8,128)}, f32[4,128,256]{2,1,0:T(8,128)S(1)}, u32[]{:S(2)}, u32[]{:S(2)}) %collective-permute-start.56) | collective-permute-done | bytes 524320 | tf_op jit(solution)/shard_map/ppermute | solution.py:37
  254.6 4.2 %collective-permute-done.54 = f32[4,128,256]{2,1,0:T(8,128)S(1)} collective-permute-done((f32[4,128,256]{2,1,0:T(8,128)}, f32[4,128,256]{2,1,0:T(8,128)S(1)}, u32[]{:S(2)}, u32[]{:S(2)}) %collective-permute-start.54) | collective-permute-done | bytes 524320 | tf_op jit(solution)/shard_map/ppermute | solution.py:37
  (135 shorter events, 86.6 us)
Async XLA Ops:
  0.7 16.3 %collective-permute-start.16 = (f32[4,128,256]{2,1,0:T(8,128)}, f32[4,128,256]{2,1,0:T(8,128)S(1)}, u32[]{:S(2)}, u32[]{:S(2)}) collective-permute-start(f32[4,128,256]{2,1,0:T(8,128)} %param.19), channel_id=1, source_target_pairs={{0,64},{1,65},{2,66},{3,67},{4,68},{5,69},{6,70},{7,71},{8,72},{9,... | collective-permute-start | bytes 1572872 | tf_op jit(solution)/shard_map/ppermute | solution.py:37
  2.3 19.7 %collective-permute-start.15 = (f32[4,128,256]{2,1,0:T(8,128)}, f32[4,128,256]{2,1,0:T(8,128)}, u32[]{:S(2)}, u32[]{:S(2)}) collective-permute-start(f32[4,128,256]{2,1,0:T(8,128)} %param.19), channel_id=1, source_target_pairs={{0,80},{1,81},{2,82},{3,83},{4,84},{5,85},{6,86},{7,87},{8,88},{9,... | collective-permute-start | bytes 1572872 | tf_op jit(solution)/shard_map/ppermute | solution.py:37
  5.9 23.0 %collective-permute-start.10 = (f32[4,128,256]{2,1,0:T(8,128)}, f32[4,128,256]{2,1,0:T(8,128)S(1)}, u32[]{:S(2)}, u32[]{:S(2)}) collective-permute-start(f32[4,128,256]{2,1,0:T(8,128)} %log.3), channel_id=1, source_target_pairs={{0,80},{1,81},{2,82},{3,83},{4,84},{5,85},{6,86},{7,87},{8,88},{9,... | collective-permute-start | bytes 1572872 | tf_op jit(solution)/shard_map/ppermute | solution.py:37
  7.5 21.5 %collective-permute-start.9 = (f32[4,128,256]{2,1,0:T(8,128)}, f32[4,128,256]{2,1,0:T(8,128)}, u32[]{:S(2)}, u32[]{:S(2)}) collective-permute-start(f32[4,128,256]{2,1,0:T(8,128)} %log.3), channel_id=1, source_target_pairs={{0,64},{1,65},{2,66},{3,67},{4,68},{5,69},{6,70},{7,71},{8,72},{9,... | collective-permute-start | bytes 1572872 | tf_op jit(solution)/shard_map/ppermute | solution.py:37
  7.9 18.7 %collective-permute-start.13 = (s32[1]{0:T(128)}, s32[1]{0:T(128)}, u32[]{:S(2)}, u32[]{:S(2)}) collective-permute-start(s32[1]{0:T(128)} %param.21), channel_id=1, source_target_pairs={{0,32},{1,33},{2,34},{3,35},{4,36},{5,37},{6,38},{7,39},{8,40},{9,... | collective-permute-start | bytes 20 | tf_op jit(solution)/shard_map/ppermute | solution.py:37
  17.7 17.3 %collective-permute-start.17 = (f32[2,128,256]{2,1,0:T(8,128)}, f32[2,128,256]{2,1,0:T(8,128)}, u32[]{:S(2)}, u32[]{:S(2)}) collective-permute-start(f32[2,128,256]{2,1,0:T(8,128)} %slice.42), channel_id=1, source_target_pairs={{0,64},{1,65},{2,66},{3,67},{4,68},{5,69},{6,70},{7,71},{8,72},{9,... | collective-permute-start | bytes 786440 | tf_op jit(solution)/shard_map/ppermute | solution.py:37
  23.7 15.2 %collective-permute-start.18 = (f32[2,128,256]{2,1,0:T(8,128)}, f32[2,128,256]{2,1,0:T(8,128)}, u32[]{:S(2)}, u32[]{:S(2)}) collective-permute-start(f32[2,128,256]{2,1,0:T(8,128)} %slice.43), channel_id=1, source_target_pairs={{0,80},{1,81},{2,82},{3,83},{4,84},{5,85},{6,86},{7,87},{8,88},{9,... | collective-permute-start | bytes 786440 | tf_op jit(solution)/shard_map/ppermute | solution.py:37
  30.1 12.5 %collective-permute-start.11 = (f32[2,128,256]{2,1,0:T(8,128)S(1)}, f32[2,128,256]{2,1,0:T(8,128)S(1)}, u32[]{:S(2)}, u32[]{:S(2)}) collective-permute-start(f32[2,128,256]{2,1,0:T(8,128)S(1)} %slice.40), channel_id=1, source_target_pairs={{0,64},{1,65},{2,66},{3,67},{4,68},{5,69},{6,70},{7,71},{8,72},{9,... | collective-permute-start | bytes 786440 | tf_op jit(solution)/shard_map/ppermute | solution.py:37
  31.3 11.4 %collective-permute-start.12 = (f32[2,128,256]{2,1,0:T(8,128)S(1)}, f32[2,128,256]{2,1,0:T(8,128)S(1)}, u32[]{:S(2)}, u32[]{:S(2)}) collective-permute-start(f32[2,128,256]{2,1,0:T(8,128)S(1)} %slice.41), channel_id=1, source_target_pairs={{0,80},{1,81},{2,82},{3,83},{4,84},{5,85},{6,86},{7,87},{8,88},{9,... | collective-permute-start | bytes 786440 | tf_op jit(solution)/shard_map/ppermute | solution.py:37
  33.4 19.4 %collective-permute-start.20 = (f32[4,176,256]{2,1,0:T(8,128)}, f32[4,176,256]{2,1,0:T(8,128)S(1)}, u32[]{:S(2)}, u32[]{:S(2)}) collective-permute-start(f32[4,176,256]{2,1,0:T(8,128)} %get-tuple-element.158), channel_id=1, source_target_pairs={{0,1},{1,2},{2,3},{3,0},{4,5},{5,6},{6,7},{7,4},{8,9},{9,10},{10,1... | collective-permute-start | bytes 2162696 | tf_op jit(solution)/shard_map/ppermute | solution.py:37
  35.1 31.3 %collective-permute-start.21 = (f32[4,176,256]{2,1,0:T(8,128)}, f32[4,176,256]{2,1,0:T(8,128)S(1)}, u32[]{:S(2)}, u32[]{:S(2)}) collective-permute-start(f32[4,176,256]{2,1,0:T(8,128)} %get-tuple-element.159), channel_id=1, source_target_pairs={{0,2},{1,3},{2,0},{3,1},{4,6},{5,7},{6,4},{7,5},{8,10},{9,11},{10,... | collective-permute-start | bytes 2162696 | tf_op jit(solution)/shard_map/ppermute | solution.py:37
  38.9 28.5 %collective-permute-start.22 = (f32[4,176,256]{2,1,0:T(8,128)}, f32[4,176,256]{2,1,0:T(8,128)S(1)}, u32[]{:S(2)}, u32[]{:S(2)}) collective-permute-start(f32[4,176,256]{2,1,0:T(8,128)} %get-tuple-element.160), channel_id=1, source_target_pairs={{0,3},{1,0},{2,1},{3,2},{4,7},{5,4},{6,5},{7,6},{8,11},{9,8},{10,9... | collective-permute-start | bytes 2162696 | tf_op jit(solution)/shard_map/ppermute | solution.py:37
  67.4 12.1 %collective-permute-start.25 = (f32[4,96,256]{2,1,0:T(8,128)}, f32[4,96,256]{2,1,0:T(8,128)S(1)}, u32[]{:S(2)}, u32[]{:S(2)}) collective-permute-start(f32[4,96,256]{2,1,0:T(8,128)} %get-tuple-element.173), channel_id=1, source_target_pairs={{0,1},{1,2},{2,3},{3,0},{4,5},{5,6},{6,7},{7,4},{8,9},{9,10},{10,1... | collective-permute-start | bytes 1179656 | tf_op jit(solution)/shard_map/ppermute | solution.py:37
  68.6 20.7 %collective-permute-start.26 = (f32[4,96,256]{2,1,0:T(8,128)}, f32[4,96,256]{2,1,0:T(8,128)}, u32[]{:S(2)}, u32[]{:S(2)}) collective-permute-start(f32[4,96,256]{2,1,0:T(8,128)} %get-tuple-element.174), channel_id=1, source_target_pairs={{0,2},{1,3},{2,0},{3,1},{4,6},{5,7},{6,4},{7,5},{8,10},{9,11},{10,... | collective-permute-start | bytes 1179656 | tf_op jit(solution)/shard_map/ppermute | solution.py:37
  71.5 17.8 %collective-permute-start.27 = (f32[4,96,256]{2,1,0:T(8,128)}, f32[4,96,256]{2,1,0:T(8,128)}, u32[]{:S(2)}, u32[]{:S(2)}) collective-permute-start(f32[4,96,256]{2,1,0:T(8,128)} %get-tuple-element.175), channel_id=1, source_target_pairs={{0,3},{1,0},{2,1},{3,2},{4,7},{5,4},{6,5},{7,6},{8,11},{9,8},{10,9... | collective-permute-start | bytes 1179656 | tf_op jit(solution)/shard_map/ppermute | solution.py:37
  73.6 25.5 %collective-permute-start.23 = (f32[4,2,144,128]{3,2,1,0:T(8,128)S(1)}, f32[4,2,144,128]{3,2,1,0:T(8,128)S(1)}, u32[]{:S(2)}, u32[]{:S(2)}) collective-permute-start(f32[4,2,144,128]{3,2,1,0:T(8,128)S(1)} %get-tuple-element.168), channel_id=1, source_target_pairs={{0,4},{1,5},{2,6},{3,7},{4,8},{5,9},{6,10},{7,11},{8,12},{9,13},{1... | collective-permute-start | bytes 1769480 | tf_op jit(solution)/shard_map/ppermute | solution.py:37
  77.5 21.6 %collective-permute-start.24 = (f32[4,2,144,128]{3,2,1,0:T(8,128)S(1)}, f32[4,2,144,128]{3,2,1,0:T(8,128)S(1)}, u32[]{:S(2)}, u32[]{:S(2)}) collective-permute-start(f32[4,2,144,128]{3,2,1,0:T(8,128)S(1)} %get-tuple-element.169), channel_id=1, source_target_pairs={{4,0},{5,1},{6,2},{7,3},{8,4},{9,5},{10,6},{11,7},{12,8},{13,9},{1... | collective-permute-start | bytes 1769480 | tf_op jit(solution)/shard_map/ppermute | solution.py:37
  90.6 12.9 %collective-permute-start.28 = (f32[4,2,112,128]{3,2,1,0:T(8,128)S(1)}, f32[4,2,112,128]{3,2,1,0:T(8,128)S(1)}, u32[]{:S(2)}, u32[]{:S(2)}) collective-permute-start(f32[4,2,112,128]{3,2,1,0:T(8,128)S(1)} %get-tuple-element.178), channel_id=1, source_target_pairs={{0,4},{1,5},{2,6},{3,7},{4,8},{5,9},{6,10},{7,11},{8,12},{9,13},{1... | collective-permute-start | bytes 1376264 | tf_op jit(solution)/shard_map/ppermute | solution.py:37
  94.4 13.4 %collective-permute-start.29 = (f32[4,2,112,128]{3,2,1,0:T(8,128)S(1)}, f32[4,2,112,128]{3,2,1,0:T(8,128)S(1)}, u32[]{:S(2)}, u32[]{:S(2)}) collective-permute-start(f32[4,2,112,128]{3,2,1,0:T(8,128)S(1)} %get-tuple-element.179), channel_id=1, source_target_pairs={{4,0},{5,1},{6,2},{7,3},{8,4},{9,5},{10,6},{11,7},{12,8},{13,9},{1... | collective-permute-start | bytes 1376264 | tf_op jit(solution)/shard_map/ppermute | solution.py:37
  116.1 9.6 %collective-permute-start.30 = (f32[8,2,32,128]{3,2,1,0:T(8,128)S(1)}, f32[8,2,32,128]{3,2,1,0:T(8,128)S(1)}, u32[]{:S(2)}, u32[]{:S(2)}) collective-permute-start(f32[8,2,32,128]{3,2,1,0:T(8,128)S(1)} %get-tuple-element.187), channel_id=1, source_target_pairs={{0,4},{1,5},{2,6},{3,7},{4,8},{5,9},{6,10},{7,11},{8,12},{9,13},{1... | collective-permute-start | bytes 786440 | tf_op jit(solution)/shard_map/ppermute | solution.py:37
  121.0 12.1 %collective-permute-start.32 = (f32[16,2,8,128]{3,2,1,0:T(8,128)S(1)}, f32[16,2,8,128]{3,2,1,0:T(8,128)S(1)}, u32[]{:S(2)}, u32[]{:S(2)}) collective-permute-start(f32[16,2,8,128]{3,2,1,0:T(8,128)S(1)} %get-tuple-element.189), channel_id=1, source_target_pairs={{0,1},{1,2},{2,3},{4,5},{5,6},{6,7},{8,9},{9,10},{10,11},{12,13},{... | collective-permute-start | bytes 393224 | tf_op jit(solution)/shard_map/ppermute | solution.py:37
  145.4 11.2 %collective-permute-start.36 = (f32[8,2,32,128]{3,2,1,0:T(8,128)S(1)}, f32[8,2,32,128]{3,2,1,0:T(8,128)S(1)}, u32[]{:S(2)}, u32[]{:S(2)}) collective-permute-start(f32[8,2,32,128]{3,2,1,0:T(8,128)S(1)} %get-tuple-element.198), channel_id=1, source_target_pairs={{0,4},{1,5},{2,6},{3,7},{4,8},{5,9},{6,10},{7,11},{8,12},{9,13},{1... | collective-permute-start | bytes 786440 | tf_op jit(solution)/shard_map/ppermute | solution.py:37
  152.5 11.0 %collective-permute-start.38 = (f32[16,2,8,128]{3,2,1,0:T(8,128)S(1)}, f32[16,2,8,128]{3,2,1,0:T(8,128)S(1)}, u32[]{:S(2)}, u32[]{:S(2)}) collective-permute-start(f32[16,2,8,128]{3,2,1,0:T(8,128)S(1)} %get-tuple-element.200), channel_id=1, source_target_pairs={{0,1},{1,2},{2,3},{4,5},{5,6},{6,7},{8,9},{9,10},{10,11},{12,13},{... | collective-permute-start | bytes 393224 | tf_op jit(solution)/shard_map/ppermute | solution.py:37
  173.6 12.1 %collective-permute-start.42 = (f32[4,2,32,128]{3,2,1,0:T(8,128)S(1)}, f32[4,2,32,128]{3,2,1,0:T(8,128)S(1)}, u32[]{:S(2)}, u32[]{:S(2)}) collective-permute-start(f32[4,2,32,128]{3,2,1,0:T(8,128)S(1)} %get-tuple-element.207), channel_id=1, source_target_pairs={{0,4},{1,5},{2,6},{3,7},{4,8},{5,9},{6,10},{7,11},{8,12},{9,13},{1... | collective-permute-start | bytes 393224 | tf_op jit(solution)/shard_map/ppermute | solution.py:37
  194.6 11.5 %collective-permute-start.46 = (f32[4,32,256]{2,1,0:T(8,128)S(1)}, f32[4,32,256]{2,1,0:T(8,128)S(1)}, u32[]{:S(2)}, u32[]{:S(2)}) collective-permute-start(f32[4,32,256]{2,1,0:T(8,128)S(1)} %get-tuple-element.216), channel_id=1, source_target_pairs={{0,1},{1,2},{2,3},{3,0},{4,5},{5,6},{6,7},{7,4},{8,9},{9,10},{10,1... | collective-permute-start | bytes 393224 | tf_op jit(solution)/shard_map/ppermute | solution.py:37
  195.6 10.5 %collective-permute-start.47 = (f32[4,32,256]{2,1,0:T(8,128)S(1)}, f32[4,32,256]{2,1,0:T(8,128)S(1)}, u32[]{:S(2)}, u32[]{:S(2)}) collective-permute-start(f32[4,32,256]{2,1,0:T(8,128)S(1)} %get-tuple-element.217), channel_id=1, source_target_pairs={{0,2},{1,3},{2,0},{3,1},{4,6},{5,7},{6,4},{7,5},{8,10},{9,11},{10,... | collective-permute-start | bytes 393224 | tf_op jit(solution)/shard_map/ppermute | solution.py:37
  195.6 10.5 %collective-permute-start.48 = (f32[4,32,256]{2,1,0:T(8,128)S(1)}, f32[4,32,256]{2,1,0:T(8,128)S(1)}, u32[]{:S(2)}, u32[]{:S(2)}) collective-permute-start(f32[4,32,256]{2,1,0:T(8,128)S(1)} %get-tuple-element.218), channel_id=1, source_target_pairs={{0,3},{1,0},{2,1},{3,2},{4,7},{5,4},{6,5},{7,6},{8,11},{9,8},{10,9... | collective-permute-start | bytes 393224 | tf_op jit(solution)/shard_map/ppermute | solution.py:37
  206.1 10.6 %collective-permute-start.50 = (f32[4,64,256]{2,1,0:T(8,128)S(1)}, f32[4,64,256]{2,1,0:T(8,128)S(1)}, u32[]{:S(2)}, u32[]{:S(2)}) collective-permute-start(f32[4,64,256]{2,1,0:T(8,128)S(1)} %get-tuple-element.229), channel_id=1, source_target_pairs={{0,2},{1,3},{2,0},{3,1},{4,6},{5,7},{6,4},{7,5},{8,10},{9,11},{10,... | collective-permute-start | bytes 786440 | tf_op jit(solution)/shard_map/ppermute | solution.py:37
  219.6 19.5 %collective-permute-start.55 = (f32[2,128,256]{2,1,0:T(8,128)S(1)}, f32[2,128,256]{2,1,0:T(8,128)S(1)}, u32[]{:S(2)}, u32[]{:S(2)}) collective-permute-start(f32[2,128,256]{2,1,0:T(8,128)S(1)} %get-tuple-element.244), channel_id=1, source_target_pairs={{0,80},{1,81},{2,82},{3,83},{4,84},{5,85},{6,86},{7,87},{8,88},{9,... | collective-permute-start | bytes 786440 | tf_op jit(solution)/shard_map/ppermute | solution.py:37
  233.2 10.5 %collective-permute-start.53 = (f32[2,128,256]{2,1,0:T(8,128)S(1)}, f32[2,128,256]{2,1,0:T(8,128)S(1)}, u32[]{:S(2)}, u32[]{:S(2)}) collective-permute-start(f32[2,128,256]{2,1,0:T(8,128)S(1)} %get-tuple-element.243), channel_id=1, source_target_pairs={{0,64},{1,65},{2,66},{3,67},{4,68},{5,69},{6,70},{7,71},{8,72},{9,... | collective-permute-start | bytes 786440 | tf_op jit(solution)/shard_map/ppermute | solution.py:37
  240.0 14.7 %collective-permute-start.56 = (f32[4,128,256]{2,1,0:T(8,128)}, f32[4,128,256]{2,1,0:T(8,128)S(1)}, u32[]{:S(2)}, u32[]{:S(2)}) collective-permute-start(f32[4,128,256]{2,1,0:T(8,128)} %pad_maximum_fusion.1), channel_id=1, source_target_pairs={{0,80},{1,81},{2,82},{3,83},{4,84},{5,85},{6,86},{7,87},{8,88},{9,... | collective-permute-start | bytes 1572872 | tf_op jit(solution)/shard_map/ppermute | solution.py:37
  244.6 14.3 %collective-permute-start.54 = (f32[4,128,256]{2,1,0:T(8,128)}, f32[4,128,256]{2,1,0:T(8,128)S(1)}, u32[]{:S(2)}, u32[]{:S(2)}) collective-permute-start(f32[4,128,256]{2,1,0:T(8,128)} %pad_maximum_fusion), channel_id=1, source_target_pairs={{0,64},{1,65},{2,66},{3,67},{4,68},{5,69},{6,70},{7,71},{8,72},{9,... | collective-permute-start | bytes 1572872 | tf_op jit(solution)/shard_map/ppermute | solution.py:37
  (28 other events, 212.9 us)

commit v5 on v4

--- a/solution.py
+++ b/solution.py
@@ -675,8 +675,7 @@
         return jnp.concatenate([first_half, second_half])
 
     (image,) = turned((image,), turn_by)
-    image, *pieces = lax.optimization_barrier((image, *sent_pieces(pieces[4:])))
-    adjoint_first, forward_last = to_slabs(pieces, chunks_in, 2)
+    image, *pieces = lax.optimization_barrier((image, *pieces[4:]))
     other = send_core(image)
 
     def share(step):
@@ -686,6 +685,10 @@
     far = share(2)
     passing_up = send_x(far[0:2], 1)
     passing_down = send_x(far[2:4], -1)
+    passing_up, passing_down, *pieces = lax.optimization_barrier(
+        (passing_up, passing_down, *sent_pieces(pieces))
+    )
+    adjoint_first, forward_last = to_slabs(pieces, chunks_in, 2)
     up = share(1)
     down = share(3)
     up = send_x(both(up[0:2] + passing_up, up[2:4]), 1)

time: 261 us -> 266 us (1.019)
  starting transfers between devices: 100 us -> 114 us
  waiting for transfers between devices: 100 us -> 92.2 us
    ppermute x48, starting transfers between devices: 100 us -> 114 us  [send(): return lax.ppermute(value, ('shot', 'sub'), pairs_by(move))]
    ppermute x48, waiting for transfers between devices: 100 us -> 92.2 us  [send(): return lax.ppermute(value, ('shot', 'sub'), pairs_by(move))]
  transfers between devices with their start and end apart: 48 -> 48, of which waited for: 25 -> 24; matrix products, arithmetic and copies ran while one was open for 7% -> 7% of each run, Pallas kernels for 3% -> 3%
where the time goes in v5:
time: 266 us; the launch traced here: 265 us
  starting transfers between devices  114 us (43%)
  waiting for transfers between devices  92.2 us (35%)
  Pallas kernels  32.2 us (12%)
  local copies, waits for them, and re-layouts  9.66 us (4%)
  other arithmetic  8.54 us (3%)
  between operations  5.26 us (2%)
  matrix products  3.17 us (1%)
    ppermute x48, starting transfers between devices, send(): return lax.ppermute(value, ('shot', 'sub'), pairs_by(move))  114 us
    ppermute x48, waiting for transfers between devices, send(): return lax.ppermute(value, ('shot', 'sub'), pairs_by(move))  92.2 us
    pallas_call x14, Pallas kernels, call(): pl.pallas_call(body, out_shape=tuple(outs), in_specs=specs, out_specs=tup...  32.2 us
  transfers between devices with their start and end apart: 48, of which 24 were waited for; matrix products, arithmetic and copies ran while one was open for 7% of the time, Pallas kernels for 3%

profile of v5, /device:TPU:0, one launch (start us, length us, event | category | flops | bytes accessed | tf_op | source)
XLA Modules:
  0.0 265.1 jit_solution(10670813382717313457)
XLA Ops:
  8.6 8.4 %collective-permute-done.16 = f32[4,128,256]{2,1,0:T(8,128)S(1)} collective-permute-done((f32[4,128,256]{2,1,0:T(8,128)}, f32[4,128,256]{2,1,0:T(8,128)S(1)}, u32[]{:S(2)}, u32[]{:S(2)}) %collective-permute-start.16) | collective-permute-done | bytes 524320 | tf_op jit(solution)/shard_map/ppermute | solution.py:37
  23.7 2.9 %collective-permute-start.18 = (f32[2,128,256]{2,1,0:T(8,128)}, f32[2,128,256]{2,1,0:T(8,128)}, u32[]{:S(2)}, u32[]{:S(2)}) collective-permute-start(f32[2,128,256]{2,1,0:T(8,128)} %slice.43), channel_id=1, source_target_pairs={{0,80},{1,81},{2,82},{3,83},{4,84},{5,85},{6,86},{7,87},{8,88},{9,... | collective-permute-start | bytes 786440 | tf_op jit(solution)/shard_map/ppermute | solution.py:37
  35.1 2.9 %collective-permute-start.21 = (f32[4,176,256]{2,1,0:T(8,128)}, f32[4,176,256]{2,1,0:T(8,128)S(1)}, u32[]{:S(2)}, u32[]{:S(2)}) collective-permute-start(f32[4,176,256]{2,1,0:T(8,128)} %get-tuple-element.165), channel_id=1, source_target_pairs={{0,2},{1,3},{2,0},{3,1},{4,6},{5,7},{6,4},{7,5},{8,10},{9,11},{10,... | collective-permute-start | bytes 2162696 | tf_op jit(solution)/shard_map/ppermute | solution.py:37
  52.8 13.5 %collective-permute-done.21.refs_2_ = f32[4,176,256]{2,1,0:T(8,128)S(1)} collective-permute-done((f32[4,176,256]{2,1,0:T(8,128)}, f32[4,176,256]{2,1,0:T(8,128)S(1)}, u32[]{:S(2)}, u32[]{:S(2)}) %collective-permute-start.21) | collective-permute-done | bytes 720928 | tf_op jit(solution)/shard_map/ppermute | solution.py:37
  68.6 2.9 %collective-permute-start.26 = (f32[4,96,256]{2,1,0:T(8,128)}, f32[4,96,256]{2,1,0:T(8,128)}, u32[]{:S(2)}, u32[]{:S(2)}) collective-permute-start(f32[4,96,256]{2,1,0:T(8,128)} %get-tuple-element.180), channel_id=1, source_target_pairs={{0,2},{1,3},{2,0},{3,1},{4,6},{5,7},{6,4},{7,5},{8,10},{9,11},{10,... | collective-permute-start | bytes 1179656 | tf_op jit(solution)/shard_map/ppermute | solution.py:37
  73.6 3.9 %collective-permute-start.23 = (f32[4,2,144,128]{3,2,1,0:T(8,128)S(1)}, f32[4,2,144,128]{3,2,1,0:T(8,128)S(1)}, u32[]{:S(2)}, u32[]{:S(2)}) collective-permute-start(f32[4,2,144,128]{3,2,1,0:T(8,128)S(1)} %get-tuple-element.174), channel_id=1, source_target_pairs={{0,4},{1,5},{2,6},{3,7},{4,8},{5,9},{6,10},{7,11},{8,12},{9,13},{1... | collective-permute-start | bytes 1769480 | tf_op jit(solution)/shard_map/ppermute | solution.py:37
  79.5 9.7 %collective-permute-done.26.refs_2_ = f32[4,96,256]{2,1,0:T(8,128)} collective-permute-done((f32[4,96,256]{2,1,0:T(8,128)}, f32[4,96,256]{2,1,0:T(8,128)}, u32[]{:S(2)}, u32[]{:S(2)}) %collective-permute-start.26) | collective-permute-done | bytes 393248 | tf_op jit(solution)/shard_map/ppermute | solution.py:37
  90.6 3.8 %collective-permute-start.28 = (f32[4,2,112,128]{3,2,1,0:T(8,128)S(1)}, f32[4,2,112,128]{3,2,1,0:T(8,128)S(1)}, u32[]{:S(2)}, u32[]{:S(2)}) collective-permute-start(f32[4,2,112,128]{3,2,1,0:T(8,128)S(1)} %get-tuple-element.184), channel_id=1, source_target_pairs={{0,4},{1,5},{2,6},{3,7},{4,8},{5,9},{6,10},{7,11},{8,12},{9,13},{1... | collective-permute-start | bytes 1376264 | tf_op jit(solution)/shard_map/ppermute | solution.py:37
  95.9 3.2 %fusion.refs_13_.refs_11_.maps = f32[24,2,48,640]{3,2,1,0:T(8,128)S(1)} fusion(f32[256,640,1,1]{0,1,3,2:T(8,128)S(1)} %bitcast.41, s32[256]{0:T(256)S(1)} %bitcast.44, s32[24,2,48]{2,1,0:T(2,128)S(1)} %multiply_add_fusion), kind=kOutput, calls=%fused_computation | convolution fusion | flops 4530438144 | bytes 6563840 | tf_op jit(solution)/shard_map/dot_general | solution.py:608
  99.4 4.1 %collective-permute-done.28.below = f32[4,2,112,128]{3,2,1,0:T(8,128)S(1)} collective-permute-done((f32[4,2,112,128]{3,2,1,0:T(8,128)S(1)}, f32[4,2,112,128]{3,2,1,0:T(8,128)S(1)}, u32[]{:S(2)}, u32[]{:S(2)}) %collective-permute-start.28) | collective-permute-done | bytes 458784 | tf_op jit(solution)/shard_map/ppermute | solution.py:37
  103.5 4.3 %collective-permute-done.29.above = f32[4,2,112,128]{3,2,1,0:T(8,128)S(1)} collective-permute-done((f32[4,2,112,128]{3,2,1,0:T(8,128)S(1)}, f32[4,2,112,128]{3,2,1,0:T(8,128)S(1)}, u32[]{:S(2)}, u32[]{:S(2)}) %collective-permute-start.29) | collective-permute-done | bytes 458784 | tf_op jit(solution)/shard_map/ppermute | solution.py:37
  107.8 2.9 %shard_map.134 = (f32[24,2,48,128]{3,2,1,0:T(8,128)S(1)}, f32[24,2,48,128]{3,2,1,0:T(8,128)S(1)}, f32[24,2,48,128]{3,2,1,0:T(8,128)S(1)}, f32[24,2,48,128]{3,2,1,0:T(8,128)S(1)}, f32[16,2,32,128]{3,2,1,0:T(8,128)S(1)}) custom-call(f32[16,2,48,128]{3,2,1,0:T(8,128)S(1)} %get-tuple-element.182.log_mass, f32[16,2,48,128]{3,2,1,0:T(8,128)S(1)} %get-tuple-element.183.speed, ...), custom_call_target="tpu_custom_call" | custom-call | tf_op jit(solution)/shard_map/pallas_call | solution.py:91
  110.7 5.3 %shard_map.135 = (f32[24,2,48,128]{3,2,1,0:T(8,128)S(1)}, f32[16,2,32,128]{3,2,1,0:T(8,128)S(1)}, f32[8,2,32,128]{3,2,1,0:T(8,128)S(1)}, f32[8,2,32,128]{3,2,1,0...) custom-call(s32[10]{0:T(128)S(1)} %stack.45.place, f32[4]{0:T(128)S(1)} %bitcast.39, ...), custom_call_target="tpu_custom_call" | custom-call | tf_op jit(solution)/shard_map/pallas_call | solution.py:91
  116.1 3.7 %collective-permute-start.30 = (f32[8,2,32,128]{3,2,1,0:T(8,128)S(1)}, f32[8,2,32,128]{3,2,1,0:T(8,128)S(1)}, u32[]{:S(2)}, u32[]{:S(2)}) collective-permute-start(f32[8,2,32,128]{3,2,1,0:T(8,128)S(1)} %get-tuple-element.193), channel_id=1, source_target_pairs={{0,4},{1,5},{2,6},{3,7},{4,8},{5,9},{6,10},{7,11},{8,12},{9,13},{1... | collective-permute-start | bytes 786440 | tf_op jit(solution)/shard_map/ppermute | solution.py:37
  121.0 3.4 %collective-permute-start.32 = (f32[16,2,8,128]{3,2,1,0:T(8,128)S(1)}, f32[16,2,8,128]{3,2,1,0:T(8,128)S(1)}, u32[]{:S(2)}, u32[]{:S(2)}) collective-permute-start(f32[16,2,8,128]{3,2,1,0:T(8,128)S(1)} %get-tuple-element.195), channel_id=1, source_target_pairs={{0,1},{1,2},{2,3},{4,5},{5,6},{6,7},{8,9},{9,10},{10,11},{12,13},{... | collective-permute-start | bytes 393224 | tf_op jit(solution)/shard_map/ppermute | solution.py:37
  128.0 3.8 %collective-permute-start.34 = (f32[8,2,8,128]{3,2,1,0:T(8,128)S(1)}, f32[8,2,8,128]{3,2,1,0:T(8,128)S(1)}, u32[]{:S(2)}, u32[]{:S(2)}) collective-permute-start(f32[8,2,8,128]{3,2,1,0:T(8,128)S(1)} %get-tuple-element.197), channel_id=1, source_target_pairs={{0,1},{1,2},{2,3},{4,5},{5,6},{6,7},{8,9},{9,10},{10,11},{12,13},{... | collective-permute-start | bytes 196616 | tf_op jit(solution)/shard_map/ppermute | solution.py:37
  133.7 4.3 %collective-permute-done.35.refs_5_ = f32[8,2,8,128]{3,2,1,0:T(8,128)S(1)} collective-permute-done((f32[8,2,8,128]{3,2,1,0:T(8,128)S(1)}, f32[8,2,8,128]{3,2,1,0:T(8,128)S(1)}, u32[]{:S(2)}, u32[]{:S(2)}) %collective-permute-start.35) | collective-permute-done | bytes 65568 | tf_op jit(solution)/shard_map/ppermute | solution.py:37
  138.0 7.4 %shard_map.137 = (f32[24,2,48,128]{3,2,1,0:T(8,128)S(1)}, f32[16,2,32,128]{3,2,1,0:T(8,128)S(1)}, f32[16,2,32,128]{3,2,1,0:T(8,128)S(1)}, f32[16,2,32,128]{3,2,1...) custom-call(s32[10]{0:T(128)S(1)} %stack.45.place, ...), custom_call_target="tpu_custom_call" | custom-call | tf_op jit(solution)/shard_map/pallas_call | solution.py:91
  145.4 5.9 %collective-permute-start.36 = (f32[8,2,32,128]{3,2,1,0:T(8,128)S(1)}, f32[8,2,32,128]{3,2,1,0:T(8,128)S(1)}, u32[]{:S(2)}, u32[]{:S(2)}) collective-permute-start(f32[8,2,32,128]{3,2,1,0:T(8,128)S(1)} %get-tuple-element.204), channel_id=1, source_target_pairs={{0,4},{1,5},{2,6},{3,7},{4,8},{5,9},{6,10},{7,11},{8,12},{9,13},{1... | collective-permute-start | bytes 786440 | tf_op jit(solution)/shard_map/ppermute | solution.py:37
  164.2 4.3 %collective-permute-done.41.refs_5_ = f32[8,2,8,128]{3,2,1,0:T(8,128)S(1)} collective-permute-done((f32[8,2,8,128]{3,2,1,0:T(8,128)S(1)}, f32[8,2,8,128]{3,2,1,0:T(8,128)S(1)}, u32[]{:S(2)}, u32[]{:S(2)}) %collective-permute-start.41) | collective-permute-done | bytes 65568 | tf_op jit(solution)/shard_map/ppermute | solution.py:37
  168.4 5.2 %shard_map.139 = (f32[24,2,48,128]{3,2,1,0:T(8,128)S(1)}, f32[16,2,32,128]{3,2,1,0:T(8,128)S(1)}, f32[16,2,32,128]{3,2,1,0:T(8,128)S(1)}, f32[4,2,32,128]{3,2,1,...) custom-call(f32[16,2,32,128]{3,2,1,0:T(8,128)S(1)} %get-tuple-element.20, ...), custom_call_target="tpu_custom_call" | custom-call | tf_op jit(solution)/shard_map/pallas_call | solution.py:91
  173.6 5.5 %collective-permute-start.42 = (f32[4,2,32,128]{3,2,1,0:T(8,128)S(1)}, f32[4,2,32,128]{3,2,1,0:T(8,128)S(1)}, u32[]{:S(2)}, u32[]{:S(2)}) collective-permute-start(f32[4,2,32,128]{3,2,1,0:T(8,128)S(1)} %get-tuple-element.213), channel_id=1, source_target_pairs={{0,4},{1,5},{2,6},{3,7},{4,8},{5,9},{6,10},{7,11},{8,12},{9,13},{1... | collective-permute-start | bytes 393224 | tf_op jit(solution)/shard_map/ppermute | solution.py:37
  180.4 3.9 %collective-permute-start.44 = (f32[16,2,8,128]{3,2,1,0:T(8,128)S(1)}, f32[16,2,8,128]{3,2,1,0:T(8,128)S(1)}, u32[]{:S(2)}, u32[]{:S(2)}) collective-permute-start(f32[16,2,8,128]{3,2,1,0:T(8,128)S(1)} %get-tuple-element.215), channel_id=1, source_target_pairs={{0,1},{1,2},{2,3},{4,5},{5,6},{6,7},{8,9},{9,10},{10,11},{12,13},{... | collective-permute-start | bytes 393224 | tf_op jit(solution)/shard_map/ppermute | solution.py:37
  187.1 4.9 %collective-permute-done.45.right = f32[16,2,8,128]{3,2,1,0:T(8,128)S(1)} collective-permute-done((f32[16,2,8,128]{3,2,1,0:T(8,128)S(1)}, f32[16,2,8,128]{3,2,1,0:T(8,128)S(1)}, u32[]{:S(2)}, u32[]{:S(2)}) %collective-permute-start.45) | collective-permute-done | bytes 131104 | tf_op jit(solution)/shard_map/ppermute | solution.py:37
  198.4 3.9 %collective-permute-done.46.p1 = f32[4,32,256]{2,1,0:T(8,128)S(1)} collective-permute-done((f32[4,32,256]{2,1,0:T(8,128)S(1)}, f32[4,32,256]{2,1,0:T(8,128)S(1)}, u32[]{:S(2)}, u32[]{:S(2)}) %collective-permute-start.46) | collective-permute-done | bytes 131104 | tf_op jit(solution)/shard_map/ppermute | solution.py:37
  204.8 3.5 %collective-permute-start.53 = (f32[4,64,256]{2,1,0:T(8,128)S(1)}, f32[4,64,256]{2,1,0:T(8,128)S(1)}, u32[]{:S(2)}, u32[]{:S(2)}) collective-permute-start(f32[4,64,256]{2,1,0:T(8,128)S(1)} %get-tuple-element.240), channel_id=1, source_target_pairs={{0,2},{1,3},{2,0},{3,1},{4,6},{5,7},{6,4},{7,5},{8,10},{9,11},{10,... | collective-permute-start | bytes 786440 | tf_op jit(solution)/shard_map/ppermute | solution.py:37
  208.6 27.9 %collective-permute-start.51 = (f32[2,128,256]{2,1,0:T(8,128)S(1)}, f32[2,128,256]{2,1,0:T(8,128)S(1)}, u32[]{:S(2)}, u32[]{:S(2)}) collective-permute-start(f32[2,128,256]{2,1,0:T(8,128)S(1)} %get-tuple-element.257), channel_id=1, source_target_pairs={{0,80},{1,81},{2,82},{3,83},{4,84},{5,85},{6,86},{7,87},{8,88},{9,... | collective-permute-start | bytes 786440 | tf_op jit(solution)/shard_map/ppermute | solution.py:37
  236.5 5.3 %collective-permute-done.51 = f32[2,128,256]{2,1,0:T(8,128)S(1)} collective-permute-done((f32[2,128,256]{2,1,0:T(8,128)S(1)}, f32[2,128,256]{2,1,0:T(8,128)S(1)}, u32[]{:S(2)}, u32[]{:S(2)}) %collective-permute-start.51) | collective-permute-done | bytes 262176 | tf_op jit(solution)/shard_map/ppermute | solution.py:37
  241.8 3.4 %collective-permute-done.50 = f32[2,128,256]{2,1,0:T(8,128)S(1)} collective-permute-done((f32[2,128,256]{2,1,0:T(8,128)S(1)}, f32[2,128,256]{2,1,0:T(8,128)S(1)}, u32[]{:S(2)}, u32[]{:S(2)}) %collective-permute-start.50) | collective-permute-done | bytes 262176 | tf_op jit(solution)/shard_map/ppermute | solution.py:37
  246.1 2.9 %collective-permute-start.56 = (f32[4,128,256]{2,1,0:T(8,128)}, f32[4,128,256]{2,1,0:T(8,128)S(1)}, u32[]{:S(2)}, u32[]{:S(2)}) collective-permute-start(f32[4,128,256]{2,1,0:T(8,128)} %pad_maximum_fusion.1), channel_id=1, source_target_pairs={{0,80},{1,81},{2,82},{3,83},{4,84},{5,85},{6,86},{7,87},{8,88},{9,... | collective-permute-start | bytes 1572872 | tf_op jit(solution)/shard_map/ppermute | solution.py:37
  251.5 8.5 %collective-permute-done.56 = f32[4,128,256]{2,1,0:T(8,128)S(1)} collective-permute-done((f32[4,128,256]{2,1,0:T(8,128)}, f32[4,128,256]{2,1,0:T(8,128)S(1)}, u32[]{:S(2)}, u32[]{:S(2)}) %collective-permute-start.56) | collective-permute-done | bytes 524320 | tf_op jit(solution)/shard_map/ppermute | solution.py:37
  260.0 4.2 %collective-permute-done.55 = f32[4,128,256]{2,1,0:T(8,128)S(1)} collective-permute-done((f32[4,128,256]{2,1,0:T(8,128)}, f32[4,128,256]{2,1,0:T(8,128)S(1)}, u32[]{:S(2)}, u32[]{:S(2)}) %collective-permute-start.55) | collective-permute-done | bytes 524320 | tf_op jit(solution)/shard_map/ppermute | solution.py:37
  (135 shorter events, 82.6 us)
Async XLA Ops:
  0.7 16.3 %collective-permute-start.16 = (f32[4,128,256]{2,1,0:T(8,128)}, f32[4,128,256]{2,1,0:T(8,128)S(1)}, u32[]{:S(2)}, u32[]{:S(2)}) collective-permute-start(f32[4,128,256]{2,1,0:T(8,128)} %param.19), channel_id=1, source_target_pairs={{0,64},{1,65},{2,66},{3,67},{4,68},{5,69},{6,70},{7,71},{8,72},{9,... | collective-permute-start | bytes 1572872 | tf_op jit(solution)/shard_map/ppermute | solution.py:37
  2.3 19.7 %collective-permute-start.15 = (f32[4,128,256]{2,1,0:T(8,128)}, f32[4,128,256]{2,1,0:T(8,128)}, u32[]{:S(2)}, u32[]{:S(2)}) collective-permute-start(f32[4,128,256]{2,1,0:T(8,128)} %param.19), channel_id=1, source_target_pairs={{0,80},{1,81},{2,82},{3,83},{4,84},{5,85},{6,86},{7,87},{8,88},{9,... | collective-permute-start | bytes 1572872 | tf_op jit(solution)/shard_map/ppermute | solution.py:37
  5.9 23.0 %collective-permute-start.10 = (f32[4,128,256]{2,1,0:T(8,128)}, f32[4,128,256]{2,1,0:T(8,128)S(1)}, u32[]{:S(2)}, u32[]{:S(2)}) collective-permute-start(f32[4,128,256]{2,1,0:T(8,128)} %log.3), channel_id=1, source_target_pairs={{0,80},{1,81},{2,82},{3,83},{4,84},{5,85},{6,86},{7,87},{8,88},{9,... | collective-permute-start | bytes 1572872 | tf_op jit(solution)/shard_map/ppermute | solution.py:37
  7.5 21.5 %collective-permute-start.9 = (f32[4,128,256]{2,1,0:T(8,128)}, f32[4,128,256]{2,1,0:T(8,128)}, u32[]{:S(2)}, u32[]{:S(2)}) collective-permute-start(f32[4,128,256]{2,1,0:T(8,128)} %log.3), channel_id=1, source_target_pairs={{0,64},{1,65},{2,66},{3,67},{4,68},{5,69},{6,70},{7,71},{8,72},{9,... | collective-permute-start | bytes 1572872 | tf_op jit(solution)/shard_map/ppermute | solution.py:37
  7.9 18.7 %collective-permute-start.13 = (s32[1]{0:T(128)}, s32[1]{0:T(128)}, u32[]{:S(2)}, u32[]{:S(2)}) collective-permute-start(s32[1]{0:T(128)} %param.21), channel_id=1, source_target_pairs={{0,32},{1,33},{2,34},{3,35},{4,36},{5,37},{6,38},{7,39},{8,40},{9,... | collective-permute-start | bytes 20 | tf_op jit(solution)/shard_map/ppermute | solution.py:37
  17.7 17.3 %collective-permute-start.17 = (f32[2,128,256]{2,1,0:T(8,128)}, f32[2,128,256]{2,1,0:T(8,128)}, u32[]{:S(2)}, u32[]{:S(2)}) collective-permute-start(f32[2,128,256]{2,1,0:T(8,128)} %slice.42), channel_id=1, source_target_pairs={{0,64},{1,65},{2,66},{3,67},{4,68},{5,69},{6,70},{7,71},{8,72},{9,... | collective-permute-start | bytes 786440 | tf_op jit(solution)/shard_map/ppermute | solution.py:37
  23.7 15.2 %collective-permute-start.18 = (f32[2,128,256]{2,1,0:T(8,128)}, f32[2,128,256]{2,1,0:T(8,128)}, u32[]{:S(2)}, u32[]{:S(2)}) collective-permute-start(f32[2,128,256]{2,1,0:T(8,128)} %slice.43), channel_id=1, source_target_pairs={{0,80},{1,81},{2,82},{3,83},{4,84},{5,85},{6,86},{7,87},{8,88},{9,... | collective-permute-start | bytes 786440 | tf_op jit(solution)/shard_map/ppermute | solution.py:37
  30.1 12.5 %collective-permute-start.11 = (f32[2,128,256]{2,1,0:T(8,128)S(1)}, f32[2,128,256]{2,1,0:T(8,128)S(1)}, u32[]{:S(2)}, u32[]{:S(2)}) collective-permute-start(f32[2,128,256]{2,1,0:T(8,128)S(1)} %slice.40), channel_id=1, source_target_pairs={{0,64},{1,65},{2,66},{3,67},{4,68},{5,69},{6,70},{7,71},{8,72},{9,... | collective-permute-start | bytes 786440 | tf_op jit(solution)/shard_map/ppermute | solution.py:37
  31.3 11.4 %collective-permute-start.12 = (f32[2,128,256]{2,1,0:T(8,128)S(1)}, f32[2,128,256]{2,1,0:T(8,128)S(1)}, u32[]{:S(2)}, u32[]{:S(2)}) collective-permute-start(f32[2,128,256]{2,1,0:T(8,128)S(1)} %slice.41), channel_id=1, source_target_pairs={{0,80},{1,81},{2,82},{3,83},{4,84},{5,85},{6,86},{7,87},{8,88},{9,... | collective-permute-start | bytes 786440 | tf_op jit(solution)/shard_map/ppermute | solution.py:37
  33.4 19.4 %collective-permute-start.20 = (f32[4,176,256]{2,1,0:T(8,128)}, f32[4,176,256]{2,1,0:T(8,128)S(1)}, u32[]{:S(2)}, u32[]{:S(2)}) collective-permute-start(f32[4,176,256]{2,1,0:T(8,128)} %get-tuple-element.164), channel_id=1, source_target_pairs={{0,1},{1,2},{2,3},{3,0},{4,5},{5,6},{6,7},{7,4},{8,9},{9,10},{10,1... | collective-permute-start | bytes 2162696 | tf_op jit(solution)/shard_map/ppermute | solution.py:37
  35.1 31.3 %collective-permute-start.21 = (f32[4,176,256]{2,1,0:T(8,128)}, f32[4,176,256]{2,1,0:T(8,128)S(1)}, u32[]{:S(2)}, u32[]{:S(2)}) collective-permute-start(f32[4,176,256]{2,1,0:T(8,128)} %get-tuple-element.165), channel_id=1, source_target_pairs={{0,2},{1,3},{2,0},{3,1},{4,6},{5,7},{6,4},{7,5},{8,10},{9,11},{10,... | collective-permute-start | bytes 2162696 | tf_op jit(solution)/shard_map/ppermute | solution.py:37
  38.9 28.5 %collective-permute-start.22 = (f32[4,176,256]{2,1,0:T(8,128)}, f32[4,176,256]{2,1,0:T(8,128)S(1)}, u32[]{:S(2)}, u32[]{:S(2)}) collective-permute-start(f32[4,176,256]{2,1,0:T(8,128)} %get-tuple-element.166), channel_id=1, source_target_pairs={{0,3},{1,0},{2,1},{3,2},{4,7},{5,4},{6,5},{7,6},{8,11},{9,8},{10,9... | collective-permute-start | bytes 2162696 | tf_op jit(solution)/shard_map/ppermute | solution.py:37
  67.4 12.1 %collective-permute-start.25 = (f32[4,96,256]{2,1,0:T(8,128)}, f32[4,96,256]{2,1,0:T(8,128)S(1)}, u32[]{:S(2)}, u32[]{:S(2)}) collective-permute-start(f32[4,96,256]{2,1,0:T(8,128)} %get-tuple-element.179), channel_id=1, source_target_pairs={{0,1},{1,2},{2,3},{3,0},{4,5},{5,6},{6,7},{7,4},{8,9},{9,10},{10,1... | collective-permute-start | bytes 1179656 | tf_op jit(solution)/shard_map/ppermute | solution.py:37
  68.6 20.7 %collective-permute-start.26 = (f32[4,96,256]{2,1,0:T(8,128)}, f32[4,96,256]{2,1,0:T(8,128)}, u32[]{:S(2)}, u32[]{:S(2)}) collective-permute-start(f32[4,96,256]{2,1,0:T(8,128)} %get-tuple-element.180), channel_id=1, source_target_pairs={{0,2},{1,3},{2,0},{3,1},{4,6},{5,7},{6,4},{7,5},{8,10},{9,11},{10,... | collective-permute-start | bytes 1179656 | tf_op jit(solution)/shard_map/ppermute | solution.py:37
  71.5 17.8 %collective-permute-start.27 = (f32[4,96,256]{2,1,0:T(8,128)}, f32[4,96,256]{2,1,0:T(8,128)}, u32[]{:S(2)}, u32[]{:S(2)}) collective-permute-start(f32[4,96,256]{2,1,0:T(8,128)} %get-tuple-element.181), channel_id=1, source_target_pairs={{0,3},{1,0},{2,1},{3,2},{4,7},{5,4},{6,5},{7,6},{8,11},{9,8},{10,9... | collective-permute-start | bytes 1179656 | tf_op jit(solution)/shard_map/ppermute | solution.py:37
  73.6 25.5 %collective-permute-start.23 = (f32[4,2,144,128]{3,2,1,0:T(8,128)S(1)}, f32[4,2,144,128]{3,2,1,0:T(8,128)S(1)}, u32[]{:S(2)}, u32[]{:S(2)}) collective-permute-start(f32[4,2,144,128]{3,2,1,0:T(8,128)S(1)} %get-tuple-element.174), channel_id=1, source_target_pairs={{0,4},{1,5},{2,6},{3,7},{4,8},{5,9},{6,10},{7,11},{8,12},{9,13},{1... | collective-permute-start | bytes 1769480 | tf_op jit(solution)/shard_map/ppermute | solution.py:37
  77.5 21.6 %collective-permute-start.24 = (f32[4,2,144,128]{3,2,1,0:T(8,128)S(1)}, f32[4,2,144,128]{3,2,1,0:T(8,128)S(1)}, u32[]{:S(2)}, u32[]{:S(2)}) collective-permute-start(f32[4,2,144,128]{3,2,1,0:T(8,128)S(1)} %get-tuple-element.175), channel_id=1, source_target_pairs={{4,0},{5,1},{6,2},{7,3},{8,4},{9,5},{10,6},{11,7},{12,8},{13,9},{1... | collective-permute-start | bytes 1769480 | tf_op jit(solution)/shard_map/ppermute | solution.py:37
  90.6 12.9 %collective-permute-start.28 = (f32[4,2,112,128]{3,2,1,0:T(8,128)S(1)}, f32[4,2,112,128]{3,2,1,0:T(8,128)S(1)}, u32[]{:S(2)}, u32[]{:S(2)}) collective-permute-start(f32[4,2,112,128]{3,2,1,0:T(8,128)S(1)} %get-tuple-element.184), channel_id=1, source_target_pairs={{0,4},{1,5},{2,6},{3,7},{4,8},{5,9},{6,10},{7,11},{8,12},{9,13},{1... | collective-permute-start | bytes 1376264 | tf_op jit(solution)/shard_map/ppermute | solution.py:37
  94.4 13.4 %collective-permute-start.29 = (f32[4,2,112,128]{3,2,1,0:T(8,128)S(1)}, f32[4,2,112,128]{3,2,1,0:T(8,128)S(1)}, u32[]{:S(2)}, u32[]{:S(2)}) collective-permute-start(f32[4,2,112,128]{3,2,1,0:T(8,128)S(1)} %get-tuple-element.185), channel_id=1, source_target_pairs={{4,0},{5,1},{6,2},{7,3},{8,4},{9,5},{10,6},{11,7},{12,8},{13,9},{1... | collective-permute-start | bytes 1376264 | tf_op jit(solution)/shard_map/ppermute | solution.py:37
  116.1 9.7 %collective-permute-start.30 = (f32[8,2,32,128]{3,2,1,0:T(8,128)S(1)}, f32[8,2,32,128]{3,2,1,0:T(8,128)S(1)}, u32[]{:S(2)}, u32[]{:S(2)}) collective-permute-start(f32[8,2,32,128]{3,2,1,0:T(8,128)S(1)} %get-tuple-element.193), channel_id=1, source_target_pairs={{0,4},{1,5},{2,6},{3,7},{4,8},{5,9},{6,10},{7,11},{8,12},{9,13},{1... | collective-permute-start | bytes 786440 | tf_op jit(solution)/shard_map/ppermute | solution.py:37
  121.0 12.1 %collective-permute-start.32 = (f32[16,2,8,128]{3,2,1,0:T(8,128)S(1)}, f32[16,2,8,128]{3,2,1,0:T(8,128)S(1)}, u32[]{:S(2)}, u32[]{:S(2)}) collective-permute-start(f32[16,2,8,128]{3,2,1,0:T(8,128)S(1)} %get-tuple-element.195), channel_id=1, source_target_pairs={{0,1},{1,2},{2,3},{4,5},{5,6},{6,7},{8,9},{9,10},{10,11},{12,13},{... | collective-permute-start | bytes 393224 | tf_op jit(solution)/shard_map/ppermute | solution.py:37
  124.4 8.7 %collective-permute-start.33 = (f32[16,2,8,128]{3,2,1,0:T(8,128)S(1)}, f32[16,2,8,128]{3,2,1,0:T(8,128)S(1)}, u32[]{:S(2)}, u32[]{:S(2)}) collective-permute-start(f32[16,2,8,128]{3,2,1,0:T(8,128)S(1)} %get-tuple-element.196), channel_id=1, source_target_pairs={{1,0},{2,1},{3,2},{5,4},{6,5},{7,6},{9,8},{10,9},{11,10},{13,12},{... | collective-permute-start | bytes 393224 | tf_op jit(solution)/shard_map/ppermute | solution.py:37
  145.4 11.2 %collective-permute-start.36 = (f32[8,2,32,128]{3,2,1,0:T(8,128)S(1)}, f32[8,2,32,128]{3,2,1,0:T(8,128)S(1)}, u32[]{:S(2)}, u32[]{:S(2)}) collective-permute-start(f32[8,2,32,128]{3,2,1,0:T(8,128)S(1)} %get-tuple-element.204), channel_id=1, source_target_pairs={{0,4},{1,5},{2,6},{3,7},{4,8},{5,9},{6,10},{7,11},{8,12},{9,13},{1... | collective-permute-start | bytes 786440 | tf_op jit(solution)/shard_map/ppermute | solution.py:37
  152.5 11.0 %collective-permute-start.38 = (f32[16,2,8,128]{3,2,1,0:T(8,128)S(1)}, f32[16,2,8,128]{3,2,1,0:T(8,128)S(1)}, u32[]{:S(2)}, u32[]{:S(2)}) collective-permute-start(f32[16,2,8,128]{3,2,1,0:T(8,128)S(1)} %get-tuple-element.206), channel_id=1, source_target_pairs={{0,1},{1,2},{2,3},{4,5},{5,6},{6,7},{8,9},{9,10},{10,11},{12,13},{... | collective-permute-start | bytes 393224 | tf_op jit(solution)/shard_map/ppermute | solution.py:37
  173.6 12.1 %collective-permute-start.42 = (f32[4,2,32,128]{3,2,1,0:T(8,128)S(1)}, f32[4,2,32,128]{3,2,1,0:T(8,128)S(1)}, u32[]{:S(2)}, u32[]{:S(2)}) collective-permute-start(f32[4,2,32,128]{3,2,1,0:T(8,128)S(1)} %get-tuple-element.213), channel_id=1, source_target_pairs={{0,4},{1,5},{2,6},{3,7},{4,8},{5,9},{6,10},{7,11},{8,12},{9,13},{1... | collective-permute-start | bytes 393224 | tf_op jit(solution)/shard_map/ppermute | solution.py:37
  203.9 32.5 %collective-permute-start.52 = (f32[4,64,256]{2,1,0:T(8,128)S(1)}, f32[4,64,256]{2,1,0:T(8,128)S(1)}, u32[]{:S(2)}, u32[]{:S(2)}) collective-permute-start(f32[4,64,256]{2,1,0:T(8,128)S(1)} %get-tuple-element.239), channel_id=1, source_target_pairs={{0,1},{1,2},{2,3},{3,0},{4,5},{5,6},{6,7},{7,4},{8,9},{9,10},{10,1... | collective-permute-start | bytes 786440 | tf_op jit(solution)/shard_map/ppermute | solution.py:37
  204.8 31.6 %collective-permute-start.53 = (f32[4,64,256]{2,1,0:T(8,128)S(1)}, f32[4,64,256]{2,1,0:T(8,128)S(1)}, u32[]{:S(2)}, u32[]{:S(2)}) collective-permute-start(f32[4,64,256]{2,1,0:T(8,128)S(1)} %get-tuple-element.240), channel_id=1, source_target_pairs={{0,2},{1,3},{2,0},{3,1},{4,6},{5,7},{6,4},{7,5},{8,10},{9,11},{10,... | collective-permute-start | bytes 786440 | tf_op jit(solution)/shard_map/ppermute | solution.py:37
  208.3 28.1 %collective-permute-start.54 = (f32[4,64,256]{2,1,0:T(8,128)S(1)}, f32[4,64,256]{2,1,0:T(8,128)S(1)}, u32[]{:S(2)}, u32[]{:S(2)}) collective-permute-start(f32[4,64,256]{2,1,0:T(8,128)S(1)} %get-tuple-element.241), channel_id=1, source_target_pairs={{0,3},{1,0},{2,1},{3,2},{4,7},{5,4},{6,5},{7,6},{8,11},{9,8},{10,9... | collective-permute-start | bytes 786440 | tf_op jit(solution)/shard_map/ppermute | solution.py:37
  208.6 33.2 %collective-permute-start.51 = (f32[2,128,256]{2,1,0:T(8,128)S(1)}, f32[2,128,256]{2,1,0:T(8,128)S(1)}, u32[]{:S(2)}, u32[]{:S(2)}) collective-permute-start(f32[2,128,256]{2,1,0:T(8,128)S(1)} %get-tuple-element.257), channel_id=1, source_target_pairs={{0,80},{1,81},{2,82},{3,83},{4,84},{5,85},{6,86},{7,87},{8,88},{9,... | collective-permute-start | bytes 786440 | tf_op jit(solution)/shard_map/ppermute | solution.py:37
  236.4 8.7 %collective-permute-start.50 = (f32[2,128,256]{2,1,0:T(8,128)S(1)}, f32[2,128,256]{2,1,0:T(8,128)S(1)}, u32[]{:S(2)}, u32[]{:S(2)}) collective-permute-start(f32[2,128,256]{2,1,0:T(8,128)S(1)} %get-tuple-element.258), channel_id=1, source_target_pairs={{0,64},{1,65},{2,66},{3,67},{4,68},{5,69},{6,70},{7,71},{8,72},{9,... | collective-permute-start | bytes 786440 | tf_op jit(solution)/shard_map/ppermute | solution.py:37
  246.1 13.9 %collective-permute-start.56 = (f32[4,128,256]{2,1,0:T(8,128)}, f32[4,128,256]{2,1,0:T(8,128)S(1)}, u32[]{:S(2)}, u32[]{:S(2)}) collective-permute-start(f32[4,128,256]{2,1,0:T(8,128)} %pad_maximum_fusion.1), channel_id=1, source_target_pairs={{0,80},{1,81},{2,82},{3,83},{4,84},{5,85},{6,86},{7,87},{8,88},{9,... | collective-permute-start | bytes 1572872 | tf_op jit(solution)/shard_map/ppermute | solution.py:37
  249.9 14.3 %collective-permute-start.55 = (f32[4,128,256]{2,1,0:T(8,128)}, f32[4,128,256]{2,1,0:T(8,128)S(1)}, u32[]{:S(2)}, u32[]{:S(2)}) collective-permute-start(f32[4,128,256]{2,1,0:T(8,128)} %pad_maximum_fusion), channel_id=1, source_target_pairs={{0,64},{1,65},{2,66},{3,67},{4,68},{5,69},{6,70},{7,71},{8,72},{9,... | collective-permute-start | bytes 1572872 | tf_op jit(solution)/shard_map/ppermute | solution.py:37
  (28 other events, 213.6 us)
